TPU v7x, 32 devices: a whole 2x2x4 slice. The times are simulated.
32 devices in a mesh: dp: 8 (over y, x, core), fsdp: 4 (over z).
Axes of the slice: x: 2, y: 2, z: 4, core: 2. Of those that a mesh axis runs over, the one named last changes fastest.
Arguments:
- tokens: bfloat16 [8, 1024, 2048], P('dp', 'fsdp'), may hold values from -6 to 6
- segments: int32 [8, 1024], P('dp'), may hold values from 0 to 5, never falling along the last dimension, each value on 1 to 512 neighbouring positions
- out_grad: bfloat16 [8, 1024, 2048], P('dp', 'fsdp'), may hold values from -6 to 6
- owners: int32 [384], replicated, may hold values from 0 to 31, as said below
- blocks: float32 [384, 256, 512], P(('dp', 'fsdp')), may hold values from -2 to 2
- first_moment: float32 [384, 256, 512], P(('dp', 'fsdp')), may hold values from -6 to 6
- second_moment: float32 [384, 256, 512], P(('dp', 'fsdp')), may hold values from 0.25 to 4
- left_bases: float32 [384, 256, 256], P(('dp', 'fsdp')), may hold values from -0.375 to 0.375
- right_bases: float32 [384, 512, 512], P(('dp', 'fsdp')), may hold values from -0.25 to 0.25
- vectors: float32 [24576], P(('dp', 'fsdp')), may hold values from -0.5 to 1.25
- vector_first: float32 [24576], P(('dp', 'fsdp')), may hold values from -6 to 6
- vector_second: float32 [24576], P(('dp', 'fsdp')), may hold values from 0.25 to 4
Outputs:
- out_tokens: bfloat16 [8, 1024, 2048], P('dp', 'fsdp')
- input_grad: float32 [8, 1024, 2048], P('dp', 'fsdp')
- block_grads: float32 [384, 256, 512], P(('dp', 'fsdp'))
- vector_grads: float32 [24576], P(('dp', 'fsdp'))
- new_blocks: float32 [384, 256, 512], P(('dp', 'fsdp'))
- new_first: float32 [384, 256, 512], P(('dp', 'fsdp'))
- new_second: float32 [384, 256, 512], P(('dp', 'fsdp'))
- block_copies: bfloat16 [384, 256, 512], P(('dp', 'fsdp'))
- new_vectors: float32 [24576], P(('dp', 'fsdp'))
- new_vector_first: float32 [24576], P(('dp', 'fsdp'))
- new_vector_second: float32 [24576], P(('dp', 'fsdp'))
- vector_copies: bfloat16 [24576], P(('dp', 'fsdp'))
- grad_norm: float32 [], replicated
- clip_factors: float32 [16], replicated
Inputs may be any that keep to these rules, and one draw needn't show every extreme that they name: `owners`: each device index of the joined axis dp+fsdp owns exactly 12 blocks. `segments`: within a sequence the ids never fall; each of the 6 documents has 1 to 512 tokens, one exactly 512.
All inputs are finite; a program needn't handle non-finite values.
Results may differ from a plain program's by a relative error of at most 0.012.
Values may be sent and summed in bfloat16 or wider, within the bound.
No kernel may reach another device: no remote copies, remote signals or barrier semaphores. Data moves between devices by JAX's collectives and lax.ppermute only.
A program may use at most 512 MiB of HBM per device.

v0:
```python
from functools import partial
import math

import jax
import jax.numpy as jnp
from jax import lax
from jax.sharding import PartitionSpec as P

D = 2048
HEADS = 16
DH = 128
FF = 8192
BR = 256
BC = 512


HIGH = lax.Precision.HIGHEST
NEG = -1e30


def layer_norm(hidden, gain_vector, shift_vector):
    average = jnp.mean(hidden, axis=-1, keepdims=True)
    centred = hidden - average
    variance = jnp.mean(centred * centred, axis=-1, keepdims=True)
    return centred * lax.rsqrt(variance + 1e-05) * gain_vector + shift_vector


def to_matrix(block_list, rows_all, cols_all):
    shaped = block_list.reshape(rows_all // BR, cols_all // BC, BR, BC)
    return shaped.transpose(0, 2, 1, 3).reshape(rows_all, cols_all)


def split_blocks(blocks_by_id):
    qkv_end = D // BR * (3 * D // BC)
    out_end = qkv_end + D // BR * (D // BC)
    up_end = out_end + D // BR * (FF // BC)
    return (
        to_matrix(blocks_by_id[:qkv_end], D, 3 * D),
        to_matrix(blocks_by_id[qkv_end:out_end], D, D),
        to_matrix(blocks_by_id[out_end:up_end], D, FF),
        to_matrix(blocks_by_id[up_end:], FF, D),
    )


def split_vectors(vector_all):
    feature_major = vector_all[: 8 * D].reshape(D, 8)
    pieces = [feature_major[:, index_one] for index_one in range(8)]
    return pieces + [vector_all[8 * D :]]


def slot_tables(owners, per_owner):
    total_blocks = owners.shape[0]
    block_ids = jnp.arange(total_blocks, dtype=jnp.int32)
    earlier = (owners[None, :] == owners[:, None]) & (block_ids[None, :] < block_ids[:, None])
    slot_of_block = owners * per_owner + jnp.sum(earlier.astype(jnp.int32), axis=1)
    block_at_slot = jnp.zeros((total_blocks,), jnp.int32).at[slot_of_block].set(block_ids)
    return (slot_of_block, block_at_slot)


def column_scale(block_ids, root_factor):
    per_row = 3 * D // BC
    qkv_total = D // BR * per_row
    columns = (block_ids % per_row)[:, None] * BC + jnp.arange(BC, dtype=jnp.int32)[None, :]
    head_of = columns % D // DH
    picked = jnp.sum(
        jnp.where(head_of[..., None] == jnp.arange(HEADS, dtype=jnp.int32), root_factor, 0.0),
        axis=-1,
    )
    inside = (block_ids < qkv_total)[:, None] & (columns < 2 * D)
    return jnp.where(inside, picked, 1.0)


def vector_scale(positions, root_factor):
    inside = (positions < 8 * D) & (positions % 8 == 2)
    head_of = positions // 8 // DH
    picked = jnp.sum(
        jnp.where(head_of[:, None] == jnp.arange(HEADS, dtype=jnp.int32), root_factor, 0.0), axis=-1
    )
    return jnp.where(inside, picked, 1.0)


def rotate_in(matrix, left_basis, right_basis):
    left_done = jnp.einsum(
        "bij,bik->bjk", left_basis, matrix, precision=HIGH, preferred_element_type=jnp.float32
    )
    return jnp.einsum(
        "bjk,bkl->bjl", left_done, right_basis, precision=HIGH, preferred_element_type=jnp.float32
    )


def rotate_out(matrix, left_basis, right_basis):
    left_done = jnp.einsum(
        "bij,bjk->bik", left_basis, matrix, precision=HIGH, preferred_element_type=jnp.float32
    )
    return jnp.einsum(
        "bik,blk->bil", left_done, right_basis, precision=HIGH, preferred_element_type=jnp.float32
    )


def masked_scores(query_low, keys_all, segments, offset):
    batch_size, local_len, model_width = query_low.shape
    full_len = keys_all.shape[1]
    query4 = query_low.reshape(batch_size, local_len, HEADS, DH)
    keys4 = keys_all.reshape(batch_size, full_len, HEADS, DH)
    scores = jnp.einsum(
        "bqhd,bkhd->bhqk", query4, keys4, preferred_element_type=jnp.float32
    ) * DH ** (-0.5)
    query_pos = offset + jnp.arange(local_len, dtype=jnp.int32)
    key_pos = jnp.arange(full_len, dtype=jnp.int32)
    query_seg = lax.dynamic_slice_in_dim(segments, offset, local_len, 1)
    allowed = (key_pos[None, None, :] <= query_pos[None, :, None]) & (
        segments[:, None, :] == query_seg[:, :, None]
    )
    return jnp.where(allowed[:, None], scores, NEG)


def transposed_product(left, right):
    return lax.dot_general(
        left, right, (((0,), (0,)), ((), ())), preferred_element_type=jnp.float32
    )


def one_block(left_full, right_full, local_id, cols_all):
    per_row = cols_all // BC
    row_block = local_id // per_row
    col_block = local_id % per_row
    left = lax.dynamic_slice_in_dim(left_full, row_block * BR, BR, 1)
    right = lax.dynamic_slice_in_dim(right_full, col_block * BC, BC, 1)
    return transposed_product(left, right)


def local(
    tokens,
    segments,
    out_grad,
    owners,
    blocks,
    first_moment,
    second_moment,
    left_bases,
    right_bases,
    vectors,
    vector_first,
    vector_second,
):
    per_owner = blocks.shape[0]
    vector_part = vectors.shape[0]
    slot_of_block, block_at_slot = slot_tables(owners, per_owner)
    rank_all = lax.axis_index(("dp", "fsdp"))
    own_ids = lax.dynamic_slice_in_dim(block_at_slot, rank_all * per_owner, per_owner)
    block_low = blocks.astype(jnp.bfloat16)
    vector_low = vectors.astype(jnp.bfloat16)
    gathered_blocks, gathered_vectors = (
        lax.all_gather(block_low, ("dp", "fsdp"), axis=0, tiled=True),
        lax.all_gather(vector_low, ("dp", "fsdp"), axis=0, tiled=True),
    )
    w_qkv, w_out, w_up, w_down = split_blocks(gathered_blocks[slot_of_block])
    ln1_gain, ln1_shift, q_bias, v_bias, out_bias, ln2_gain, ln2_shift, down_bias, up_bias = (
        split_vectors(gathered_vectors.astype(jnp.float32))
    )
    batch_size, local_len, model_width = tokens.shape
    offset = lax.axis_index("fsdp") * local_len
    inputs = tokens.astype(jnp.float32).reshape(-1, model_width)
    normed = layer_norm(inputs, ln1_gain, ln1_shift)
    normed_low = normed.astype(jnp.bfloat16)
    projected = jnp.dot(normed_low, w_qkv, preferred_element_type=jnp.float32)
    query_low = (projected[:, :D] + q_bias).astype(jnp.bfloat16).reshape(batch_size, local_len, D)
    key_low = projected[:, D : 2 * D].astype(jnp.bfloat16).reshape(batch_size, local_len, D)
    value_low = (
        (projected[:, 2 * D :] + v_bias).astype(jnp.bfloat16).reshape(batch_size, local_len, D)
    )
    keys_all, values_all = (
        lax.all_gather(key_low, "fsdp", axis=1, tiled=True),
        lax.all_gather(value_low, "fsdp", axis=1, tiled=True),
    )
    masked = masked_scores(query_low, keys_all, segments, offset)
    row_top = jnp.max(masked, axis=-1, keepdims=True)
    log_total = row_top + jnp.log(jnp.sum(jnp.exp(masked - row_top), axis=-1, keepdims=True))
    probs = jnp.exp(masked - log_total)
    values4 = values_all.reshape(batch_size, -1, HEADS, DH)
    mixed = jnp.einsum(
        "bhqk,bkhd->bqhd", probs.astype(jnp.bfloat16), values4, preferred_element_type=jnp.float32
    )
    mixed_low = mixed.reshape(-1, D).astype(jnp.bfloat16)
    head_top = jnp.max(row_top, axis=(0, 2, 3))
    attended = jnp.dot(mixed_low, w_out, preferred_element_type=jnp.float32) + out_bias
    hidden_one = inputs + attended
    normed_two_low = layer_norm(hidden_one, ln2_gain, ln2_shift).astype(jnp.bfloat16)
    upper = jnp.dot(normed_two_low, w_up, preferred_element_type=jnp.float32) + up_bias
    activated, gelu_back = jax.vjp(partial(jax.nn.gelu, approximate=False), upper)
    activated_low = activated.astype(jnp.bfloat16)
    branch = jnp.dot(activated_low, w_down, preferred_element_type=jnp.float32) + down_bias
    out_tokens = (hidden_one + branch).astype(jnp.bfloat16).reshape(batch_size, local_len, D)
    again_blocks = lax.all_gather(block_low, ("dp", "fsdp"), axis=0, tiled=True)
    w_qkv, w_out, w_up, w_down = split_blocks(again_blocks[slot_of_block])
    keys_all, values_all = (
        lax.all_gather(key_low, "fsdp", axis=1, tiled=True),
        lax.all_gather(value_low, "fsdp", axis=1, tiled=True),
    )
    values4 = values_all.reshape(batch_size, -1, HEADS, DH)
    grad_top = out_grad.reshape(-1, D)
    grad_top_wide = grad_top.astype(jnp.float32)
    down_bias_grad = jnp.sum(grad_top_wide, axis=0)
    grad_act = jnp.dot(grad_top, w_down.T, preferred_element_type=jnp.float32)
    grad_upper_low = gelu_back(grad_act)[0].astype(jnp.bfloat16)
    up_bias_grad = jnp.sum(grad_upper_low.astype(jnp.float32), axis=0)
    grad_normed_two = jnp.dot(grad_upper_low, w_up.T, preferred_element_type=jnp.float32)
    norm_value, norm_two_back = jax.vjp(layer_norm, hidden_one, ln2_gain, ln2_shift)
    grad_hidden_ln, ln2_gain_grad, ln2_shift_grad = norm_two_back(grad_normed_two)
    grad_hidden = grad_top_wide + grad_hidden_ln
    grad_attn_low = grad_hidden.astype(jnp.bfloat16)
    out_bias_grad = jnp.sum(grad_attn_low.astype(jnp.float32), axis=0)
    grad_mixed = (
        jnp.dot(grad_attn_low, w_out.T, preferred_element_type=jnp.float32)
        .astype(jnp.bfloat16)
        .reshape(batch_size, local_len, HEADS, DH)
    )
    masked = masked_scores(query_low, keys_all, segments, offset)
    probs = jnp.exp(masked - log_total)
    grad_probs = jnp.einsum(
        "bqhd,bkhd->bhqk", grad_mixed, values4, preferred_element_type=jnp.float32
    )
    inner = jnp.sum(probs * grad_probs, axis=-1, keepdims=True)
    grad_scores_low = (probs * (grad_probs - inner)).astype(jnp.bfloat16)
    keys4 = keys_all.reshape(batch_size, -1, HEADS, DH)
    query4 = query_low.reshape(batch_size, local_len, HEADS, DH)
    grad_query = (
        jnp.einsum("bhqk,bkhd->bqhd", grad_scores_low, keys4, preferred_element_type=jnp.float32)
        * DH ** (-0.5)
    ).astype(jnp.bfloat16)
    key_terms = jnp.einsum(
        "bhqk,bqhd->bkhd", grad_scores_low, query4, preferred_element_type=jnp.float32
    ).reshape(batch_size, -1, D) * DH ** (-0.5)
    value_terms = jnp.einsum(
        "bhqk,bqhd->bkhd",
        probs.astype(jnp.bfloat16),
        grad_mixed,
        preferred_element_type=jnp.float32,
    ).reshape(batch_size, -1, D)
    grad_keys, grad_values = (
        lax.psum_scatter(
            key_terms.astype(jnp.bfloat16), "fsdp", scatter_dimension=1, tiled=True
        ).astype(jnp.float32),
        lax.psum_scatter(
            value_terms.astype(jnp.bfloat16), "fsdp", scatter_dimension=1, tiled=True
        ).astype(jnp.float32),
    )
    grad_values_low = grad_values.reshape(-1, D).astype(jnp.bfloat16)
    grad_query_flat = grad_query.reshape(-1, D)
    grad_proj_low = jnp.concatenate(
        [grad_query_flat, grad_keys.reshape(-1, D).astype(jnp.bfloat16), grad_values_low], axis=1
    )
    q_bias_grad = jnp.sum(grad_query_flat.astype(jnp.float32), axis=0)
    v_bias_grad = jnp.sum(grad_values_low.astype(jnp.float32), axis=0)
    grad_normed = jnp.dot(grad_proj_low, w_qkv.T, preferred_element_type=jnp.float32)
    norm_first, norm_one_back = jax.vjp(layer_norm, inputs, ln1_gain, ln1_shift)
    grad_input_ln, ln1_gain_grad, ln1_shift_grad = norm_one_back(grad_normed)
    input_grad = (grad_hidden + grad_input_ln).reshape(batch_size, local_len, D)
    qkv_end = D // BR * (3 * D // BC)
    out_end = qkv_end + D // BR * (D // BC)
    up_end = out_end + D // BR * (FF // BC)
    first_ids = jnp.array([0, qkv_end, out_end, up_end], dtype=jnp.int32)
    branches = [
        lambda local_id: one_block(normed_low, grad_proj_low, local_id, 3 * D),
        lambda local_id: one_block(mixed_low, grad_attn_low, local_id, D),
        lambda local_id: one_block(normed_two_low, grad_upper_low, local_id, FF),
        lambda local_id: one_block(activated_low, grad_top, local_id, D),
    ]

    def block_grad(block_id):
        matrix_id = (
            (block_id >= qkv_end).astype(jnp.int32)
            + (block_id >= out_end).astype(jnp.int32)
            + (block_id >= up_end).astype(jnp.int32)
        )
        local_id = block_id - jnp.sum(
            jnp.where(jnp.arange(4, dtype=jnp.int32) == matrix_id, first_ids, 0)
        )
        return lax.switch(matrix_id, branches, local_id)

    owned_grads = lax.psum_scatter(
        lax.map(block_grad, block_at_slot), ("dp", "fsdp"), scatter_dimension=0, tiled=True
    )
    feature_terms = jnp.stack(
        [
            ln1_gain_grad,
            ln1_shift_grad,
            q_bias_grad,
            v_bias_grad,
            out_bias_grad,
            ln2_gain_grad,
            ln2_shift_grad,
            down_bias_grad,
        ],
        axis=1,
    ).reshape(-1)
    vector_term = jnp.concatenate([feature_terms, up_bias_grad])
    owned_vector_grads = lax.psum_scatter(
        vector_term, ("dp", "fsdp"), scatter_dimension=0, tiled=True
    )
    square_local = jnp.sum(owned_grads * owned_grads) + jnp.sum(
        owned_vector_grads * owned_vector_grads
    )
    square_total = lax.psum(square_local, ("dp", "fsdp"))
    grad_norm = jnp.sqrt(square_total)
    total_params = block_at_slot.shape[0] * BR * BC + vector_term.shape[0]
    clip_factor = jnp.minimum(1.0, math.sqrt(total_params) / (grad_norm + 1e-06))
    clipped = owned_grads * clip_factor
    new_first = 0.5 * first_moment + 0.5 * clipped
    rotated_grad = rotate_in(clipped, left_bases, right_bases)
    rotated_first = rotate_in(new_first, left_bases, right_bases)
    new_second = 0.5 * second_moment + 0.5 * rotated_grad * rotated_grad
    step_back = rotate_out(rotated_first / (jnp.sqrt(new_second) + 1e-08), left_bases, right_bases)
    updated = blocks - 0.01 * step_back
    vclipped = owned_vector_grads * clip_factor
    new_vector_first = 0.5 * vector_first + 0.5 * vclipped
    new_vector_second = 0.5 * vector_second + 0.5 * vclipped * vclipped
    vupdated = vectors - 0.1 * new_vector_first / (jnp.sqrt(new_vector_second) + 1e-08)
    head_max = lax.pmax(head_top, ("dp", "fsdp"))
    tau_value = jnp.mean(head_max)
    clip_factors = tau_value / jnp.maximum(head_max, tau_value)
    root_factor = jnp.sqrt(clip_factors)
    new_blocks = updated * column_scale(own_ids, root_factor)[:, None, :]
    positions = rank_all * vector_part + jnp.arange(vector_part, dtype=jnp.int32)
    new_vectors = vupdated * vector_scale(positions, root_factor)
    return (
        out_tokens,
        input_grad,
        owned_grads,
        owned_vector_grads,
        new_blocks,
        new_first,
        new_second,
        new_blocks.astype(jnp.bfloat16),
        new_vectors,
        new_vector_first,
        new_vector_second,
        new_vectors.astype(jnp.bfloat16),
        grad_norm,
        clip_factors,
    )


def solution(mesh):
    placed = (
        P("dp", "fsdp", None),
        P("dp", None),
        P("dp", "fsdp", None),
        P(),
        P(("dp", "fsdp"), None, None),
        P(("dp", "fsdp"), None, None),
        P(("dp", "fsdp"), None, None),
        P(("dp", "fsdp"), None, None),
        P(("dp", "fsdp"), None, None),
        P(("dp", "fsdp")),
        P(("dp", "fsdp")),
        P(("dp", "fsdp")),
    )
    return jax.shard_map(
        local,
        mesh=mesh,
        in_specs=placed,
        out_specs=(
            P("dp", "fsdp", None),
            P("dp", "fsdp", None),
            P(("dp", "fsdp"), None, None),
            P(("dp", "fsdp")),
            P(("dp", "fsdp"), None, None),
            P(("dp", "fsdp"), None, None),
            P(("dp", "fsdp"), None, None),
            P(("dp", "fsdp"), None, None),
            P(("dp", "fsdp")),
            P(("dp", "fsdp")),
            P(("dp", "fsdp")),
            P(("dp", "fsdp")),
            P(),
            P(),
        ),
        check_vma=False,
    )
```

profile of v0, /device:TPU:6, one launch (start us, length us, event | category | flops | bytes accessed | tf_op | source)
XLA Modules:
  0.0 6275.4 jit_solution(9201278841467124249)
XLA Ops:
  7.3 5.0 convert_element_type.167
  12.4 61.9 all-gather.2
  80.0 9.6 slice_reduce_fusion
  89.6 441.6 %all-gather.7.cloned.1.call-done = bf16[384,256,512]{2,1,0:T(8,128)(2,1)} async-done(((bf16[12,256,512]{2,1,0:T(8,128)(2,1)}), bf16[384,256,512]{2,1,0:T(8,128)(2,1)}) %all-gather.7.cloned.1.call-update) | async-done | bytes 100663312 | tf_op jit(solution)/shard_map/all_gather | solution.py:154
  531.2 66.6 %gather_fusion = bf16[384,256,512]{2,1,0:T(8,128)(2,1)} fusion(bf16[384,256,512]{2,1,0:T(8,128)(2,1)} %all-gather.7.cloned.1.call-done, s32[1024]{0:T(1024)S(1)} %pad_clamp_fusion), kind=kCustom, calls=%fused_computation | custom fusion | bytes 201328128 | tf_op jit(solution)/shard_map/gather | solution.py:157
  597.8 20.4 slice.89
  618.2 34.6 copy.79
  652.8 24.0 copy.112
  676.8 13.7 fusion.66
  690.5 2.7 slice.118
  693.9 4.0 fusion.58
  698.5 8.1 slice.95
  706.6 14.8 copy.83
  721.5 10.3 copy.113
  731.7 43.6 fusion.110
  775.3 56.2 copy.85
  831.5 31.0 copy.115
  862.5 31.2 copy.84
  893.7 31.0 copy.114
  924.7 2.3 copy.108
  927.0 6.4 copy.109
  933.4 5.9 fusion.111
  939.3 3.6 exponential_reduce_fusion
  945.1 9.3 fusion.59
  954.4 6.4 fusion.112
  961.8 32.4 multiply_convert_fusion.2
  994.2 31.9 convert_reduce_fusion
  1026.0 18.0 multiply_reduce_fusion.2
  1044.1 2.8 fusion.109
  1051.1 6.7 convolution_convert_fusion.1
  1057.8 2.3 copy.110
  1060.1 11.1 convolution_convert_fusion
  1071.2 6.5 copy.92
  1077.8 14.4 fusion.103
  1092.2 12.0 multiply_convert_fusion
  1104.2 4.0 multiply_convert_fusion.1
  1108.8 6.5 copy.90
  1115.4 3.0 scatter_custom_fusion
  1118.4 2.7 copy.94
  1121.1 8.7 convert_reduce_fusion.5
  1129.7 2.3 copy.93
  1132.0 22.5 reduce-scatter.6.cloned.1.call-done
  1154.5 79.6 %reduce-scatter.4.cloned.1.call-done = bf16[1,256,2048]{2,1,0:T(8,128)(2,1)} async-done(((bf16[1,1024,2048]{2,1,0:T(8,128)(2,1)}), bf16[1,256,2048]{2,1,0:T(8,128)(2,1)}) %reduce-scatter.4.cloned.1.call-update) | async-done | bytes 1048592 | tf_op jit(solution)/shard_map/reduce_scatter | solution.py:241
  1234.2 16.0 fusion.104
  1258.2 3257.6 %while.11 = (s32[]{:T(128)}, f32[384,256,512]{2,1,0:T(8,128)}, s32[384]{0:T(512)S(1)}, bf16[256,2048]{1,0:T(8,128)(2,1)}, bf16[256,6144]{1,0:T(8,128)(2,1)}, /*i...) while((s32[]{:T(128)}, f32[384,256,512]{2,1,0:T(8,128)}, ...), condition=%wide.region_21.22_spmd.clone, body=%wide.region_15.21_spmd.sunk.clone.sunk | while | flops 67108912 | bytes 1966778 | solution.py:282
  1424.0 2.1 conditional.4
  1432.5 2.1 conditional.4
  1458.0 2.1 conditional.4
  1755.0 2.1 conditional.4
  1856.7 2.1 conditional.4
  4516.1 52.5 pmax.7
  4570.6 24.8 fusion.43
  4596.8 1517.4 %reduce-scatter.8.cloned.1.call-done = f32[12,256,512]{2,1,0:T(8,128)} async-done(((f32[384,256,512]{2,1,0:T(8,128)}), f32[12,256,512]{2,1,0:T(8,128)}) %reduce-scatter.8.cloned.1.call-update) | async-done | bytes 6291472 | tf_op jit(solution)/shard_map/reduce_scatter | solution.py:281
  6114.2 5.0 multiply_reduce_fusion.1
  6120.5 5.1 add_bitcast_fusion
  6125.6 38.4 psum.7
  6164.7 6.2 add_multiply_fusion
  6171.0 2.7 copy-done.3
  6173.7 7.7 fusion.114
  6181.4 18.7 fusion.115
  6200.1 8.1 fusion.25
  6208.2 19.8 fusion.20
  6227.9 18.5 fusion.21
  6246.4 20.2 fusion.113
  (2076 shorter events, 2820.2 us)
Async XLA Ops:
  7.2 6166.5 %copy-start = (f32[12,256,256]{2,1,0:T(8,128)S(1)}, f32[12,256,256]{2,1,0:T(8,128)}, u32[]{:S(2)}) copy-start(f32[12,256,256]{2,1,0:T(8,128)} %param.26) | copy-start | bytes 9437188
  7.2 5.2 copy-start.27
  7.2 68.8 %copy-start.26 = (s32[384]{0:T(512)S(1)}, s32[384]{0:T(512)}, u32[]{:S(2)}) copy-start(s32[384]{0:T(512)} %param.22) | copy-start | bytes 4612
  7.2 523.9 %all-gather.7.cloned.1.call-start = ((), (), s32[]{:S(2)}) async-start(), calls=%async_computation.3 | async-start | bytes 103809024 | tf_op jit(solution)/shard_map/all_gather | solution.py:154
  12.3 914.6 %all-gather.11.cloned.1.call-start = ((), (), s32[]{:S(2)}) async-start(), calls=%async_computation.8 | async-start | bytes 5242880 | tf_op jit(solution)/shard_map/all_gather | solution.py:173
  76.3 521.5 %copy-start.40 = (s32[384]{0:T(512)}, s32[384]{0:T(512)S(1)}, u32[]{:S(2)}) copy-start(s32[384]{0:T(512)S(1)} %compare_select_fusion.1) | copy-start | bytes 4612
  77.7 599.0 %copy-start.30 = (f32[256]{0:T(256)}, f32[256]{0:T(256)S(1)}, u32[]{:S(2)}) copy-start(f32[256]{0:T(256)S(1)} %broadcast_multiply_fusion.1) | copy-start | bytes 3076
  79.4 0.6 copy-start.38
  80.0 596.8 %copy-start.34 = (f32[256]{0:T(256)}, f32[256]{0:T(256)S(1)}, u32[]{:S(2)}) copy-start(f32[256]{0:T(256)S(1)} %fusion.96) | copy-start | bytes 3076
  89.6 587.2 %copy-start.19 = (f32[2048]{0:T(1024)}, f32[2048]{0:T(1024)S(1)}, u32[]{:S(2)}) copy-start(f32[2048]{0:T(1024)S(1)} %get-tuple-element.215) | copy-start | bytes 24580
  89.6 587.2 %copy-start.23 = (f32[2048]{0:T(1024)}, f32[2048]{0:T(1024)S(1)}, u32[]{:S(2)}) copy-start(f32[2048]{0:T(1024)S(1)} %get-tuple-element.214) | copy-start | bytes 24580
  676.8 17.1 copy-start.43
  693.2 251.8 %all-gather.9.cloned.1.call-start = ((), (), s32[]{:S(2)}) async-start(), calls=%async_computation.7 | async-start | bytes 5242880 | tf_op jit(solution)/shard_map/all_gather | solution.py:174
  698.0 456.6 %reduce-scatter.6.cloned.1.call-start = ((), (), s32[]{:S(2)}) async-start(), calls=%async_computation.5 | async-start | bytes 5242880 | tf_op jit(solution)/shard_map/reduce_scatter | solution.py:244
  939.3 5.7 copy-start.1
  945.0 9.4 copy-start.17
  945.0 9.4 copy-start.42
  945.1 9.3 copy-start.6
  954.4 6.5 copy-start.12
  954.4 6.9 copy-start.21
  954.4 6.9 copy-start.25
  954.4 7.3 copy-start.22
  960.9 33.3 copy-start.5
  961.2 32.9 copy-start.32
  961.7 32.4 copy-start.15
  961.8 32.4 copy-start.9
  1026.0 18.0 copy-start.33
  1046.9 1.4 copy-start.4
  1046.9 10.9 copy-start.36
  1050.1 1.0 copy-start.11
  1051.1 9.0 copy-start.18
  1077.7 156.4 %reduce-scatter.4.cloned.1.call-start = ((), (), s32[]{:S(2)}) async-start(), calls=%async_computation.4 | async-start | bytes 5242880 | tf_op jit(solution)/shard_map/reduce_scatter | solution.py:241
  1092.2 12.0 copy-start.8
  1104.2 4.6 copy-start.2
  1115.3 3480.1 %all-reduce.3.cloned.1.call-start = ((), (), s32[]{:S(2)}) async-start(), calls=%async_computation.9 | async-start | bytes 196608
  1121.1 113.0 %copy-start.20 = (f32[2048]{0:T(1024)S(1)}, f32[2048]{0:T(1024)}, u32[]{:S(2)}) copy-start(f32[2048]{0:T(1024)} %copy-done.19) | copy-start | bytes 24580
  1121.1 113.0 %copy-start.31 = (f32[256]{0:T(256)S(1)}, f32[256]{0:T(256)}, u32[]{:S(2)}) copy-start(f32[256]{0:T(256)} %copy-done.30) | copy-start | bytes 3076
  1234.1 16.0 copy-start.13
  1234.1 16.1 copy-start.14
  1234.1 16.1 copy-start.16
  1234.1 18.0 copy-start.39
  1234.1 18.0 copy-start.7
  1234.1 18.0 copy-start.24
  1234.2 18.0 copy-start.35
  1250.2 4.0 copy-start.10
  1250.2 8.0 copy-start.46
  1258.1 4856.0 %reduce-scatter.8.cloned.1.call-start = ((), (), s32[]{:S(2)}) async-start(), calls=%async_computation.6 | async-start | bytes 207618048 | tf_op jit(solution)/shard_map/reduce_scatter | solution.py:281
  4515.8 54.9 copy-start.41
  4570.6 1549.8 %copy-start.37 = (f32[256]{0:T(256)S(1)}, f32[256]{0:T(256)}, u32[]{:S(2)}) copy-start(f32[256]{0:T(256)} %copy-done.36) | copy-start | bytes 3076
  4596.8 1669.8 %copy-start.29 = (f32[768]{0:T(1024)}, f32[768]{0:T(1024)S(1)}, u32[]{:S(2)}) copy-start(f32[768]{0:T(1024)S(1)} %get-tuple-element.243) | copy-start | bytes 9220
  6170.9 2.7 copy-start.3
  6173.6 26.4 slice-start
  6181.4 18.7 slice-start.1
  6246.4 20.2 copy-start.28
  6246.4 20.2 copy-start.44
  6246.4 20.2 copy-start.45
Sparse Core Ops, SparseCore 0:
  12.4 518.6 all-gather.6
  693.3 79.8 all-gather.10
  775.4 79.2 all-gather.8
  1077.9 76.6 reduce-scatter.5
  1156.8 77.2 reduce-scatter.3
  1258.3 120.6 all-reduce.2
  4515.9 1598.2 reduce-scatter.7
where the time goes:
time: 6330 us; the launch traced here: 6280 us
  waiting for transfers between devices  2060 us (33%)
  local copies, waits for them, and re-layouts  1380 us (22%)
  loops' own time  1270 us (20%)
  matrix products  1090 us (17%)
  other arithmetic  301 us (5%)
  blocking collectives  153 us (2%)
    reduce_scatter x1, waiting for transfers between devices, local(): lax.psum_scatter(lax.map(block_grad, block_at_slot), ('dp', 'fsdp'), scat...  1520 us
    another operation x1, loops' own time, local(): lax.map(block_grad, block_at_slot)  1250 us
    dot_general x384, matrix products, transposed_product(): lax.dot_general(left, right, (((0,), (0,)), ((), ())), preferred_element_...  796 us
    dynamic_update_slice x384, local copies, waits for them, and re-layouts, local(): lax.map(block_grad, block_at_slot)  722 us
    all_gather x1, waiting for transfers between devices, local(): lax.all_gather(block_low, ('dp', 'fsdp'), axis=0, tiled=True)  442 us
    reduce_sum x384, other arithmetic, block_grad(): jnp.sum(jnp.where(jnp.arange(4, dtype=jnp.int32) == matrix_id, first_ids,...  243 us
    dynamic_slice x384, local copies, waits for them, and re-layouts, local(): lax.map(block_grad, block_at_slot)  224 us
    reshape x4, local copies, waits for them, and re-layouts, to_matrix(): shaped = block_list.reshape(rows_all // BR, cols_all // BC, BR, BC)  137 us
  transfers between devices with their start and end apart: 7, of which 4 were waited for; matrix products, arithmetic and copies ran while one was open for 37% of the time, Pallas kernels for 0%

commit v1 on v0

v1 whole, which is shorter than its diff:
```python
import math

import jax
import jax.numpy as jnp
from jax import lax
from jax.experimental import pallas as pl
from jax.experimental.pallas import tpu as pltpu
from jax.sharding import Mesh
from jax.sharding import PartitionSpec as P

D = 2048
HEADS = 16
DH = 128
FF = 8192
BR = 256
BC = 512
TP = 8
LEN = 1024
CH = 256

F32 = jnp.float32
BF16 = jnp.bfloat16
NEG = -1e30
SCALE = DH ** (-0.5)

EVERY = ("o", "i", "c", "h", "l")
GROUP = ("i", "c", "l")


def at(array, index, axis=0):
    return lax.dynamic_index_in_dim(array, index, axis, keepdims=False)


def trade(array, axis):
    return lax.ppermute(array, axis, [(0, 1), (1, 0)])


def swap_tokens(array):
    return lax.ppermute(array, ("c", "h"), [(0, 0), (1, 2), (2, 1), (3, 3)])


def gather_axis(array, axis, size):
    if size == 1:
        return array[None]
    if size != 2:
        return lax.all_gather(array, axis, axis=0)
    other = trade(array, axis)
    mine = lax.axis_index(axis) == 0
    return jnp.stack([jnp.where(mine, array, other), jnp.where(mine, other, array)])


def scatter_axis(array, axis, size):
    if size == 1:
        return array[0]
    if size != 2:
        return lax.psum_scatter(array, axis, scatter_dimension=0, tiled=False)
    me = lax.axis_index(axis)
    other = trade(at(array, 1 - me), axis)
    return (at(array, me).astype(F32) + other.astype(F32)).astype(BF16)


def over_all(value, combine, collective, outer):
    for axis in ("l", "h", "c", "i"):
        value = combine(value, trade(value, axis))
    if outer == 1:
        return value
    if outer == 2:
        return combine(value, trade(value, "o"))
    return collective(value, "o")


def group_gather(array):
    return lax.all_gather(array, GROUP, axis=0, tiled=True)


def group_scatter(partial):
    i, c, l = (lax.axis_index(name) for name in GROUP)
    x = partial.reshape(2, 2, 2, CH, D)
    other = trade(at(x, 1 - c, 1), "c")
    y = (at(x, c, 1).astype(F32) + other.astype(F32)).astype(BF16)
    first, second = y[..., : D // 2], y[..., D // 2 :]
    first_other = trade(at(first, 1 - i, 0), "i")
    second_other = trade(at(second, 1 - l, 1), "l")
    first = (at(first, i, 0).astype(F32) + first_other.astype(F32)).astype(BF16)
    second = (at(second, l, 1).astype(F32) + second_other.astype(F32)).astype(BF16)
    first_other = trade(at(first, 1 - l), "l")
    second_other = trade(at(second, 1 - i), "i")
    first = at(first, l).astype(F32) + first_other.astype(F32)
    second = at(second, i).astype(F32) + second_other.astype(F32)
    return jnp.concatenate([first, second], axis=1)


def norm_parts(hidden):
    average = jnp.mean(hidden, axis=-1, keepdims=True)
    centred = hidden - average
    variance = jnp.mean(centred * centred, axis=-1, keepdims=True)
    inverse = lax.rsqrt(variance + 1e-05)
    return centred * inverse, inverse


def norm_back(grad, unit, inverse, gain):
    scaled = grad * gain
    inner = jnp.mean(scaled * unit, axis=-1, keepdims=True)
    back = inverse * (scaled - jnp.mean(scaled, axis=-1, keepdims=True) - unit * inner)
    return back, jnp.sum(grad * unit, axis=0), jnp.sum(grad, axis=0)


def contract(left, right, left_dim, right_dim):
    return lax.dot_general(
        left, right, (((left_dim,), (right_dim,)), ((), ())), preferred_element_type=F32
    )


def allowed_pairs(seg_col, seg_row, j, low, high):
    rows = j * CH + lax.broadcasted_iota(jnp.int32, (CH, high - low), 0)
    cols = low + lax.broadcasted_iota(jnp.int32, (CH, high - low), 1)
    same = seg_col[0, j * CH : (j + 1) * CH, :] == seg_row[0, :, low:high]
    return same & (cols <= rows)


def attend_kernel(seg_col, seg_row, q_ref, k_ref, v_ref, o_ref, lse_ref, top_ref):
    top = jnp.full((1, 1), NEG, F32)
    for j in range(LEN // CH):
        low, high = max(0, j - 2) * CH, (j + 1) * CH
        scores = contract(q_ref[j * CH : high, :], k_ref[low:high, :], 1, 1) * SCALE
        scores = jnp.where(allowed_pairs(seg_col, seg_row, j, low, high), scores, NEG)
        peak = jnp.max(scores, axis=-1, keepdims=True)
        weights = jnp.exp(scores - peak)
        total = jnp.sum(weights, axis=-1, keepdims=True)
        probs = (weights * (1.0 / total)).astype(BF16)
        o_ref[j * CH : high, :] = contract(probs, v_ref[low:high, :], 1, 0).astype(BF16)
        lse_ref[0, j * CH : high, :] = peak + jnp.log(total)
        top = jnp.maximum(top, jnp.max(peak, axis=0, keepdims=True))
    top_ref[0] = jnp.broadcast_to(top, (8, 128))


def attend_back_kernel(
    seg_col, seg_row, q_ref, k_ref, v_ref, do_ref, lse_ref, dq_ref, dk_ref, dv_ref, dk_sum, dv_sum
):
    dk_sum[...] = jnp.zeros_like(dk_sum)
    dv_sum[...] = jnp.zeros_like(dv_sum)
    for j in range(LEN // CH):
        low, high = max(0, j - 2) * CH, (j + 1) * CH
        query, keys = q_ref[j * CH : high, :], k_ref[low:high, :]
        grad = do_ref[j * CH : high, :]
        scores = contract(query, keys, 1, 1) * SCALE
        allowed = allowed_pairs(seg_col, seg_row, j, low, high)
        probs = jnp.where(allowed, jnp.exp(scores - lse_ref[0, j * CH : high, :]), 0.0)
        grad_probs = contract(grad, v_ref[low:high, :], 1, 1)
        inner = jnp.sum(probs * grad_probs, axis=-1, keepdims=True)
        grad_scores = (probs * (grad_probs - inner)).astype(BF16)
        dq_ref[j * CH : high, :] = (contract(grad_scores, keys, 1, 0) * SCALE).astype(BF16)
        dk_sum[low:high, :] += contract(grad_scores, query, 0, 0)
        dv_sum[low:high, :] += contract(probs.astype(BF16), grad, 0, 0)
    dk_ref[...] = (dk_sum[...] * SCALE).astype(BF16)
    dv_ref[...] = dv_sum[...].astype(BF16)


def head_specs():
    seg_col = pl.BlockSpec((1, LEN, 1), lambda s, h: (s, 0, 0))
    seg_row = pl.BlockSpec((1, 1, LEN), lambda s, h: (s, 0, 0))
    thirds = [pl.BlockSpec((LEN, DH), lambda s, h, n=n: (s, 2 * n + h)) for n in range(3)]
    lse = pl.BlockSpec((1, LEN, 1), lambda s, h: (2 * s + h, 0, 0))
    return seg_col, seg_row, thirds, lse


def attend(seg_col, seg_row, qkv):
    seg_c, seg_r, thirds, lse = head_specs()
    return pl.pallas_call(
        attend_kernel,
        name="attend",
        grid=(2, 2),
        in_specs=[seg_c, seg_r, *thirds],
        out_specs=[thirds[0], lse, pl.BlockSpec((1, 8, 128), lambda s, h: (2 * s + h, 0, 0))],
        out_shape=[
            jax.ShapeDtypeStruct((2 * LEN, 2 * DH), BF16),
            jax.ShapeDtypeStruct((4, LEN, 1), F32),
            jax.ShapeDtypeStruct((4, 8, 128), F32),
        ],
        compiler_params=pltpu.CompilerParams(vmem_limit_bytes=40 << 20),
        cost_estimate=pl.CostEstimate(flops=1 << 31, bytes_accessed=6 << 20, transcendentals=1 << 22),
    )(seg_col, seg_row, qkv, qkv, qkv)


def attend_back(seg_col, seg_row, qkv, grad, lse_all):
    seg_c, seg_r, thirds, lse = head_specs()
    return pl.pallas_call(
        attend_back_kernel,
        name="attend_back",
        grid=(2, 2),
        in_specs=[seg_c, seg_r, *thirds, thirds[0], lse],
        out_specs=[thirds[0]] * 3,
        out_shape=[jax.ShapeDtypeStruct((2 * LEN, 2 * DH), BF16)] * 3,
        scratch_shapes=[pltpu.VMEM((LEN, DH), F32), pltpu.VMEM((LEN, DH), F32)],
        compiler_params=pltpu.CompilerParams(vmem_limit_bytes=40 << 20),
        cost_estimate=pl.CostEstimate(flops=5 << 30, bytes_accessed=8 << 20, transcendentals=1 << 22),
    )(seg_col, seg_row, qkv, qkv, qkv, grad, lse_all)


def block_tables(owners, per_owner, rank):
    ids = jnp.arange(owners.shape[0], dtype=jnp.int32)
    earlier = (owners[None, :] == owners[:, None]) & (ids[None, :] < ids[:, None])
    slots = owners * per_owner + jnp.sum(earlier.astype(jnp.int32), axis=1)
    mine = rank * per_owner + jnp.arange(per_owner, dtype=jnp.int32)
    own_ids = jnp.sum(jnp.where(slots[None, :] == mine[:, None], ids[None, :], 0), axis=1)
    return slots, own_ids


def column_scale(block_ids, root_factor):
    per_row = 3 * D // BC
    columns = (block_ids % per_row)[:, None] * BC + jnp.arange(BC, dtype=jnp.int32)[None, :]
    head_of = columns % D // DH
    picked = jnp.sum(
        jnp.where(head_of[..., None] == jnp.arange(HEADS, dtype=jnp.int32), root_factor, 0.0), axis=-1
    )
    inside = (block_ids < D // BR * per_row)[:, None] & (columns < 2 * D)
    return jnp.where(inside, picked, 1.0)


def vector_scale(positions, root_factor):
    inside = (positions < 8 * D) & (positions % 8 == 2)
    head_of = positions // 8 // DH
    picked = jnp.sum(
        jnp.where(head_of[:, None] == jnp.arange(HEADS, dtype=jnp.int32), root_factor, 0.0), axis=-1
    )
    return jnp.where(inside, picked, 1.0)


def rotate(left, matrix, right, left_dim, right_dim):
    done = lax.dot_general(
        left, matrix, (((left_dim,), (1,)), ((0,), (0,))),
        precision=lax.Precision.HIGH, preferred_element_type=F32,
    )
    return lax.dot_general(
        done, right, (((2,), (right_dim,)), ((0,), (0,))),
        precision=lax.Precision.HIGH, preferred_element_type=F32,
    )


def make_local(outer):
    devices = outer * 16
    rows = BR // devices
    qkv_end = D // BR * (3 * D // BC)
    out_end = qkv_end + D // BR * (D // BC)
    up_end = out_end + D // BR * (FF // BC)

    def pieces_to_group(pieces):
        got = lax.all_to_all(pieces, GROUP, 0, 0, tiled=True)
        return gather_axis(gather_axis(got, "h", 2), "o", outer)

    def piece_major(full, unit_shape):
        return full.reshape(outer, 2, 2, 2, 2, *unit_shape)

    def in_qkv(full):
        full = piece_major(full, (8, 3, rows, CH))
        return full.transpose(5, 0, 2, 3, 1, 4, 7, 6, 8).reshape(D, 3 * CH)

    def in_out(full):
        full = piece_major(full, (4, rows, BC))
        return full.transpose(0, 2, 3, 1, 4, 6, 5, 7).reshape(CH, D)

    def in_up(full):
        full = piece_major(full, (8, 2, rows, BC))
        return full.transpose(5, 0, 2, 3, 1, 4, 7, 6, 8).reshape(D, FF // TP)

    def in_down(full):
        full = piece_major(full, (4, 4, rows, BC))
        return full.transpose(5, 0, 2, 3, 1, 4, 7, 6, 8).reshape(FF // TP, D)

    def reduce_pieces(full):
        part = scatter_axis(scatter_axis(full, "o", outer), "h", 2)
        return lax.all_to_all(part, GROUP, 0, 0, tiled=True)

    def out_three(grad, row_units, col_units, width):
        full = grad.astype(BF16).reshape(row_units, outer, 2, 2, 2, 2, rows, col_units, width)
        full = full.transpose(1, 4, 2, 3, 5, 0, 7, 6, 8)
        return full.reshape(outer, 2, TP * row_units * col_units, rows, width)

    def local(
        tokens, segments, out_grad, owners, blocks, first_moment, second_moment,
        left_bases, right_bases, vectors, vector_first, vector_second,
    ):
        per_owner, vector_part = blocks.shape[0], vectors.shape[0]
        o, i, c, h, l = (lax.axis_index(name) for name in EVERY)
        rank = (((o * 2 + i) * 2 + c) * 2 + h) * 2 + l
        member = (i * 2 + c) * 2 + l
        slots, own_ids = block_tables(owners, per_owner, rank)

        order = jnp.concatenate(
            [
                slots[:qkv_end].reshape(8, 3, 4).transpose(2, 0, 1).reshape(-1),
                slots[qkv_end:out_end],
                slots[out_end:up_end].reshape(8, 8, 2).transpose(1, 0, 2).reshape(-1),
                slots[up_end:],
            ]
        )
        pick = (order[:, None] == jnp.arange(order.shape[0], dtype=jnp.int32)[None, :]).astype(BF16)
        sent = blocks.astype(BF16).reshape(per_owner, devices, rows, BC).transpose(1, 0, 2, 3)
        pieces = lax.all_to_all(sent.reshape(-1, rows, BC), EVERY, 0, 0, tiled=True)
        pieces = lax.dot_general(pick, pieces, (((1,), (0,)), ((), ())), preferred_element_type=BF16)
        part_qkv = (
            pieces[:qkv_end].reshape(4, 24, rows, 2, CH).transpose(0, 3, 1, 2, 4).reshape(-1, rows, CH)
        )
        w_qkv = in_qkv(pieces_to_group(part_qkv))
        w_out = in_out(pieces_to_group(pieces[qkv_end:out_end]))
        w_up = in_up(pieces_to_group(pieces[out_end:up_end]))
        w_down = in_down(pieces_to_group(pieces[up_end:]))

        vector_all = vectors.astype(BF16)
        for axis in ("l", "h", "c", "i"):
            vector_all = gather_axis(vector_all, axis, 2).reshape(-1)
        vector_all = gather_axis(vector_all, "o", outer).reshape(-1).astype(F32)
        feature = vector_all[: 8 * D].reshape(D, 8)
        ln1_gain, ln1_shift, q_bias, v_bias, out_bias, ln2_gain, ln2_shift, down_bias = (
            feature[:, n] for n in range(8)
        )
        up_bias = lax.dynamic_slice_in_dim(vector_all, 8 * D + member * (FF // TP), FF // TP)
        qkv_bias = jnp.concatenate(
            [
                lax.dynamic_slice_in_dim(q_bias, member * CH, CH),
                jnp.zeros((CH,), F32),
                lax.dynamic_slice_in_dim(v_bias, member * CH, CH),
            ]
        )

        x = swap_tokens(tokens.reshape(CH, D)).astype(F32)
        dy = swap_tokens(out_grad.reshape(CH, D))
        dy_all = group_gather(dy)
        seg = jnp.where(c == h, segments, trade(segments, "c"))
        seg = gather_axis(seg, "i", 2).reshape(2, LEN)
        seg_col, seg_row = seg[:, :, None], seg[:, None, :]
        unit1, inverse1 = norm_parts(x)
        a_all = group_gather((unit1 * ln1_gain + ln1_shift).astype(BF16))
        qkv = (jnp.dot(a_all, w_qkv, preferred_element_type=F32) + qkv_bias).astype(BF16)
        mixed, lse, tops = attend(seg_col, seg_row, qkv)
        attended = group_scatter(jnp.dot(mixed, w_out, preferred_element_type=F32).astype(BF16))
        h1 = x + attended + out_bias
        unit2, inverse2 = norm_parts(h1)
        c_all = group_gather((unit2 * ln2_gain + ln2_shift).astype(BF16))
        u = jnp.dot(c_all, w_up, preferred_element_type=F32) + up_bias
        cdf = 0.5 * (1.0 + lax.erf(u * math.sqrt(0.5)))
        g = (u * cdf).astype(BF16)
        branch = group_scatter(jnp.dot(g, w_down, preferred_element_type=F32).astype(BF16))
        out_tokens = swap_tokens((h1 + branch + down_bias).astype(BF16))

        dg = contract(dy_all, w_down, 1, 1)
        slope = cdf + u * jnp.exp(-0.5 * u * u) * (1.0 / math.sqrt(2.0 * math.pi))
        du = (dg * slope).astype(BF16)
        dc = group_scatter(contract(du, w_up, 1, 1).astype(BF16))
        back2, ln2_gain_grad, ln2_shift_grad = norm_back(dc, unit2, inverse2, ln2_gain)
        dh1 = dy.astype(F32) + back2
        da_own = dh1.astype(BF16)
        da_all = group_gather(da_own)
        do = contract(da_all, w_out, 1, 1).astype(BF16)
        dqkv = jnp.concatenate(attend_back(seg_col, seg_row, qkv, do, lse), axis=1)
        da = group_scatter(contract(dqkv, w_qkv, 1, 1).astype(BF16))
        back1, ln1_gain_grad, ln1_shift_grad = norm_back(da, unit1, inverse1, ln1_gain)
        input_grad = swap_tokens((dh1 + back1).astype(BF16)).astype(F32)

        got_down = reduce_pieces(out_three(contract(g, dy_all, 0, 0), 4, 4, BC))
        got_up = reduce_pieces(out_three(contract(c_all, du, 0, 0), 8, 2, BC))
        got_out = reduce_pieces(out_three(contract(mixed, da_all, 0, 0), 1, 4, BC))
        got_qkv = reduce_pieces(out_three(contract(a_all, dqkv, 0, 0), 8, 3, CH))
        got_qkv = got_qkv.reshape(4, 2, 24, rows, CH).transpose(0, 2, 3, 1, 4).reshape(-1, rows, BC)
        got = jnp.concatenate([got_qkv, got_out, got_up, got_down], axis=0)
        got = lax.dot_general(pick, got, (((0,), (0,)), ((), ())), preferred_element_type=BF16)
        got = lax.all_to_all(got, EVERY, 0, 0, tiled=True)
        block_grads = (
            got.reshape(devices, per_owner, rows, BC).transpose(1, 0, 2, 3)
            .reshape(per_owner, BR, BC).astype(F32)
        )

        dqkv_sum = jnp.sum(dqkv.astype(F32), axis=0)

        def spread(values, size):
            return lax.dynamic_update_slice_in_dim(jnp.zeros((size,), F32), values, member * values.shape[0], 0)

        terms = jnp.stack(
            [
                ln1_gain_grad, ln1_shift_grad, spread(dqkv_sum[:CH], D), spread(dqkv_sum[2 * CH :], D),
                jnp.sum(da_own.astype(F32), axis=0), ln2_gain_grad, ln2_shift_grad,
                jnp.sum(dy.astype(F32), axis=0),
            ],
            axis=1,
        ).reshape(-1)
        terms = jnp.concatenate([terms, spread(jnp.sum(du.astype(F32), axis=0), FF)])
        terms = lax.all_to_all(terms.reshape(devices, vector_part), EVERY, 0, 0, tiled=True)
        vector_grads = jnp.sum(terms, axis=0)

        square = jnp.sum(block_grads * block_grads) + jnp.sum(vector_grads * vector_grads)
        grad_norm = jnp.sqrt(over_all(square, jnp.add, lax.psum, outer))
        total_params = slots.shape[0] * BR * BC + vector_part * devices
        clip = jnp.minimum(1.0, math.sqrt(total_params) / (grad_norm + 1e-06))
        turned_first = rotate(left_bases, first_moment, right_bases, 1, 1)
        turned_grad = rotate(left_bases, block_grads, right_bases, 1, 1)
        new_first = 0.5 * first_moment + (0.5 * clip) * block_grads
        new_second = 0.5 * second_moment + 0.5 * jnp.square(clip * turned_grad)
        ratio = (0.5 * turned_first + (0.5 * clip) * turned_grad) / (jnp.sqrt(new_second) + 1e-08)
        updated = blocks - 0.01 * rotate(left_bases, ratio, right_bases, 2, 2)
        vclipped = vector_grads * clip
        new_vector_first = 0.5 * vector_first + 0.5 * vclipped
        new_vector_second = 0.5 * vector_second + 0.5 * vclipped * vclipped
        vupdated = vectors - 0.1 * new_vector_first / (jnp.sqrt(new_vector_second) + 1e-08)
        head_ids = jnp.arange(HEADS, dtype=jnp.int32)
        tops = jnp.max(tops[:, 0, 0].reshape(2, 2), axis=0)
        tops = jnp.where(head_ids // 2 == member, jnp.where(head_ids % 2 == 0, tops[0], tops[1]), NEG)
        head_max = over_all(tops, jnp.maximum, lax.pmax, outer)
        tau = jnp.mean(head_max)
        clip_factors = tau / jnp.maximum(head_max, tau)
        root_factor = jnp.sqrt(clip_factors)
        new_blocks = updated * column_scale(own_ids, root_factor)[:, None, :]
        positions = rank * vector_part + jnp.arange(vector_part, dtype=jnp.int32)
        new_vectors = vupdated * vector_scale(positions, root_factor)
        return (
            out_tokens[None],
            input_grad[None],
            block_grads,
            vector_grads,
            new_blocks,
            new_first,
            new_second,
            new_blocks.astype(BF16),
            new_vectors,
            new_vector_first,
            new_vector_second,
            new_vectors.astype(BF16),
            grad_norm,
            clip_factors,
        )

    return local


def solution(mesh):
    outer = mesh.shape["dp"] // 4
    fine = Mesh(mesh.devices.reshape(outer, 2, 2, 2, 2), EVERY)
    seq, pos = ("o", "i", "c"), ("h", "l")
    token, owned, entry = P(seq, pos, None), P(EVERY, None, None), P(EVERY)
    return jax.shard_map(
        make_local(outer),
        mesh=fine,
        in_specs=(token, P(seq, None), token, P(), *[owned] * 5, *[entry] * 3),
        out_specs=(token, token, owned, entry, *[owned] * 4, *[entry] * 4, P(), P()),
        check_vma=False,
    )
```

time: 6330 us -> 1360 us (0.21)
  waiting for transfers between devices: 2060 us -> 574 us
  loops' own time: 1270 us -> 0 us
  local copies, waits for them, and re-layouts: 1380 us -> 156 us
  matrix products: 1090 us -> 206 us
  starting transfers between devices: 0.46 us -> 190 us
  other arithmetic: 301 us -> 136 us
  blocking collectives: 153 us -> 34.1 us
    reduce_scatter x3 -> x0, waiting for transfers between devices: 1620 us -> none  [the longest x1 1520 us: local(): lax.psum_scatter(lax.map(block_grad, block_at_slot), ('dp', 'fsdp'), scat...]
    another operation x385 -> x0, loops' own time: 1270 us -> none  [the longest x1 1250 us: local(): lax.map(block_grad, block_at_slot)]
    dot_general x404 -> x20, matrix products: 1090 us -> 206 us  [the longest x8 80.6 us: contract(): lax.dot_general(left, right, (((left_dim,), (right_dim,)), ((), ())), pre...]
    dynamic_update_slice x384 -> x3, local copies, waits for them, and re-layouts: 722 us -> 1.44 us  [spread(): lax.dynamic_update_slice_in_dim(jnp.zeros((size,), F32), values, member *...]
    ppermute x0 -> x57, waiting for transfers between devices: none -> 445 us  [the longest x53 445 us: trade(): return lax.ppermute(array, axis, [(0, 1), (1, 0)])]
    all_gather x3 -> x4, waiting for transfers between devices: 442 us -> 0.03 us  [group_gather(): return lax.all_gather(array, GROUP, axis=0, tiled=True)]
    reduce_sum x396 -> x14, other arithmetic: 264 us -> 22.5 us  [the longest x1 4.87 us: local(): jnp.sum(da_own.astype(F32), axis=0)]
    dynamic_slice x385 -> x10, local copies, waits for them, and re-layouts: 224 us -> 35.1 us  [the longest x8 34 us: at(): return lax.dynamic_index_in_dim(array, index, axis, keepdims=False)]
  transfers between devices with their start and end apart: 7 -> 70, of which waited for: 4 -> 43; matrix products, arithmetic and copies ran while one was open for 37% -> 26% of each run, Pallas kernels for 0% -> 1%
where the time goes in v1:
time: 1360 us; the launch traced here: 1340 us
  waiting for transfers between devices  574 us (42%)
  matrix products  206 us (15%)
  starting transfers between devices  190 us (14%)
  local copies, waits for them, and re-layouts  156 us (11%)
  other arithmetic  136 us (10%)
  blocking collectives  34.1 us (3%)
  Pallas kernels  22.3 us (2%)
  between operations  21.8 us (2%)
    ppermute x53, waiting for transfers between devices, trade(): return lax.ppermute(array, axis, [(0, 1), (1, 0)])  445 us
    ppermute x53, starting transfers between devices, trade(): return lax.ppermute(array, axis, [(0, 1), (1, 0)])  84.5 us
    dot_general x8, matrix products, contract(): lax.dot_general(left, right, (((left_dim,), (right_dim,)), ((), ())), pre...  80.6 us
    all_to_all x1, waiting for transfers between devices, local(): pieces = lax.all_to_all(sent.reshape(-1, rows, BC), EVERY, 0, 0, tiled=True)  70.7 us
    dot_general x3, matrix products, rotate(): lax.dot_general(done, right, (((2,), (right_dim,)), ((0,), (0,))), precis...  53.5 us
    all_to_all x2, waiting for transfers between devices, pieces_to_group(): got = lax.all_to_all(pieces, GROUP, 0, 0, tiled=True)  46.6 us
    ppermute x4, starting transfers between devices, swap_tokens(): return lax.ppermute(array, ('c', 'h'), [(0, 0), (1, 2), (2, 1), (3, 3)])  37.9 us
    unnamed x174, local copies, waits for them, and re-layouts  36.3 us
  transfers between devices with their start and end apart: 70, of which 43 were waited for; matrix products, arithmetic and copies ran while one was open for 26% of the time, Pallas kernels for 1%

profile of v1, /device:TPU:6, one launch (start us, length us, event | category | flops | bytes accessed | tf_op | source)
XLA Modules:
  0.0 1341.2 jit_solution(3861851750356842239)
XLA Ops:
  19.0 9.5 collective-permute-start
  34.8 9.4 slice_reduce_fusion
  55.8 9.4 all-to-all-start
  66.9 70.7 %all-to-all-done = bf16[384,8,512]{2,1,0:T(8,128)(2,1)} async-done(((bf16[384,8,512]{2,1,0:T(8,128)(2,1)}), bf16[384,8,512]{2,1,0:T(8,128)(2,1)}, u32[]{:S(2)}, u32[]{:S(2)}) %all-to-all-start) | async-done | bytes 3145760 | tf_op jit(solution)/shard_map/all_to_all | solution.py:299
  149.1 14.2 %all_to_all.59 = bf16[192,8,256]{2,1,0:T(8,128)(2,1)S(1)} all-to-all(bf16[192,8,256]{2,1,0:T(8,128)(2,1)S(1)} %bitcast.347), channel_id=1, replica_groups=mesh['o'=2,'i'=2,'c'=2,'h'=2,'l'=2] {'i','c','l'}, dimensions={0} | all-to-all | bytes 1572864 | tf_op jit(solution)/shard_map/all_to_all | solution.py:248
  167.7 20.0 %all_to_all.60 = bf16[32,8,512]{2,1,0:T(8,128)(2,1)S(1)} all-to-all(bf16[32,8,512]{2,1,0:T(8,128)(2,1)S(1)} %copy.212), channel_id=1, replica_groups=mesh['o'=2,'i'=2,'c'=2,'h'=2,'l'=2] {'i','c','l'}, dimensions={0} | all-to-all | bytes 524288 | tf_op jit(solution)/shard_map/all_to_all | solution.py:248
  189.1 19.0 %collective-permute-done.8 = bf16[192,8,256]{2,1,0:T(8,128)(2,1)S(1)} collective-permute-done((bf16[192,8,256]{2,1,0:T(8,128)(2,1)S(1)}, bf16[192,8,256]{2,1,0:T(8,128)(2,1)S(1)}, u32[]{:S(2)}, u32[]{:S(2)}) %collective-permute-start.8) | collective-permute-done | bytes 786464 | tf_op jit(solution)/shard_map/ppermute | solution.py:35
  220.1 37.9 %collective-permute-done.11 = bf16[2,32,8,512]{3,2,1,0:T(8,128)(2,1)} collective-permute-done((bf16[2,32,8,512]{3,2,1,0:T(8,128)(2,1)}, bf16[2,32,8,512]{3,2,1,0:T(8,128)(2,1)}, u32[]{:S(2)}, u32[]{:S(2)}) %collective-permute-start.11) | collective-permute-done | bytes 524320 | tf_op jit(solution)/shard_map/ppermute | solution.py:35
  271.4 10.1 add_convert_fusion.q_ref.k_ref.v_ref
  281.5 9.6 attend.1
  302.6 7.5 collective-permute-done.12
  310.1 5.4 fusion.9
  323.1 22.1 %collective-permute-done.13 = bf16[2,256,1024]{2,1,0:T(8,128)(2,1)} collective-permute-done((bf16[2,256,1024]{2,1,0:T(8,128)(2,1)}, bf16[2,256,1024]{2,1,0:T(8,128)(2,1)}, u32[]{:S(2)}, u32[]{:S(2)}) %collective-permute-start.13) | collective-permute-done | bytes 1048608 | tf_op jit(solution)/shard_map/ppermute | solution.py:35
  350.9 9.4 collective-permute-done.14
  367.5 9.5 collective-permute-start.27
  381.3 21.0 %all-to-all-start.3 = ((bf16[128,8,512]{2,1,0:T(8,128)(2,1)}), bf16[128,8,512]{2,1,0:T(8,128)(2,1)}, u32[]{:S(2)}, u32[]{:S(2)}) async-start(bf16[128,8,512]{2,1,0:T(8,128)(2,1)} %copy.217), calls=%async_computation.3 | async-start | bytes 2097152 | tf_op jit(solution)/shard_map/all_to_all | solution.py:248
  405.1 16.7 %all-to-all-done.3 = bf16[128,8,512]{2,1,0:T(8,128)(2,1)} async-done(((bf16[128,8,512]{2,1,0:T(8,128)(2,1)}), bf16[128,8,512]{2,1,0:T(8,128)(2,1)}, u32[]{:S(2)}, u32[]{:S(2)}) %all-to-all-start.3) | async-done | bytes 1048608 | tf_op jit(solution)/shard_map/all_to_all | solution.py:248
  421.8 5.7 all-to-all-start.4
  431.2 29.9 %all-to-all-done.4 = bf16[128,8,512]{2,1,0:T(8,128)(2,1)} async-done(((bf16[128,8,512]{2,1,0:T(8,128)(2,1)}), bf16[128,8,512]{2,1,0:T(8,128)(2,1)}, u32[]{:S(2)}, u32[]{:S(2)}) %all-to-all-start.4) | async-done | bytes 1048608 | tf_op jit(solution)/shard_map/all_to_all | solution.py:248
  461.8 33.9 %collective-permute-done.17 = bf16[128,8,512]{2,1,0:T(8,128)(2,1)} collective-permute-done((bf16[128,8,512]{2,1,0:T(8,128)(2,1)}, bf16[128,8,512]{2,1,0:T(8,128)(2,1)}, u32[]{:S(2)}, u32[]{:S(2)}) %collective-permute-start.17) | collective-permute-done | bytes 1048608 | tf_op jit(solution)/shard_map/ppermute | solution.py:35
  499.5 23.0 %collective-permute-done.19 = bf16[128,8,512]{2,1,0:T(8,128)(2,1)S(1)} collective-permute-done((bf16[128,8,512]{2,1,0:T(8,128)(2,1)}, bf16[128,8,512]{2,1,0:T(8,128)(2,1)S(1)}, u32[]{:S(2)}, u32[]{:S(2)}) %collective-permute-start.19) | collective-permute-done | bytes 1048608 | tf_op jit(solution)/shard_map/ppermute | solution.py:35
  526.8 21.2 %collective-permute-done.18 = bf16[2,128,8,512]{3,2,1,0:T(8,128)(2,1)} collective-permute-done((bf16[2,128,8,512]{3,2,1,0:T(8,128)(2,1)}, bf16[2,128,8,512]{3,2,1,0:T(8,128)(2,1)}, u32[]{:S(2)}, u32[]{:S(2)}) %collective-permute-start.18) | collective-permute-done | bytes 2097184 | tf_op jit(solution)/shard_map/ppermute | solution.py:35
  556.6 9.7 pad_maximum_fusion.1
  566.3 5.9 copy.265
  572.3 16.9 %collective-permute-done.20 = bf16[2,128,8,512]{3,2,1,0:T(8,128)(2,1)} collective-permute-done((bf16[2,128,8,512]{3,2,1,0:T(8,128)(2,1)}, bf16[2,128,8,512]{3,2,1,0:T(8,128)(2,1)}, u32[]{:S(2)}, u32[]{:S(2)}) %collective-permute-start.20) | collective-permute-done | bytes 2097184 | tf_op jit(solution)/shard_map/ppermute | solution.py:35
  599.6 15.2 %multiply_convert_fusion = (bf16[2048,1024]{1,0:T(8,128)(2,1)S(1)}, f32[2048,1024]{1,0:T(8,128)}) fusion(f32[1024]{0:T(1024)S(1)} %dynamic_slice.205, bf16[2048,2048]{1,0:T(8,128)(2,1)} %all-gather.7.cloned.1.call-done, bf16[2048,1024]{1,0:T(8,128)(2,1)} %bitcast.333), kind=kOutput, calls=%fused_computation.16 | convolution fusion | flops 8602517504 | bytes 25169920 | tf_op jit(solution)/shard_map/dot_general | solution.py:340
  614.9 10.9 convolution_convert_fusion.2
  625.8 6.7 constant_dynamic-slice_fusion.5
  634.9 17.0 %convert_reduce_fusion = (f32[1024]{0:T(1024)}, bf16[2048,1024]{1,0:T(8,128)(2,1)S(1)}) fusion(f32[2048,1024]{1,0:T(8,128)} %get-tuple-element.114, f32[1024]{0:T(1024)S(1)} %dynamic_slice.205, bf16[1024,2048]{1,0:T(8,128)(2,1)} %bitcast.335, bf16[2048,2048]{1,0:T(8,128)(2,1)} %all-gather.9.cloned.1.call-done), kind=kOutput, calls=%fused_computation.15 | convolution fusion | flops 8617196544 | bytes 25174016 | tf_op jit(solution)/shard_map/dot_general | solution.py:109
  651.8 11.3 convolution_convert_fusion.1
  675.9 7.1 collective-permute-start.22
  689.8 17.4 %collective-permute-done.22 = bf16[2,256,1024]{2,1,0:T(8,128)(2,1)} collective-permute-done((bf16[2,256,1024]{2,1,0:T(8,128)(2,1)S(1)}, bf16[2,256,1024]{2,1,0:T(8,128)(2,1)}, u32[]{:S(2)}, u32[]{:S(2)}) %collective-permute-start.22) | collective-permute-done | bytes 1048608 | tf_op jit(solution)/shard_map/ppermute | solution.py:35
  709.5 19.8 %collective-permute-done.29 = bf16[2,256,1024]{2,1,0:T(8,128)(2,1)S(1)} collective-permute-done((bf16[2,256,1024]{2,1,0:T(8,128)(2,1)S(1)}, bf16[2,256,1024]{2,1,0:T(8,128)(2,1)S(1)}, u32[]{:S(2)}, u32[]{:S(2)}) %collective-permute-start.29) | collective-permute-done | bytes 1048608 | tf_op jit(solution)/shard_map/ppermute | solution.py:35
  737.3 20.4 %collective-permute-done.30 = bf16[256,1024]{1,0:T(8,128)(2,1)S(1)} collective-permute-done((bf16[256,1024]{1,0:T(8,128)(2,1)S(1)}, bf16[256,1024]{1,0:T(8,128)(2,1)S(1)}, u32[]{:S(2)}, u32[]{:S(2)}) %collective-permute-start.30) | collective-permute-done | bytes 524320 | tf_op jit(solution)/shard_map/ppermute | solution.py:35
  759.8 4.9 convert_reduce_fusion.4
  764.7 12.8 convolution_convert_fusion.5
  782.7 11.8 convolution_convert_fusion.4
  799.1 29.5 %collective-permute-done.43 = bf16[2,128,8,512]{3,2,1,0:T(8,128)(2,1)} collective-permute-done((bf16[2,128,8,512]{3,2,1,0:T(8,128)(2,1)}, bf16[2,128,8,512]{3,2,1,0:T(8,128)(2,1)}, u32[]{:S(2)}, u32[]{:S(2)}) %collective-permute-start.43) | collective-permute-done | bytes 2097184 | tf_op jit(solution)/shard_map/ppermute | solution.py:35
  835.5 36.3 %collective-permute-done.45 = bf16[2,128,8,512]{3,2,1,0:T(8,128)(2,1)} collective-permute-done((bf16[2,128,8,512]{3,2,1,0:T(8,128)(2,1)}, bf16[2,128,8,512]{3,2,1,0:T(8,128)(2,1)}, u32[]{:S(2)}, u32[]{:S(2)}) %collective-permute-start.45) | collective-permute-done | bytes 2097184 | tf_op jit(solution)/shard_map/ppermute | solution.py:35
  881.6 5.8 all-to-all-start.7
  887.4 6.2 convolution_convert_fusion.8.do_ref
  893.6 12.7 attend_back.1
  908.2 9.0 convolution_convert_fusion
  917.2 6.7 constant_dynamic-slice_fusion.1
  926.5 10.2 convolution_convert_fusion.6
  945.6 41.0 %collective-permute-done.41 = bf16[2,32,8,512]{3,2,1,0:T(8,128)(2,1)S(1)} collective-permute-done((bf16[2,32,8,512]{3,2,1,0:T(8,128)(2,1)S(1)}, bf16[2,32,8,512]{3,2,1,0:T(8,128)(2,1)S(1)}, u32[]{:S(2)}, u32[]{:S(2)}) %collective-permute-start.41) | collective-permute-done | bytes 524320 | tf_op jit(solution)/shard_map/ppermute | solution.py:35
  1008.3 8.8 all-to-all-done.8
  1017.1 5.1 all-to-all-start.6
  1039.8 5.1 all-to-all-start.5
  1051.7 9.2 collective-permute-done.36
  1073.2 7.0 collective-permute-done.35
  1103.4 6.3 all-to-all-start.9
  1109.9 5.0 fusion.117
  1115.0 14.2 %fusion.118 = f32[12,256,512]{2,1,0:T(8,128)} fusion(f32[12,256,512]{2,1,0:T(8,128)S(1)} %fusion.117, f32[12,512,512]{2,1,0:T(8,128)} %param.20), kind=kOutput, calls=%fused_computation.333 | convolution fusion | flops 4831838208 | bytes 25165824 | tf_op jit(solution)/shard_map/dot_general | solution.py:234
  1132.9 28.3 %collective-permute-done.52 = f32[16]{0:T(128)S(1)} collective-permute-done((f32[16]{0:T(128)S(1)}, f32[16]{0:T(128)S(1)}, u32[]{:S(2)}, u32[]{:S(2)}) %collective-permute-start.52) | collective-permute-done | bytes 96 | tf_op jit(solution)/shard_map/ppermute | solution.py:35
  1166.7 13.7 %collective-permute-done.53 = f32[16]{0:T(128)S(1)} collective-permute-done((f32[16]{0:T(128)S(1)}, f32[16]{0:T(128)S(1)}, u32[]{:S(2)}, u32[]{:S(2)}) %collective-permute-start.53) | collective-permute-done | bytes 96 | tf_op jit(solution)/shard_map/ppermute | solution.py:35
  1184.9 9.5 collective-permute-start.26
  1198.7 9.5 collective-permute-start.38
  1221.6 6.4 fusion.28
  1233.6 21.4 %collective-permute-start.48 = (f32[]{:T(128)}, f32[]{:T(128)}, u32[]{:S(2)}, u32[]{:S(2)}) collective-permute-start(f32[]{:T(128)} %add.515), channel_id=1, source_target_pairs={{0,2},{2,0},{1,3},{3,1},{4,6},{6,4},{5,7},{7,5},{8,10},{10,8},{9,1... | collective-permute-start | bytes 20 | tf_op jit(solution)/shard_map/ppermute | solution.py:35
  1266.4 10.5 multiply_add_fusion
  1277.0 17.5 %add_multiply_fusion.1 = (f32[12,256,512]{2,1,0:T(8,128)}, f32[12,256,512]{2,1,0:T(8,128)}) fusion(f32[12,256,512]{2,1,0:T(8,128)} %param.18, f32[]{:T(128)S(6)} %min.3, f32[12,512,256]{1,2,0:T(8,128)} %fusion.28, f32[12,512,512]{2,1,0:T(8,128)} %param.20), kind=kOutput, calls=%fused_computation.28 | convolution fusion | flops 4838129664 | bytes 37748740 | tf_op jit(solution)/shard_map/dot_general | solution.py:234
  1294.5 14.2 %fusion.10 = f32[12,512,256]{1,2,0:T(8,128)} fusion(f32[12,256,256]{2,1,0:T(8,128)S(1)} %copy-done, f32[12,256,512]{2,1,0:T(8,128)} %get-tuple-element.143, f32[12,256,512]{2,1,0:T(8,128)} %get-tuple-element.118, f32[12,256,512]{2,1,0:T(8,128)} %fusion.118, f32[]{:T(128)S(6)} %mul.302), kind=kOutput, calls=%fused_computation.24 | convolution fusion | flops 2423783424 | bytes 28311556 | tf_op jit(solution)/shard_map/dot_general | solution.py:230
  1308.7 21.7 %fusion.116 = (bf16[12,256,512]{2,1,0:T(8,128)(2,1)}, f32[12,256,512]{2,1,0:T(8,128)}) fusion(f32[12,512]{1,0:T(8,128)S(1)} %fusion.82, f32[12,256,512]{2,1,0:T(8,128)} %param.16, f32[12,512,256]{1,2,0:T(8,128)} %fusion.10, f32[12,512,512]{2,1,0:T(8,128)} %param.20), kind=kOutput, calls=%fused_computation.331 | convolution fusion | flops 4838129664 | bytes 34627584 | tf_op jit(solution)/shard_map/dot_general | solution.py:234
  (491 shorter events, 345.8 us)
Async XLA Ops:
  7.2 264.2 %all-gather.5.cloned.1.call-start = ((), (), s32[]{:S(2)}) async-start(), calls=%async_computation.11 | async-start | bytes 9437184 | tf_op jit(solution)/shard_map/all_gather | solution.py:73
  12.4 4.6 collective-permute-start.4
  18.4 10.1 collective-permute-start.6
  19.0 25.2 %collective-permute-start = (bf16[256,2048]{1,0:T(8,128)(2,1)}, bf16[256,2048]{1,0:T(8,128)(2,1)}, u32[]{:S(2)}, u32[]{:S(2)}) collective-permute-start(bf16[256,2048]{1,0:T(8,128)(2,1)} %bitcast.365), channel_id=1, source_target_pairs={{0,0},{2,4},{4,2},{6,6},{1,1},{3,5},{5,3},{7,7},{8,8},{10,12},{12,... | collective-permute-start | bytes 3145736 | tf_op jit(solution)/shard_map/ppermute | solution.py:39
  28.6 3.9 collective-permute-start.7
  55.8 81.7 %all-to-all-start = ((bf16[384,8,512]{2,1,0:T(8,128)(2,1)}), bf16[384,8,512]{2,1,0:T(8,128)(2,1)}, u32[]{:S(2)}, u32[]{:S(2)}) async-start(bf16[384,8,512]{2,1,0:T(8,128)(2,1)} %bitcast.322), calls=%async_computation | async-start | bytes 6291456 | tf_op jit(solution)/shard_map/all_to_all | solution.py:299
  65.3 534.4 %all-gather.7.cloned.1.call-start = ((), (), s32[]{:S(2)}) async-start(), calls=%async_computation.12 | async-start | bytes 9437184 | tf_op jit(solution)/shard_map/all_gather | solution.py:73
  163.3 44.8 %collective-permute-start.8 = (bf16[192,8,256]{2,1,0:T(8,128)(2,1)S(1)}, bf16[192,8,256]{2,1,0:T(8,128)(2,1)S(1)}, u32[]{:S(2)}, u32[]{:S(2)}) collective-permute-start(bf16[192,8,256]{2,1,0:T(8,128)(2,1)S(1)} %all_to_all.59), channel_id=1, source_target_pairs={{0,2},{2,0},{1,3},{3,1},{4,6},{6,4},{5,7},{7,5},{8,10},{10,8},{9,1... | collective-permute-start | bytes 2359304 | tf_op jit(solution)/shard_map/ppermute | solution.py:35
  187.6 26.1 %collective-permute-start.10 = (bf16[32,8,512]{2,1,0:T(8,128)(2,1)S(1)}, bf16[32,8,512]{2,1,0:T(8,128)(2,1)}, u32[]{:S(2)}, u32[]{:S(2)}) collective-permute-start(bf16[32,8,512]{2,1,0:T(8,128)(2,1)S(1)} %all_to_all.60), channel_id=1, source_target_pairs={{0,2},{2,0},{1,3},{3,1},{4,6},{6,4},{5,7},{7,5},{8,10},{10,8},{9,1... | collective-permute-start | bytes 786440 | tf_op jit(solution)/shard_map/ppermute | solution.py:35
  210.4 51.4 %collective-permute-start.9 = (bf16[2,192,8,256]{3,2,1,0:T(8,128)(2,1)}, bf16[2,192,8,256]{3,2,1,0:T(8,128)(2,1)}, u32[]{:S(2)}, u32[]{:S(2)}) collective-permute-start(bf16[2,192,8,256]{3,2,1,0:T(8,128)(2,1)} %pad_maximum_fusion.7), channel_id=1, source_target_pairs={{0,16},{16,0},{1,17},{17,1},{2,18},{18,2},{3,19},{19,3},{4,20},{20... | collective-permute-start | bytes 4718600 | tf_op jit(solution)/shard_map/ppermute | solution.py:35
  212.1 5.6 collective-permute-start.2
  216.3 41.7 %collective-permute-start.11 = (bf16[2,32,8,512]{3,2,1,0:T(8,128)(2,1)}, bf16[2,32,8,512]{3,2,1,0:T(8,128)(2,1)}, u32[]{:S(2)}, u32[]{:S(2)}) collective-permute-start(bf16[2,32,8,512]{3,2,1,0:T(8,128)(2,1)} %pad_maximum_fusion.9), channel_id=1, source_target_pairs={{0,16},{16,0},{1,17},{17,1},{2,18},{18,2},{3,19},{19,3},{4,20},{20... | collective-permute-start | bytes 1572872 | tf_op jit(solution)/shard_map/ppermute | solution.py:35
  302.6 7.5 collective-permute-start.12
  319.6 25.5 %collective-permute-start.13 = (bf16[2,256,1024]{2,1,0:T(8,128)(2,1)}, bf16[2,256,1024]{2,1,0:T(8,128)(2,1)}, u32[]{:S(2)}, u32[]{:S(2)}) collective-permute-start(bf16[2,256,1024]{2,1,0:T(8,128)(2,1)} %dynamic-slice_bitcast_fusion.12), channel_id=1, source_target_pairs={{0,8},{8,0},{1,9},{9,1},{2,10},{10,2},{3,11},{11,3},{4,12},{12,4},... | collective-permute-start | bytes 3145736 | tf_op jit(solution)/shard_map/ppermute | solution.py:35
  323.0 25.2 %collective-permute-start.15 = (bf16[2,256,1024]{2,1,0:T(8,128)(2,1)}, bf16[2,256,1024]{2,1,0:T(8,128)(2,1)}, u32[]{:S(2)}, u32[]{:S(2)}) collective-permute-start(bf16[2,256,1024]{2,1,0:T(8,128)(2,1)} %dynamic-slice_bitcast_fusion.11), channel_id=1, source_target_pairs={{0,1},{1,0},{2,3},{3,2},{4,5},{5,4},{6,7},{7,6},{8,9},{9,8},{10,11... | collective-permute-start | bytes 3145736 | tf_op jit(solution)/shard_map/ppermute | solution.py:35
  347.1 13.2 collective-permute-start.14
  350.0 12.9 collective-permute-start.16
  367.4 267.4 %all-gather.9.cloned.1.call-start = ((), (), s32[]{:S(2)}) async-start(), calls=%async_computation.13 | async-start | bytes 9437184 | tf_op jit(solution)/shard_map/all_gather | solution.py:73
  367.5 9.5 collective-permute-start.27
  381.3 40.5 %all-to-all-start.3 = ((bf16[128,8,512]{2,1,0:T(8,128)(2,1)}), bf16[128,8,512]{2,1,0:T(8,128)(2,1)}, u32[]{:S(2)}, u32[]{:S(2)}) async-start(bf16[128,8,512]{2,1,0:T(8,128)(2,1)} %copy.217), calls=%async_computation.3 | async-start | bytes 2097152 | tf_op jit(solution)/shard_map/all_to_all | solution.py:248
  421.8 39.3 %all-to-all-start.4 = ((bf16[128,8,512]{2,1,0:T(8,128)(2,1)}), bf16[128,8,512]{2,1,0:T(8,128)(2,1)}, u32[]{:S(2)}, u32[]{:S(2)}) async-start(bf16[128,8,512]{2,1,0:T(8,128)(2,1)} %copy.220), calls=%async_computation.4 | async-start | bytes 2097152 | tf_op jit(solution)/shard_map/all_to_all | solution.py:248
  427.5 459.9 %all-gather.11.cloned.1.call-start = ((), (), s32[]{:S(2)}) async-start(), calls=%async_computation.14 | async-start | bytes 9437184 | tf_op jit(solution)/shard_map/all_gather | solution.py:73
  427.7 68.1 %collective-permute-start.17 = (bf16[128,8,512]{2,1,0:T(8,128)(2,1)}, bf16[128,8,512]{2,1,0:T(8,128)(2,1)}, u32[]{:S(2)}, u32[]{:S(2)}) collective-permute-start(bf16[128,8,512]{2,1,0:T(8,128)(2,1)} %all-to-all-done.3), channel_id=1, source_target_pairs={{0,2},{2,0},{1,3},{3,1},{4,6},{6,4},{5,7},{7,5},{8,10},{10,8},{9,1... | collective-permute-start | bytes 3145736 | tf_op jit(solution)/shard_map/ppermute | solution.py:35
  461.1 61.4 %collective-permute-start.19 = (bf16[128,8,512]{2,1,0:T(8,128)(2,1)}, bf16[128,8,512]{2,1,0:T(8,128)(2,1)S(1)}, u32[]{:S(2)}, u32[]{:S(2)}) collective-permute-start(bf16[128,8,512]{2,1,0:T(8,128)(2,1)} %all-to-all-done.4), channel_id=1, source_target_pairs={{0,2},{2,0},{1,3},{3,1},{4,6},{6,4},{5,7},{7,5},{8,10},{10,8},{9,1... | collective-permute-start | bytes 3145736 | tf_op jit(solution)/shard_map/ppermute | solution.py:35
  499.1 48.9 %collective-permute-start.18 = (bf16[2,128,8,512]{3,2,1,0:T(8,128)(2,1)}, bf16[2,128,8,512]{3,2,1,0:T(8,128)(2,1)}, u32[]{:S(2)}, u32[]{:S(2)}) collective-permute-start(bf16[2,128,8,512]{3,2,1,0:T(8,128)(2,1)} %pad_maximum_fusion.3), channel_id=1, source_target_pairs={{0,16},{16,0},{1,17},{17,1},{2,18},{18,2},{3,19},{19,3},{4,20},{20... | collective-permute-start | bytes 6291464 | tf_op jit(solution)/shard_map/ppermute | solution.py:35
  526.3 62.9 %collective-permute-start.20 = (bf16[2,128,8,512]{3,2,1,0:T(8,128)(2,1)}, bf16[2,128,8,512]{3,2,1,0:T(8,128)(2,1)}, u32[]{:S(2)}, u32[]{:S(2)}) collective-permute-start(bf16[2,128,8,512]{3,2,1,0:T(8,128)(2,1)} %pad_maximum_fusion.4), channel_id=1, source_target_pairs={{0,16},{16,0},{1,17},{17,1},{2,18},{18,2},{3,19},{19,3},{4,20},{20... | collective-permute-start | bytes 6291464 | tf_op jit(solution)/shard_map/ppermute | solution.py:35
  634.8 35.5 %collective-permute-start.21 = (bf16[2,2,256,2048]{3,2,0,1:T(8,128)(2,1)}, bf16[2,2,256,2048]{3,2,0,1:T(8,128)(2,1)}, u32[]{:S(2)}, u32[]{:S(2)}) collective-permute-start(bf16[2,2,256,2048]{3,2,0,1:T(8,128)(2,1)} %bitcast.308), channel_id=1, source_target_pairs={{0,4},{4,0},{1,5},{5,1},{2,6},{6,2},{3,7},{7,3},{8,12},{12,8},{9,1... | collective-permute-start | bytes 12582920 | tf_op jit(solution)/shard_map/ppermute | solution.py:35
  669.9 13.2 collective-permute-start.28
  675.9 31.2 %collective-permute-start.22 = (bf16[2,256,1024]{2,1,0:T(8,128)(2,1)S(1)}, bf16[2,256,1024]{2,1,0:T(8,128)(2,1)}, u32[]{:S(2)}, u32[]{:S(2)}) collective-permute-start(bf16[2,256,1024]{2,1,0:T(8,128)(2,1)S(1)} %dynamic-slice_bitcast_fusion.10), channel_id=1, source_target_pairs={{0,8},{8,0},{1,9},{9,1},{2,10},{10,2},{3,11},{11,3},{4,12},{12,4},... | collective-permute-start | bytes 3145736 | tf_op jit(solution)/shard_map/ppermute | solution.py:35
  686.0 43.3 %collective-permute-start.29 = (bf16[2,256,1024]{2,1,0:T(8,128)(2,1)S(1)}, bf16[2,256,1024]{2,1,0:T(8,128)(2,1)S(1)}, u32[]{:S(2)}, u32[]{:S(2)}) collective-permute-start(bf16[2,256,1024]{2,1,0:T(8,128)(2,1)S(1)} %dynamic-slice_bitcast_fusion.8), channel_id=1, source_target_pairs={{0,8},{8,0},{1,9},{9,1},{2,10},{10,2},{3,11},{11,3},{4,12},{12,4},... | collective-permute-start | bytes 3145736 | tf_op jit(solution)/shard_map/ppermute | solution.py:35
  687.6 42.7 %collective-permute-start.31 = (bf16[2,256,1024]{2,1,0:T(8,128)(2,1)S(1)}, bf16[2,256,1024]{2,1,0:T(8,128)(2,1)S(1)}, u32[]{:S(2)}, u32[]{:S(2)}) collective-permute-start(bf16[2,256,1024]{2,1,0:T(8,128)(2,1)S(1)} %dynamic-slice_bitcast_fusion.7), channel_id=1, source_target_pairs={{0,1},{1,0},{2,3},{3,2},{4,5},{5,4},{6,7},{7,6},{8,9},{9,8},{10,11... | collective-permute-start | bytes 3145736 | tf_op jit(solution)/shard_map/ppermute | solution.py:35
  687.7 48.4 %collective-permute-start.24 = (bf16[2,256,1024]{2,1,0:T(8,128)(2,1)S(1)}, bf16[2,256,1024]{2,1,0:T(8,128)(2,1)S(1)}, u32[]{:S(2)}, u32[]{:S(2)}) collective-permute-start(bf16[2,256,1024]{2,1,0:T(8,128)(2,1)S(1)} %dynamic-slice_bitcast_fusion.9), channel_id=1, source_target_pairs={{0,1},{1,0},{2,3},{3,2},{4,5},{5,4},{6,7},{7,6},{8,9},{9,8},{10,11... | collective-permute-start | bytes 3145736 | tf_op jit(solution)/shard_map/ppermute | solution.py:35
  708.8 50.3 %collective-permute-start.23 = (bf16[256,1024]{1,0:T(8,128)(2,1)S(1)}, bf16[256,1024]{1,0:T(8,128)(2,1)S(1)}, u32[]{:S(2)}, u32[]{:S(2)}) collective-permute-start(bf16[256,1024]{1,0:T(8,128)(2,1)S(1)} %dynamic-slice_bitcast_fusion.20), channel_id=1, source_target_pairs={{0,1},{1,0},{2,3},{3,2},{4,5},{5,4},{6,7},{7,6},{8,9},{9,8},{10,11... | collective-permute-start | bytes 1572872 | tf_op jit(solution)/shard_map/ppermute | solution.py:35
  729.8 27.9 %collective-permute-start.30 = (bf16[256,1024]{1,0:T(8,128)(2,1)S(1)}, bf16[256,1024]{1,0:T(8,128)(2,1)S(1)}, u32[]{:S(2)}, u32[]{:S(2)}) collective-permute-start(bf16[256,1024]{1,0:T(8,128)(2,1)S(1)} %dynamic-slice_bitcast_fusion.18), channel_id=1, source_target_pairs={{0,1},{1,0},{2,3},{3,2},{4,5},{5,4},{6,7},{7,6},{8,9},{9,8},{10,11... | collective-permute-start | bytes 1572872 | tf_op jit(solution)/shard_map/ppermute | solution.py:35
  730.7 27.2 %collective-permute-start.32 = (bf16[256,1024]{1,0:T(8,128)(2,1)S(1)}, bf16[256,1024]{1,0:T(8,128)(2,1)S(1)}, u32[]{:S(2)}, u32[]{:S(2)}) collective-permute-start(bf16[256,1024]{1,0:T(8,128)(2,1)S(1)} %dynamic-slice_bitcast_fusion.17), channel_id=1, source_target_pairs={{0,8},{8,0},{1,9},{9,1},{2,10},{10,2},{3,11},{11,3},{4,12},{12,4},... | collective-permute-start | bytes 1572872 | tf_op jit(solution)/shard_map/ppermute | solution.py:35
  736.6 22.7 %collective-permute-start.25 = (bf16[256,1024]{1,0:T(8,128)(2,1)S(1)}, bf16[256,1024]{1,0:T(8,128)(2,1)S(1)}, u32[]{:S(2)}, u32[]{:S(2)}) collective-permute-start(bf16[256,1024]{1,0:T(8,128)(2,1)S(1)} %dynamic-slice_bitcast_fusion.19), channel_id=1, source_target_pairs={{0,8},{8,0},{1,9},{9,1},{2,10},{10,2},{3,11},{11,3},{4,12},{12,4},... | collective-permute-start | bytes 1572872 | tf_op jit(solution)/shard_map/ppermute | solution.py:35
  779.7 48.9 %collective-permute-start.43 = (bf16[2,128,8,512]{3,2,1,0:T(8,128)(2,1)}, bf16[2,128,8,512]{3,2,1,0:T(8,128)(2,1)}, u32[]{:S(2)}, u32[]{:S(2)}) collective-permute-start(bf16[2,128,8,512]{3,2,1,0:T(8,128)(2,1)} %dynamic-slice_bitcast_fusion.1), channel_id=1, source_target_pairs={{0,16},{16,0},{1,17},{17,1},{2,18},{18,2},{3,19},{19,3},{4,20},{20... | collective-permute-start | bytes 6291464 | tf_op jit(solution)/shard_map/ppermute | solution.py:35
  798.5 73.2 %collective-permute-start.45 = (bf16[2,128,8,512]{3,2,1,0:T(8,128)(2,1)}, bf16[2,128,8,512]{3,2,1,0:T(8,128)(2,1)}, u32[]{:S(2)}, u32[]{:S(2)}) collective-permute-start(bf16[2,128,8,512]{3,2,1,0:T(8,128)(2,1)} %dynamic-slice_bitcast_fusion), channel_id=1, source_target_pairs={{0,16},{16,0},{1,17},{17,1},{2,18},{18,2},{3,19},{19,3},{4,20},{20... | collective-permute-start | bytes 6291464 | tf_op jit(solution)/shard_map/ppermute | solution.py:35
  833.8 45.3 %collective-permute-start.44 = (bf16[128,8,512]{2,1,0:T(8,128)(2,1)}, bf16[128,8,512]{2,1,0:T(8,128)(2,1)}, u32[]{:S(2)}, u32[]{:S(2)}) collective-permute-start(bf16[128,8,512]{2,1,0:T(8,128)(2,1)} %dynamic-slice_bitcast_fusion.4), channel_id=1, source_target_pairs={{0,2},{2,0},{1,3},{3,1},{4,6},{6,4},{5,7},{7,5},{8,10},{10,8},{9,1... | collective-permute-start | bytes 3145736 | tf_op jit(solution)/shard_map/ppermute | solution.py:35
  876.9 66.2 %collective-permute-start.46 = (bf16[128,8,512]{2,1,0:T(8,128)(2,1)}, bf16[128,8,512]{2,1,0:T(8,128)(2,1)}, u32[]{:S(2)}, u32[]{:S(2)}) collective-permute-start(bf16[128,8,512]{2,1,0:T(8,128)(2,1)} %dynamic-slice_bitcast_fusion.3), channel_id=1, source_target_pairs={{0,2},{2,0},{1,3},{3,1},{4,6},{6,4},{5,7},{7,5},{8,10},{10,8},{9,1... | collective-permute-start | bytes 3145736 | tf_op jit(solution)/shard_map/ppermute | solution.py:35
  881.6 106.8 %all-to-all-start.7 = ((bf16[128,8,512]{2,1,0:T(8,128)(2,1)}), bf16[128,8,512]{2,1,0:T(8,128)(2,1)}, u32[]{:S(2)}, u32[]{:S(2)}) async-start(bf16[128,8,512]{2,1,0:T(8,128)(2,1)} %fusion.55), calls=%async_computation.7 | async-start | bytes 2097152 | tf_op jit(solution)/shard_map/all_to_all | solution.py:272
  926.4 71.9 %collective-permute-start.33 = (bf16[2,2,256,2048]{3,2,0,1:T(8,128)(2,1)}, bf16[2,2,256,2048]{3,2,0,1:T(8,128)(2,1)}, u32[]{:S(2)}, u32[]{:S(2)}) collective-permute-start(bf16[2,2,256,2048]{3,2,0,1:T(8,128)(2,1)} %bitcast.306), channel_id=1, source_target_pairs={{0,4},{4,0},{1,5},{5,1},{2,6},{6,2},{3,7},{7,3},{8,12},{12,8},{9,1... | collective-permute-start | bytes 12582920 | tf_op jit(solution)/shard_map/ppermute | solution.py:35
  938.4 54.2 %collective-permute-start.39 = (bf16[2,192,8,256]{3,2,1,0:T(8,128)(2,1)}, bf16[2,192,8,256]{3,2,1,0:T(8,128)(2,1)}, u32[]{:S(2)}, u32[]{:S(2)}) collective-permute-start(bf16[2,192,8,256]{3,2,1,0:T(8,128)(2,1)} %dynamic-slice_bitcast_fusion.2), channel_id=1, source_target_pairs={{0,16},{16,0},{1,17},{17,1},{2,18},{18,2},{3,19},{19,3},{4,20},{20... | collective-permute-start | bytes 4718600 | tf_op jit(solution)/shard_map/ppermute | solution.py:35
  941.7 44.9 %collective-permute-start.41 = (bf16[2,32,8,512]{3,2,1,0:T(8,128)(2,1)S(1)}, bf16[2,32,8,512]{3,2,1,0:T(8,128)(2,1)S(1)}, u32[]{:S(2)}, u32[]{:S(2)}) collective-permute-start(bf16[2,32,8,512]{3,2,1,0:T(8,128)(2,1)S(1)} %dynamic-slice_bitcast_fusion.14), channel_id=1, source_target_pairs={{0,16},{16,0},{1,17},{17,1},{2,18},{18,2},{3,19},{19,3},{4,20},{20... | collective-permute-start | bytes 1572872 | tf_op jit(solution)/shard_map/ppermute | solution.py:35
  987.6 19.0 %collective-permute-start.42 = (bf16[32,8,512]{2,1,0:T(8,128)(2,1)S(1)}, bf16[32,8,512]{2,1,0:T(8,128)(2,1)}, u32[]{:S(2)}, u32[]{:S(2)}) collective-permute-start(bf16[32,8,512]{2,1,0:T(8,128)(2,1)S(1)} %dynamic-slice_bitcast_fusion.23), channel_id=1, source_target_pairs={{0,2},{2,0},{1,3},{3,1},{4,6},{6,4},{5,7},{7,5},{8,10},{10,8},{9,1... | collective-permute-start | bytes 786440 | tf_op jit(solution)/shard_map/ppermute | solution.py:35
  988.4 28.7 %all-to-all-start.8 = ((bf16[128,8,512]{2,1,0:T(8,128)(2,1)}), bf16[128,8,512]{2,1,0:T(8,128)(2,1)}, u32[]{:S(2)}, u32[]{:S(2)}) async-start(bf16[128,8,512]{2,1,0:T(8,128)(2,1)} %fusion.54), calls=%async_computation.8 | async-start | bytes 2097152 | tf_op jit(solution)/shard_map/all_to_all | solution.py:272
  996.0 40.0 %collective-permute-start.40 = (bf16[192,8,256]{2,1,0:T(8,128)(2,1)}, bf16[192,8,256]{2,1,0:T(8,128)(2,1)}, u32[]{:S(2)}, u32[]{:S(2)}) collective-permute-start(bf16[192,8,256]{2,1,0:T(8,128)(2,1)} %dynamic-slice_bitcast_fusion.13), channel_id=1, source_target_pairs={{0,2},{2,0},{1,3},{3,1},{4,6},{6,4},{5,7},{7,5},{8,10},{10,8},{9,1... | collective-permute-start | bytes 2359304 | tf_op jit(solution)/shard_map/ppermute | solution.py:35
  1006.6 40.9 %collective-permute-start.34 = (bf16[2,256,1024]{2,1,0:T(8,128)(2,1)}, bf16[2,256,1024]{2,1,0:T(8,128)(2,1)}, u32[]{:S(2)}, u32[]{:S(2)}) collective-permute-start(bf16[2,256,1024]{2,1,0:T(8,128)(2,1)} %dynamic-slice_bitcast_fusion.6), channel_id=1, source_target_pairs={{0,8},{8,0},{1,9},{9,1},{2,10},{10,2},{3,11},{11,3},{4,12},{12,4},... | collective-permute-start | bytes 3145736 | tf_op jit(solution)/shard_map/ppermute | solution.py:35
  1017.1 22.7 %all-to-all-start.6 = ((bf16[32,8,512]{2,1,0:T(8,128)(2,1)}), bf16[32,8,512]{2,1,0:T(8,128)(2,1)S(1)}, u32[]{:S(2)}, u32[]{:S(2)}) async-start(bf16[32,8,512]{2,1,0:T(8,128)(2,1)} %fusion.72), calls=%async_computation.6 | async-start | bytes 524288 | tf_op jit(solution)/shard_map/all_to_all | solution.py:272
  1024.5 36.5 %collective-permute-start.36 = (bf16[2,256,1024]{2,1,0:T(8,128)(2,1)}, bf16[2,256,1024]{2,1,0:T(8,128)(2,1)}, u32[]{:S(2)}, u32[]{:S(2)}) collective-permute-start(bf16[2,256,1024]{2,1,0:T(8,128)(2,1)} %dynamic-slice_bitcast_fusion.5), channel_id=1, source_target_pairs={{0,1},{1,0},{2,3},{3,2},{4,5},{5,4},{6,7},{7,6},{8,9},{9,8},{10,11... | collective-permute-start | bytes 3145736 | tf_op jit(solution)/shard_map/ppermute | solution.py:35
  1039.8 27.4 %all-to-all-start.5 = ((bf16[192,8,256]{2,1,0:T(8,128)(2,1)}), bf16[192,8,256]{2,1,0:T(8,128)(2,1)}, u32[]{:S(2)}, u32[]{:S(2)}) async-start(bf16[192,8,256]{2,1,0:T(8,128)(2,1)} %fusion.64), calls=%async_computation.5 | async-start | bytes 1572864 | tf_op jit(solution)/shard_map/all_to_all | solution.py:272
  1050.3 29.9 %collective-permute-start.35 = (bf16[256,1024]{1,0:T(8,128)(2,1)}, bf16[256,1024]{1,0:T(8,128)(2,1)}, u32[]{:S(2)}, u32[]{:S(2)}) collective-permute-start(bf16[256,1024]{1,0:T(8,128)(2,1)} %dynamic-slice_bitcast_fusion.16), channel_id=1, source_target_pairs={{0,1},{1,0},{2,3},{3,2},{4,5},{5,4},{6,7},{7,6},{8,9},{9,8},{10,11... | collective-permute-start | bytes 1572872 | tf_op jit(solution)/shard_map/ppermute | solution.py:35
  1063.7 17.8 %collective-permute-start.37 = (bf16[256,1024]{1,0:T(8,128)(2,1)}, bf16[256,1024]{1,0:T(8,128)(2,1)}, u32[]{:S(2)}, u32[]{:S(2)}) collective-permute-start(bf16[256,1024]{1,0:T(8,128)(2,1)} %dynamic-slice_bitcast_fusion.15), channel_id=1, source_target_pairs={{0,8},{8,0},{1,9},{9,1},{2,10},{10,2},{3,11},{11,3},{4,12},{12,4},... | collective-permute-start | bytes 1572872 | tf_op jit(solution)/shard_map/ppermute | solution.py:35
  1091.8 11.5 all-to-all-start.10
  1103.4 114.1 %all-to-all-start.9 = ((bf16[384,8,512]{2,1,0:T(8,128)(2,1)}), bf16[384,8,512]{2,1,0:T(8,128)(2,1)}, u32[]{:S(2)}, u32[]{:S(2)}) async-start(bf16[384,8,512]{2,1,0:T(8,128)(2,1)} %copy.239), calls=%async_computation.9 | async-start | bytes 6291456 | tf_op jit(solution)/shard_map/all_to_all | solution.py:367
  1131.3 29.9 %collective-permute-start.52 = (f32[16]{0:T(128)S(1)}, f32[16]{0:T(128)S(1)}, u32[]{:S(2)}, u32[]{:S(2)}) collective-permute-start(f32[16]{0:T(128)S(1)} %compare_select_fusion.1), channel_id=1, source_target_pairs={{0,1},{1,0},{2,3},{3,2},{4,5},{5,4},{6,7},{7,6},{8,9},{9,8},{10,11... | collective-permute-start | bytes 200 | tf_op jit(solution)/shard_map/ppermute | solution.py:35
  1162.5 17.9 %collective-permute-start.53 = (f32[16]{0:T(128)S(1)}, f32[16]{0:T(128)S(1)}, u32[]{:S(2)}, u32[]{:S(2)}) collective-permute-start(f32[16]{0:T(128)S(1)} %fusion.153), channel_id=1, source_target_pairs={{0,2},{2,0},{1,3},{3,1},{4,6},{6,4},{5,7},{7,5},{8,10},{10,8},{9,1... | collective-permute-start | bytes 200 | tf_op jit(solution)/shard_map/ppermute | solution.py:35
  1182.9 25.3 %collective-permute-start.55 = (f32[16]{0:T(128)S(1)}, f32[16]{0:T(128)S(1)}, u32[]{:S(2)}, u32[]{:S(2)}) collective-permute-start(f32[16]{0:T(128)S(1)} %max.21), channel_id=1, source_target_pairs={{0,8},{8,0},{1,9},{9,1},{2,10},{10,2},{3,11},{11,3},{4,12},{12,4},... | collective-permute-start | bytes 200 | tf_op jit(solution)/shard_map/ppermute | solution.py:35
  1184.9 29.0 %collective-permute-start.26 = (bf16[256,2048]{1,0:T(8,128)(2,1)}, bf16[256,2048]{1,0:T(8,128)(2,1)}, u32[]{:S(2)}, u32[]{:S(2)}) collective-permute-start(bf16[256,2048]{1,0:T(8,128)(2,1)} %get-tuple-element.79), channel_id=1, source_target_pairs={{0,0},{2,4},{4,2},{6,6},{1,1},{3,5},{5,3},{7,7},{8,8},{10,12},{12,... | collective-permute-start | bytes 3145736 | tf_op jit(solution)/shard_map/ppermute | solution.py:39
  1198.7 15.9 %collective-permute-start.38 = (bf16[256,2048]{1,0:T(8,128)(2,1)}, bf16[256,2048]{1,0:T(8,128)(2,1)}, u32[]{:S(2)}, u32[]{:S(2)}) collective-permute-start(bf16[256,2048]{1,0:T(8,128)(2,1)} %fusion.48), channel_id=1, source_target_pairs={{0,0},{2,4},{4,2},{6,6},{1,1},{3,5},{5,3},{7,7},{8,8},{10,12},{12,... | collective-permute-start | bytes 3145736 | tf_op jit(solution)/shard_map/ppermute | solution.py:39
  1229.3 3.8 collective-permute-start.47
  1233.6 21.7 %collective-permute-start.48 = (f32[]{:T(128)}, f32[]{:T(128)}, u32[]{:S(2)}, u32[]{:S(2)}) collective-permute-start(f32[]{:T(128)} %add.515), channel_id=1, source_target_pairs={{0,2},{2,0},{1,3},{3,1},{4,6},{6,4},{5,7},{7,5},{8,10},{10,8},{9,1... | collective-permute-start | bytes 20 | tf_op jit(solution)/shard_map/ppermute | solution.py:35
  1257.8 3.7 collective-permute-start.50
  1262.1 3.7 collective-permute-start.51
  (89 other events, 2301.4 us)
Sparse Core Ops, SparseCore 0:
  50.7 99.1 all-gather.4
  367.5 84.8 all-gather.6
  454.0 90.1 all-gather.8
  764.8 47.9 all-gather.10

commit v2 on v1

v2 whole, which is shorter than its diff:
```python
import functools
import math

import jax
import jax.numpy as jnp
from jax import lax
from jax.experimental import pallas as pl
from jax.experimental.pallas import tpu as pltpu
from jax.sharding import Mesh
from jax.sharding import PartitionSpec as P

D = 2048
HEADS = 16
DH = 128
FF = 8192
BR = 256
BC = 512
TP = 8
LEN = 1024
CH = 256

F32 = jnp.float32
BF16 = jnp.bfloat16
NEG = -1e30
SCALE = DH ** (-0.5)

EVERY = ("p", "q", "i", "c", "h", "l")
GROUP = ("q", "i", "c")
DATA = ("p", "h", "l")


def at(array, index, axis=0):
    return lax.dynamic_index_in_dim(array, index, axis, keepdims=False)


def trade(array, axis):
    return lax.ppermute(array, axis, [(0, 1), (1, 0)])


def after(value, *others):
    return lax.optimization_barrier((value, others))[0]


def together(*values):
    return lax.optimization_barrier(values)


def nothing_of(array):
    return array[(0,) * array.ndim].astype(F32) * 0.0


def swap_tokens(array):
    bits = [(i, c, h, l) for i in range(2) for c in range(2) for h in range(2) for l in range(2)]
    pairs = [(8 * i + 4 * c + 2 * h + l, 8 * l + 4 * h + 2 * c + i) for i, c, h, l in bits]
    other = lax.ppermute(array, ("i", "c", "h", "l"), [pair for pair in pairs if pair[0] != pair[1]])
    i, c, h, l = (lax.axis_index(name) for name in ("i", "c", "h", "l"))
    return jnp.where((i == l) & (c == h), array, other)


def pair_up(array, axis):
    other = trade(array, axis)
    mine = lax.axis_index(axis) == 0
    return jnp.stack([jnp.where(mine, array, other), jnp.where(mine, other, array)])


def group_gather(array):
    return lax.all_gather(array, GROUP, axis=0, tiled=True)


def to_relative(array):
    q, i, c = (lax.axis_index(name) for name in GROUP)
    rows = [at(at(at(array, q ^ m, 0), c ^ n, 0), i ^ k, 0) for n in range(2) for m in range(2) for k in range(2)]
    return jnp.stack(rows).reshape(2, 2, 2, *array.shape[3:])


def to_member(array):
    q, i, c = (lax.axis_index(name) for name in GROUP)
    rows = [at(at(at(array, c ^ n, 0), q ^ m, 0), i ^ k, 0) for m in range(2) for n in range(2) for k in range(2)]
    return jnp.stack(rows).reshape(2, 2, 2, *array.shape[3:])


def gather_relative(own, *fillers):
    first, second = own[:, : D // 2], own[:, D // 2 :]
    first = jnp.stack([first, trade(first, "i")])
    second = jnp.stack([second, trade(second, "q")])
    first_other, second_other = trade(first, "q"), trade(second, "i")
    zero = sum((nothing_of(filler) for filler in fillers), jnp.float32(0)).astype(BF16)
    first = jnp.stack([first, first_other + zero])
    second = jnp.stack([second, second_other + zero]).transpose(1, 0, 2, 3)
    mine = jnp.concatenate([first, second], axis=-1).reshape(4 * CH, D)
    return mine, trade(mine, "c")


def scatter_relative(pair, *fillers):
    total = (pair[0] + pair[1].astype(F32)).astype(BF16).reshape(2, 2, CH, D)
    first, second = total[..., : D // 2], total[..., D // 2 :]
    first_other = trade(first[1], "q")
    second_other = trade(second[:, 1], "i")
    zero = sum((nothing_of(filler) for filler in fillers), jnp.float32(0))
    first = (first[0].astype(F32) + (first_other.astype(F32) + zero)).astype(BF16)
    second = (second[:, 0].astype(F32) + (second_other.astype(F32) + zero)).astype(BF16)
    first_other = trade(first[1], "i")
    second_other = trade(second[1], "q")
    return jnp.concatenate(
        [first[0].astype(F32) + first_other.astype(F32), second[0].astype(F32) + second_other.astype(F32)], axis=1
    )


def scatter_core(left, right, right_dim):
    c = lax.axis_index("c")
    left = left.reshape(2, 2, 2 * CH, -1)
    send = contract(at(left, 1 - c, 1).reshape(4 * CH, -1), right, 1, right_dim).astype(BF16)
    keep = contract(at(left, c, 1).reshape(4 * CH, -1), right, 1, right_dim)
    return keep, trade(send, "c")


def scatter_chips(pair):
    q, i = lax.axis_index("q"), lax.axis_index("i")
    total = (pair[0] + pair[1].astype(F32)).astype(BF16).reshape(2, 2, CH, D)
    first, second = total[..., : D // 2], total[..., D // 2 :]
    first_other = trade(at(first, 1 - q, 0), "q")
    second_other = trade(at(second, 1 - i, 1), "i")
    first = (at(first, q, 0).astype(F32) + first_other.astype(F32)).astype(BF16)
    second = (at(second, i, 1).astype(F32) + second_other.astype(F32)).astype(BF16)
    first_other = trade(at(first, 1 - i), "i")
    second_other = trade(at(second, 1 - q), "q")
    first = at(first, i).astype(F32) + first_other.astype(F32)
    second = at(second, q).astype(F32) + second_other.astype(F32)
    return jnp.concatenate([first, second], axis=1)


def norm_parts(hidden):
    average = jnp.mean(hidden, axis=-1, keepdims=True)
    centred = hidden - average
    variance = jnp.mean(centred * centred, axis=-1, keepdims=True)
    inverse = lax.rsqrt(variance + 1e-05)
    return centred * inverse, inverse


def norm_back(grad, unit, inverse, gain):
    scaled = grad * gain
    inner = jnp.mean(scaled * unit, axis=-1, keepdims=True)
    back = inverse * (scaled - jnp.mean(scaled, axis=-1, keepdims=True) - unit * inner)
    return back, jnp.sum(grad * unit, axis=0), jnp.sum(grad, axis=0)


def contract(left, right, left_dim, right_dim):
    return lax.dot_general(
        left, right, (((left_dim,), (right_dim,)), ((), ())), preferred_element_type=F32
    )


def allowed_pairs(seg_col, seg_row, j, low, high):
    rows = j * CH + lax.broadcasted_iota(jnp.int32, (CH, high - low), 0)
    cols = low + lax.broadcasted_iota(jnp.int32, (CH, high - low), 1)
    same = seg_col[0, j * CH : (j + 1) * CH, :] == seg_row[0, :, low:high]
    return same & (cols <= rows)


def attend_kernel(seg_col, seg_row, q_ref, k_ref, v_ref, o_ref, lse_ref, top_ref):
    top = jnp.full((1, 1), NEG, F32)
    for j in range(LEN // CH):
        low, high = max(0, j - 2) * CH, (j + 1) * CH
        scores = contract(q_ref[j * CH : high, :], k_ref[low:high, :], 1, 1) * SCALE
        scores = jnp.where(allowed_pairs(seg_col, seg_row, j, low, high), scores, NEG)
        peak = jnp.max(scores, axis=-1, keepdims=True)
        weights = jnp.exp(scores - peak)
        total = jnp.sum(weights, axis=-1, keepdims=True)
        probs = (weights * (1.0 / total)).astype(BF16)
        o_ref[j * CH : high, :] = contract(probs, v_ref[low:high, :], 1, 0).astype(BF16)
        lse_ref[0, j * CH : high, :] = peak + jnp.log(total)
        top = jnp.maximum(top, jnp.max(peak, axis=0, keepdims=True))
    top_ref[0] = jnp.broadcast_to(top, (8, 128))


def attend_back_kernel(
    seg_col, seg_row, q_ref, k_ref, v_ref, do_ref, lse_ref, dq_ref, dk_ref, dv_ref, dk_sum, dv_sum
):
    dk_sum[...] = jnp.zeros_like(dk_sum)
    dv_sum[...] = jnp.zeros_like(dv_sum)
    for j in range(LEN // CH):
        low, high = max(0, j - 2) * CH, (j + 1) * CH
        query, keys = q_ref[j * CH : high, :], k_ref[low:high, :]
        grad = do_ref[j * CH : high, :]
        scores = contract(query, keys, 1, 1) * SCALE
        allowed = allowed_pairs(seg_col, seg_row, j, low, high)
        probs = jnp.where(allowed, jnp.exp(scores - lse_ref[0, j * CH : high, :]), 0.0)
        grad_probs = contract(grad, v_ref[low:high, :], 1, 1)
        inner = jnp.sum(probs * grad_probs, axis=-1, keepdims=True)
        grad_scores = (probs * (grad_probs - inner)).astype(BF16)
        dq_ref[j * CH : high, :] = (contract(grad_scores, keys, 1, 0) * SCALE).astype(BF16)
        dk_sum[low:high, :] += contract(grad_scores, query, 0, 0)
        dv_sum[low:high, :] += contract(probs.astype(BF16), grad, 0, 0)
    dk_ref[...] = (dk_sum[...] * SCALE).astype(BF16)
    dv_ref[...] = dv_sum[...].astype(BF16)


def head_specs():
    seg_col = pl.BlockSpec((1, LEN, 1), lambda s, h: (s, 0, 0))
    seg_row = pl.BlockSpec((1, 1, LEN), lambda s, h: (s, 0, 0))
    thirds = [pl.BlockSpec((LEN, DH), lambda s, h, n=n: (s, 2 * n + h)) for n in range(3)]
    lse = pl.BlockSpec((1, LEN, 1), lambda s, h: (2 * s + h, 0, 0))
    return seg_col, seg_row, thirds, lse


def attend(seg_col, seg_row, qkv):
    seg_c, seg_r, thirds, lse = head_specs()
    return pl.pallas_call(
        attend_kernel,
        name="attend",
        grid=(2, 2),
        in_specs=[seg_c, seg_r, *thirds],
        out_specs=[thirds[0], lse, pl.BlockSpec((1, 8, 128), lambda s, h: (2 * s + h, 0, 0))],
        out_shape=[
            jax.ShapeDtypeStruct((2 * LEN, 2 * DH), BF16),
            jax.ShapeDtypeStruct((4, LEN, 1), F32),
            jax.ShapeDtypeStruct((4, 8, 128), F32),
        ],
        compiler_params=pltpu.CompilerParams(vmem_limit_bytes=40 << 20),
        cost_estimate=pl.CostEstimate(flops=1 << 20, bytes_accessed=1 << 10, transcendentals=0),
    )(seg_col, seg_row, qkv, qkv, qkv)


def attend_back(seg_col, seg_row, qkv, grad, lse_all):
    seg_c, seg_r, thirds, lse = head_specs()
    return pl.pallas_call(
        attend_back_kernel,
        name="attend_back",
        grid=(2, 2),
        in_specs=[seg_c, seg_r, *thirds, thirds[0], lse],
        out_specs=[thirds[0]] * 3,
        out_shape=[jax.ShapeDtypeStruct((2 * LEN, 2 * DH), BF16)] * 3,
        scratch_shapes=[pltpu.VMEM((LEN, DH), F32), pltpu.VMEM((LEN, DH), F32)],
        compiler_params=pltpu.CompilerParams(vmem_limit_bytes=40 << 20),
        cost_estimate=pl.CostEstimate(flops=5 << 30, bytes_accessed=8 << 20, transcendentals=1 << 22),
    )(seg_col, seg_row, qkv, qkv, qkv, grad, lse_all)


def lay_out_kernel(fold, in_ref, out_ref):
    parts, _, col_units, rows, width = in_ref.shape
    height, width = parts * rows, width // fold
    for j in range(col_units):
        for k in range(fold):
            piece = in_ref[:, 0, j, :, k * width : (k + 1) * width].reshape(height, width)
            out_ref[k * height : (k + 1) * height, j * width : (j + 1) * width] = piece


def lay_out(full, fold=1):
    parts, row_units, col_units, rows, width = full.shape
    block = (fold * parts * rows, col_units * width // fold)
    shape = (row_units * block[0], block[1])
    return pl.pallas_call(
        functools.partial(lay_out_kernel, fold),
        name="lay_out",
        grid=(row_units,),
        in_specs=[pl.BlockSpec((parts, 1, col_units, rows, width), lambda n: (0, n, 0, 0, 0))],
        out_specs=pl.BlockSpec(block, lambda n: (n, 0)),
        out_shape=jax.ShapeDtypeStruct(shape, BF16),
        compiler_params=pltpu.CompilerParams(vmem_limit_bytes=24 << 20),
        cost_estimate=pl.CostEstimate(flops=0, bytes_accessed=4 * shape[0] * shape[1], transcendentals=0),
    )(full)


def block_tables(owners, per_owner, rank):
    ids = jnp.arange(owners.shape[0], dtype=jnp.int32)
    earlier = (owners[None, :] == owners[:, None]) & (ids[None, :] < ids[:, None])
    slots = owners * per_owner + jnp.sum(earlier.astype(jnp.int32), axis=1)
    mine = rank * per_owner + jnp.arange(per_owner, dtype=jnp.int32)
    own_ids = jnp.sum(jnp.where(slots[None, :] == mine[:, None], ids[None, :], 0), axis=1)
    return slots, own_ids


def column_scale(block_ids, root_factor):
    per_row = 3 * D // BC
    columns = (block_ids % per_row)[:, None] * BC + jnp.arange(BC, dtype=jnp.int32)[None, :]
    head_of = columns % D // DH
    picked = jnp.sum(
        jnp.where(head_of[..., None] == jnp.arange(HEADS, dtype=jnp.int32), root_factor, 0.0), axis=-1
    )
    inside = (block_ids < D // BR * per_row)[:, None] & (columns < 2 * D)
    return jnp.where(inside, picked, 1.0)


def vector_scale(positions, root_factor):
    inside = (positions < 8 * D) & (positions % 8 == 2)
    head_of = positions // 8 // DH
    picked = jnp.sum(
        jnp.where(head_of[:, None] == jnp.arange(HEADS, dtype=jnp.int32), root_factor, 0.0), axis=-1
    )
    return jnp.where(inside, picked, 1.0)


def split3(matrix):
    high = matrix.astype(BF16)
    return high, (matrix - high.astype(F32)).astype(BF16)


def dot3(left, right, right_dim=0):
    (a, b), (c, d) = left, right
    return contract(a, c, 1, right_dim) + (contract(a, d, 1, right_dim) + contract(b, c, 1, right_dim))


def update_kernel(
    clip_ref, scale_ref, grad_ref, first_ref, second_ref, left_ref, right_ref, block_ref,
    new_block_ref, new_first_ref, new_second_ref, copy_ref,
):
    grad = clip_ref[0] * grad_ref[0]
    new_first = 0.5 * first_ref[0] + 0.5 * grad
    new_first_ref[0] = new_first
    left, right = left_ref[0], split3(right_ref[0])
    turned = dot3(split3(left.T), split3(jnp.concatenate([grad, new_first], axis=1)))
    turned = dot3(split3(jnp.concatenate([turned[:, :BC], turned[:, BC:]], axis=0)), right)
    new_second = 0.5 * second_ref[0] + 0.5 * jnp.square(turned[:BR])
    new_second_ref[0] = new_second
    ratio = turned[BR:] / (jnp.sqrt(new_second) + 1e-08)
    back = dot3(split3(dot3(split3(left), split3(ratio))), right, 1)
    new_block = (block_ref[0] - 0.01 * back) * scale_ref[0]
    new_block_ref[0] = new_block
    copy_ref[0] = new_block.astype(BF16)


def update_blocks(clip, scale, grads, first, second, left, right, blocks):
    count = blocks.shape[0]
    one = pl.BlockSpec((1, BR, BC), lambda n: (n, 0, 0))
    whole = jax.ShapeDtypeStruct(blocks.shape, F32)
    return pl.pallas_call(
        update_kernel,
        name="update_blocks",
        grid=(count,),
        in_specs=[
            pl.BlockSpec(memory_space=pltpu.SMEM),
            pl.BlockSpec((1, 1, BC), lambda n: (n, 0, 0)),
            one, one, one,
            pl.BlockSpec((1, BR, BR), lambda n: (n, 0, 0)),
            pl.BlockSpec((1, BC, BC), lambda n: (n, 0, 0)),
            one,
        ],
        out_specs=[one] * 4,
        out_shape=[whole, whole, whole, jax.ShapeDtypeStruct(blocks.shape, BF16)],
        compiler_params=pltpu.CompilerParams(vmem_limit_bytes=40 << 20),
        cost_estimate=pl.CostEstimate(
            flops=count * (18 << 26), bytes_accessed=count * (23 << 18), transcendentals=count << 17
        ),
    )(clip.reshape(1), scale[:, None, :], grads, first, second, left, right, blocks)


def make_local(outer):
    devices = outer * 32
    rows = BR // devices
    qkv_end = D // BR * (3 * D // BC)
    out_end = qkv_end + D // BR * (D // BC)
    up_end = out_end + D // BR * (FF // BC)

    def everyone(array):
        return lax.all_to_all(array, EVERY, 0, 0, tiled=True)

    def grouped(array):
        return lax.all_to_all(array, GROUP, 0, 0, tiled=True)

    def cut(matrices):
        parts = matrices.reshape(matrices.shape[0], outer, 2, 2, 2, 2, 2, rows, BC)
        return parts.transpose(1, 4, 5, 6, 2, 3, 0, 7, 8).reshape(-1, rows, BC)

    def uncut(parts, count):
        parts = parts.reshape(outer, 2, 2, 2, 2, 2, count, rows, BC)
        return parts.transpose(6, 0, 4, 5, 1, 2, 3, 7, 8).reshape(count, BR, BC)

    def assemble(full, row_units, col_units, width):
        full = full.reshape(devices, row_units, col_units, rows, width)
        if rows != 8:
            return full.transpose(1, 0, 3, 2, 4).reshape(row_units * BR, col_units * width)
        return lay_out(full)

    def assemble_qkv(full):
        full = full.reshape(devices, 4, 3, rows, BC)
        if rows != 8:
            full = full.reshape(devices, 4, 3, rows, 2, CH).transpose(1, 4, 0, 3, 2, 5)
            return full.reshape(D, 3 * CH)
        return lay_out(full, 2)

    def take_apart(grad, row_units, col_units, width):
        full = grad.astype(BF16).reshape(row_units, devices, rows, col_units, width)
        full = full.transpose(1, 0, 3, 2, 4)
        return full.reshape(outer * 4, TP, row_units * col_units, rows, width)

    def local(
        tokens, segments, out_grad, owners, blocks, first_moment, second_moment,
        left_bases, right_bases, vectors, vector_first, vector_second,
    ):
        per_owner, vector_part = blocks.shape[0], vectors.shape[0]
        p, q, i, c, h, l = (lax.axis_index(name) for name in EVERY)
        rank = ((((p * 2 + q) * 2 + i) * 2 + c) * 2 + h) * 2 + l
        member = (q * 2 + i) * 2 + c

        def data_gather(piece):
            return lax.all_gather(piece, DATA, axis=0)

        def data_scatter(full):
            return lax.psum_scatter(full, DATA, scatter_dimension=0, tiled=False)

        low = jnp.pad(vectors.astype(BF16), (0, rows * BC - vector_part))
        low = jnp.broadcast_to(low.reshape(1, 1, rows, BC), (devices, 1, rows, BC))
        sent = jnp.concatenate([cut(blocks.astype(BF16)).reshape(devices, per_owner, rows, BC), low], axis=1)
        pieces = everyone(sent.reshape(-1, rows, BC))
        seg = at(at(pair_up(pair_up(segments, "c"), "i"), l), h)
        seg = pair_up(seg, "q").reshape(2, LEN)
        seg_col, seg_row = seg[:, :, None], seg[:, None, :]
        x_low = swap_tokens(tokens.reshape(CH, D))
        dy = swap_tokens(out_grad.reshape(CH, D))
        x_all = group_gather(x_low).reshape(2, 2, 2, CH, D)
        dy_all = group_gather(dy).reshape(2, 2, 2, CH, D)
        slots, own_ids = block_tables(owners, per_owner, rank)
        rest_order = jnp.concatenate(
            [
                slots[qkv_end:out_end].reshape(TP, -1),
                slots[out_end:up_end].reshape(8, TP, 2).transpose(1, 0, 2).reshape(TP, -1),
                slots[up_end:].reshape(TP, -1),
            ],
            axis=1,
        )
        order = jnp.concatenate(
            [slots[:qkv_end].reshape(8, 3, 4).transpose(2, 0, 1).reshape(-1), rest_order.reshape(-1)]
        )
        order = order + order // per_owner + (nothing_of(seg_row) + nothing_of(x_low) + nothing_of(dy)).astype(jnp.int32)
        got_order = order - order // (per_owner + 1)
        place = jnp.arange(devices * (per_owner + 1), dtype=jnp.int32)
        pick = (order[:, None] == place[None, :]).astype(BF16)
        got_pick = (got_order[:, None] == place[None, : devices * per_owner]).astype(BF16)
        vector_all = pieces.reshape(devices, per_owner + 1, rows * BC)[:, per_owner, :vector_part]
        vector_all = vector_all.reshape(-1).astype(F32)
        feature = vector_all[: 8 * D].reshape(D, 8)
        ln1_gain, ln1_shift, q_bias, v_bias, out_bias, ln2_gain, ln2_shift, down_bias = (
            feature[:, n] for n in range(8)
        )
        up_bias = lax.dynamic_slice_in_dim(vector_all, 8 * D + member * (FF // TP), FF // TP)
        qkv_bias = jnp.concatenate(
            [
                lax.dynamic_slice_in_dim(q_bias, member * CH, CH),
                jnp.zeros((CH,), F32),
                lax.dynamic_slice_in_dim(v_bias, member * CH, CH),
            ]
        )
        pieces = lax.dot_general(pick, pieces, (((1,), (0,)), ((), ())), preferred_element_type=BF16)
        part = pieces[:qkv_end].reshape(4, 4, 2, 3, rows, 2, CH).transpose(0, 5, 1, 3, 4, 2, 6)
        part = jnp.concatenate(
            [part.reshape(TP, 12, rows, BC), pieces[qkv_end:].reshape(TP, 36, rows, BC)], axis=1
        )
        part = grouped(part.reshape(-1, rows, BC)).reshape(TP, 48, rows, BC)
        part, x_all = together(part, x_all)
        w_first, part = together(data_gather(part[:, :16]), part)
        w_qkv, w_out = w_first[:, :, :12], w_first[:, :, 12:]
        w_up = data_gather(part[:, 16:32])
        w_down = data_gather(part[:, 32:])
        w_qkv = assemble_qkv(w_qkv)
        w_out = assemble(w_out, 1, 4, BC)
        x = x_low.astype(F32)
        unit_all, _ = norm_parts(x_all.reshape(2 * LEN, D).astype(F32))
        a_all = (unit_all * ln1_gain + ln1_shift).astype(BF16)
        a_all = a_all.reshape(2, 2, 2, CH, D).transpose(0, 2, 1, 3, 4).reshape(2 * LEN, D)
        dy_all = to_relative(dy_all.transpose(0, 2, 1, 3, 4)).reshape(2, 4 * CH, D)
        unit1, inverse1 = norm_parts(x)

        a_all, dy_all = together(a_all, dy_all)
        qkv = (jnp.dot(a_all, w_qkv, preferred_element_type=F32) + qkv_bias).astype(BF16)
        mixed, lse, tops = attend(seg_col, seg_row, qkv)
        h1 = x + scatter_chips(scatter_core(mixed, w_out, 0)) + out_bias
        unit2, inverse2 = norm_parts(h1)
        c_own, w_up = together((unit2 * ln2_gain + ln2_shift).astype(BF16), w_up)
        w_up = assemble(w_up, 8, 2, BC)
        c_two = gather_relative(c_own)

        u_two = [jnp.dot(tokens_of, w_up, preferred_element_type=F32) + up_bias for tokens_of in c_two]
        u_two[0], u_two[1], w_down = together(u_two[0], u_two[1], w_down)
        w_down = assemble(w_down, 4, 4, BC)

        def half(u, grads):
            dg = contract(grads, w_down, 1, 1)
            cdf = 0.5 * (1.0 + lax.erf(u * math.sqrt(0.5)))
            slope = cdf + u * jnp.exp(-0.5 * u * u) * (1.0 / math.sqrt(2.0 * math.pi))
            return (u * cdf).astype(BF16), (dg * slope).astype(BF16)

        g_mine, du_mine = half(u_two[0], dy_all[0])
        g_other, du_other = half(u_two[1], dy_all[1])
        grad_down = contract(g_mine, dy_all[0], 0, 0) + contract(g_other, dy_all[1], 0, 0)
        grad_down = take_apart(grad_down, 4, 4, BC)
        du_mine, du_other, grad_down = together(du_mine, du_other, grad_down)
        got_down = data_scatter(grad_down)
        send = contract(du_other, w_up, 1, 1).astype(BF16)
        keep = contract(after(du_mine, send), w_up, 1, 1)
        dc_core = keep, trade(send, "c")
        du_mine, du_other = after((du_mine, du_other), keep)
        grad_up = contract(c_two[0], du_mine, 0, 0) + contract(c_two[1], du_other, 0, 0)
        grad_up = take_apart(grad_up, 8, 2, BC)
        got_up = data_scatter(grad_up)
        dc = scatter_relative(dc_core, grad_up)
        back2, ln2_gain_grad, ln2_shift_grad = norm_back(dc, unit2, inverse2, ln2_gain)
        dh1 = dy.astype(F32) + back2
        da_own, got_down = together(dh1.astype(BF16), got_down)
        g_mine, g_other = after((g_mine, g_other), da_own)
        send = contract(g_other, w_down, 1, 0).astype(BF16)
        keep = contract(g_mine, w_down, 1, 0)
        da_two = gather_relative(da_own, keep)
        do = jnp.stack([contract(rows, w_out, 1, 1).astype(BF16) for rows in da_two])
        do = to_member(do.reshape(2, 2, 2, CH, 2 * DH)).reshape(2 * LEN, 2 * DH)
        dqkv = jnp.concatenate(attend_back(seg_col, seg_row, qkv, do, lse), axis=1)
        dqkv, got_up = together(dqkv, got_up)
        grad_qkv = take_apart(contract(a_all, dqkv, 0, 0), 8, 3, CH)
        mixed_two = to_relative(mixed.reshape(2, 2, 2, CH, 2 * DH)).reshape(2, 4 * CH, 2 * DH)
        mixed_two = after(mixed_two, grad_qkv)
        grad_out = contract(mixed_two[0], da_two[0], 0, 0) + contract(mixed_two[1], da_two[1], 0, 0)
        grad_out = take_apart(grad_out, 1, 8, CH)
        got_first = data_scatter(jnp.concatenate([grad_qkv, grad_out], axis=2))
        dqkv, grad_out = together(dqkv, grad_out)
        da = scatter_chips(scatter_core(dqkv, w_qkv, 1))
        got_rest = grouped(jnp.concatenate([got_up, got_down], axis=1).reshape(-1, rows, BC))
        da, got_rest = together(da, got_rest)
        back1, ln1_gain_grad, ln1_shift_grad = norm_back(da, unit1, inverse1, ln1_gain)
        send, ln1_gain_grad = together(send, ln1_gain_grad)
        branch = keep, trade(send, "c")
        du_sum = jnp.sum(du_mine.astype(F32), axis=0) + jnp.sum(du_other.astype(F32), axis=0)
        dqkv_sum = jnp.sum(dqkv.astype(F32), axis=0)

        def spread(values, size):
            return lax.dynamic_update_slice_in_dim(jnp.zeros((size,), F32), values, member * values.shape[0], 0)

        terms = jnp.stack(
            [
                ln1_gain_grad, ln1_shift_grad, spread(dqkv_sum[:CH], D), spread(dqkv_sum[2 * CH :], D),
                jnp.sum(da_own.astype(F32), axis=0), ln2_gain_grad, ln2_shift_grad,
                jnp.sum(dy.astype(F32), axis=0),
            ],
            axis=1,
        ).reshape(-1)
        terms = jnp.concatenate([terms, spread(du_sum, FF)])
        vector_grads = jnp.sum(everyone(terms.reshape(devices, vector_part)), axis=0)

        got_first, branch, vector_grads, got_rest = together(got_first, branch, vector_grads, got_rest)
        got_first = grouped(got_first.reshape(-1, rows, CH))
        got_first = got_first.reshape(TP, 32, rows, CH)
        got_qkv = got_first[:, :24].reshape(4, 2, 24, rows, CH).transpose(0, 2, 3, 1, 4).reshape(-1, rows, BC)
        got_out = got_first[:, 24:].reshape(TP, 4, 2, rows, CH).transpose(0, 1, 3, 2, 4)
        got_rest = jnp.concatenate(
            [got_out.reshape(TP, 4, rows, BC), got_rest.reshape(TP, 32, rows, BC)], axis=1
        ).reshape(-1, rows, BC)
        got = jnp.concatenate([got_qkv, got_rest], axis=0)
        got = lax.dot_general(got_pick, got, (((0,), (0,)), ((), ())), preferred_element_type=BF16)
        branch, got = together(branch, got)
        owned = everyone(got)
        block_grads = uncut(owned, per_owner).astype(F32)
        branch = scatter_relative(branch)
        out_own = (h1 + branch + down_bias).astype(BF16)
        input_own = (dh1 + back1).astype(BF16)
        head_ids = jnp.arange(HEADS, dtype=jnp.int32)
        tops = jnp.max(tops[:, 0, 0].reshape(2, 2), axis=0)
        tops = jnp.where(head_ids // 2 == member, jnp.where(head_ids % 2 == 0, tops[0], tops[1]), NEG)
        square = jnp.sum(block_grads * block_grads) + jnp.sum(vector_grads * vector_grads)
        square, out_own = together(square, out_own)
        told = jnp.concatenate([tops, square[None], jnp.zeros((128 - HEADS - 1,), F32)])
        told = everyone(jnp.broadcast_to(told[None, None], (devices, 1, 128))).reshape(devices, 128)
        out_own, input_own, told = together(out_own, input_own, told)
        out_tokens = swap_tokens(out_own)
        input_grad = swap_tokens(input_own).astype(F32)
        head_max = jnp.max(told[:, :HEADS], axis=0)
        grad_norm = jnp.sqrt(jnp.sum(told[:, HEADS]))
        total_params = slots.shape[0] * BR * BC + vector_part * devices
        clip = jnp.minimum(1.0, math.sqrt(total_params) / (grad_norm + 1e-06))
        tau = jnp.mean(head_max)
        clip_factors = tau / jnp.maximum(head_max, tau)
        root_factor = jnp.sqrt(clip_factors)
        new_blocks, new_first, new_second, copies = update_blocks(
            clip, column_scale(own_ids, root_factor), block_grads, first_moment, second_moment,
            left_bases, right_bases, blocks,
        )
        vclipped = vector_grads * clip
        new_vector_first = 0.5 * vector_first + 0.5 * vclipped
        new_vector_second = 0.5 * vector_second + 0.5 * vclipped * vclipped
        vupdated = vectors - 0.1 * new_vector_first / (jnp.sqrt(new_vector_second) + 1e-08)
        positions = rank * vector_part + jnp.arange(vector_part, dtype=jnp.int32)
        new_vectors = vupdated * vector_scale(positions, root_factor)
        return (
            out_tokens[None],
            input_grad[None],
            block_grads,
            vector_grads,
            new_blocks,
            new_first,
            new_second,
            copies,
            new_vectors,
            new_vector_first,
            new_vector_second,
            new_vectors.astype(BF16),
            grad_norm,
            clip_factors,
        )

    return local


def solution(mesh):
    outer = mesh.shape["dp"] // 8
    fine = Mesh(mesh.devices.reshape(outer, 2, 2, 2, 2, 2), EVERY)
    seq, pos = ("p", "q", "i", "c"), ("h", "l")
    token, owned, entry = P(seq, pos, None), P(EVERY, None, None), P(EVERY)
    return jax.shard_map(
        make_local(outer),
        mesh=fine,
        in_specs=(token, P(seq, None), token, P(), *[owned] * 5, *[entry] * 3),
        out_specs=(token, token, owned, entry, *[owned] * 4, *[entry] * 4, P(), P()),
        check_vma=False,
    )
```

time: 1360 us -> 1090 us (0.80)
  starting transfers between devices: 190 us -> 51.7 us
  matrix products: 206 us -> 136 us
  blocking collectives: 34.1 us -> 91.9 us
  local copies, waits for them, and re-layouts: 156 us -> 99.6 us
  waiting for transfers between devices: 574 us -> 521 us
  other arithmetic: 136 us -> 98.9 us
  Pallas kernels: 22.3 us -> 56.8 us
    ppermute x53 -> x33, waiting for transfers between devices: 445 us -> 267 us  [trade(): return lax.ppermute(array, axis, [(0, 1), (1, 0)])]
    ppermute x4, waiting for transfers between devices: 0.01 us -> 101 us  [swap_tokens(): lax.ppermute(array, ('i', 'c', 'h', 'l'), [pair for pair in pairs if pair...]
    all_gather x0 -> x3, waiting for transfers between devices: none -> 96.7 us  [data_gather(): return lax.all_gather(piece, DATA, axis=0)]
    all_to_all x9 -> x4, waiting for transfers between devices: 130 us -> 34 us  [the longest x3 34 us: everyone(): return lax.all_to_all(array, EVERY, 0, 0, tiled=True)]
    dot_general x10 -> x3, matrix products: 111 us -> 20.9 us  [the longest x2 18 us: local(): jnp.dot(tokens_of, w_up, preferred_element_type=F32) + up_bias]
    ppermute x53 -> x33, starting transfers between devices: 84.5 us -> 17.8 us  [trade(): return lax.ppermute(array, axis, [(0, 1), (1, 0)])]
    all_to_all x2 -> x3, blocking collectives: 34.1 us -> 91.9 us  [the longest x2 80.2 us: grouped(): return lax.all_to_all(array, GROUP, 0, 0, tiled=True)]
    all_to_all x9 -> x4, starting transfers between devices: 67.1 us -> 21.1 us  [the longest x3 14.8 us: everyone(): return lax.all_to_all(array, EVERY, 0, 0, tiled=True)]
  transfers between devices with their start and end apart: 70 -> 49, of which waited for: 43 -> 36; matrix products, arithmetic and copies ran while one was open for 26% -> 19% of each run, Pallas kernels for 1% -> 4%
where the time goes in v2:
time: 1090 us; the launch traced here: 1080 us
  waiting for transfers between devices  521 us (48%)
  matrix products  136 us (12%)
  local copies, waits for them, and re-layouts  99.6 us (9%)
  other arithmetic  98.9 us (9%)
  blocking collectives  91.9 us (8%)
  Pallas kernels  56.8 us (5%)
  starting transfers between devices  51.7 us (5%)
  between operations  23.5 us (2%)
    ppermute x33, waiting for transfers between devices, trade(): return lax.ppermute(array, axis, [(0, 1), (1, 0)])  267 us
    dot_general x19, matrix products, contract(): lax.dot_general(left, right, (((left_dim,), (right_dim,)), ((), ())), pre...  105 us
    ppermute x4, waiting for transfers between devices, swap_tokens(): lax.ppermute(array, ('i', 'c', 'h', 'l'), [pair for pair in pairs if pair...  101 us
    all_gather x3, waiting for transfers between devices, data_gather(): return lax.all_gather(piece, DATA, axis=0)  96.7 us
    all_to_all x2, blocking collectives, grouped(): return lax.all_to_all(array, GROUP, 0, 0, tiled=True)  80.2 us
    all_to_all x3, waiting for transfers between devices, everyone(): return lax.all_to_all(array, EVERY, 0, 0, tiled=True)  34 us
    unnamed x176, local copies, waits for them, and re-layouts  33.5 us
    pallas_call x1, Pallas kernels, update_blocks(): pl.pallas_call(update_kernel, name='update_blocks', grid=(count,), in_spe...  32.3 us
  transfers between devices with their start and end apart: 49, of which 36 were waited for; matrix products, arithmetic and copies ran while one was open for 19% of the time, Pallas kernels for 4%

profile of v2, /device:TPU:6, one launch (start us, length us, event | category | flops | bytes accessed | tf_op | source)
XLA Modules:
  0.0 1079.3 jit_solution(8723721981218025061)
XLA Ops:
  7.2 3.6 collective-permute-start.3
  10.9 58.9 %collective-permute-done.3 = bf16[256,2048]{1,0:T(8,128)(2,1)S(1)} collective-permute-done((bf16[256,2048]{1,0:T(8,128)(2,1)}, bf16[256,2048]{1,0:T(8,128)(2,1)S(1)}, u32[]{:S(2)}, u32[]{:S(2)}) %collective-permute-start.3) | collective-permute-done | bytes 1048608 | tf_op jit(solution)/shard_map/ppermute | solution.py:55
  74.3 15.8 %collective-permute-done.4 = bf16[256,2048]{1,0:T(8,128)(2,1)S(1)} collective-permute-done((bf16[256,2048]{1,0:T(8,128)(2,1)S(1)}, bf16[256,2048]{1,0:T(8,128)(2,1)S(1)}, u32[]{:S(2)}, u32[]{:S(2)}) %collective-permute-start.4) | collective-permute-done | bytes 1048608 | tf_op jit(solution)/shard_map/ppermute | solution.py:55
  103.3 28.8 %collective-permute-done.1 = s32[2,1,1024]{2,1,0:T(1,128)S(1)} collective-permute-done((s32[2,1,1024]{2,1,0:T(1,128)S(1)}, s32[2,1,1024]{2,1,0:T(1,128)S(1)}, u32[]{:S(2)}, u32[]{:S(2)}) %collective-permute-start.1) | collective-permute-done | bytes 8224 | tf_op jit(solution)/shard_map/ppermute | solution.py:37
  141.4 34.0 %all-to-all-done = bf16[416,8,512]{2,1,0:T(8,128)(2,1)S(1)} async-done(((bf16[416,8,512]{2,1,0:T(8,128)(2,1)}), bf16[416,8,512]{2,1,0:T(8,128)(2,1)S(1)}, u32[]{:S(2)}, u32[]{:S(2)}) %all-to-all-start) | async-done | bytes 3407904 | tf_op jit(solution)/shard_map/all_to_all | solution.py:355
  187.5 61.1 %all_to_all.39 = bf16[384,8,512]{2,1,0:T(8,128)(2,1)S(1)} all-to-all(bf16[384,8,512]{2,1,0:T(8,128)(2,1)S(1)} %bitcast.438), channel_id=1, replica_groups=mesh['p'=1,'q'=2,'i'=2,'c'=2,'h'=2,'l'=2] {'q','i','c'}, dimensions={0} | all-to-all | bytes 6291456 | tf_op jit(solution)/shard_map/all_to_all | solution.py:358
  251.0 6.9 reshape.747
  260.1 3.6 slice_reduce_fusion
  263.9 4.5 convert_reduce_fusion
  268.5 5.4 fusion.2
  281.4 3.6 slice-done.1
  284.9 5.3 fusion.5
  290.3 43.6 %all-gather.13.cloned.1.call-done = bf16[32,16,8,512]{3,2,1,0:T(8,128)(2,1)} async-done(((bf16[8,16,8,512]{3,2,1,0:T(8,128)(2,1)}), bf16[32,16,8,512]{3,2,1,0:T(8,128)(2,1)}) %all-gather.13.cloned.1.call-update) | async-done | bytes 4194320 | tf_op jit(solution)/shard_map/all_gather | solution.py:396
  341.0 6.8 add_convert_fusion.6.q_ref.k_ref.v_ref
  347.8 9.8 attend.1
  363.5 5.2 collective-permute-done.5
  368.8 3.9 add_convert_fusion.5
  378.1 23.0 %collective-permute-done.8 = bf16[2,256,1024]{2,1,0:T(8,128)(2,1)} collective-permute-done((bf16[2,256,1024]{2,1,0:T(8,128)(2,1)}, bf16[2,256,1024]{2,1,0:T(8,128)(2,1)}, u32[]{:S(2)}, u32[]{:S(2)}) %collective-permute-start.8) | collective-permute-done | bytes 1048608 | tf_op jit(solution)/shard_map/ppermute | solution.py:37
  404.5 11.4 %collective-permute-done.9 = bf16[256,1024]{1,0:T(8,128)(2,1)S(1)} collective-permute-done((bf16[256,1024]{1,0:T(8,128)(2,1)S(1)}, bf16[256,1024]{1,0:T(8,128)(2,1)S(1)}, u32[]{:S(2)}, u32[]{:S(2)}) %collective-permute-start.9) | collective-permute-done | bytes 524320 | tf_op jit(solution)/shard_map/ppermute | solution.py:37
  420.0 22.9 %all-gather.15.cloned.1.call-done = bf16[32,16,8,512]{3,2,1,0:T(8,128)(2,1)} async-done(((bf16[8,16,8,512]{3,2,1,0:T(8,128)(2,1)}), bf16[32,16,8,512]{3,2,1,0:T(8,128)(2,1)}) %all-gather.15.cloned.1.call-update) | async-done | bytes 4194320 | tf_op jit(solution)/shard_map/all_gather | solution.py:396
  444.4 12.6 %collective-permute-done.12 = bf16[256,1024]{1,0:T(8,128)(2,1)S(1)} collective-permute-done((bf16[256,1024]{1,0:T(8,128)(2,1)S(1)}, bf16[256,1024]{1,0:T(8,128)(2,1)S(1)}, u32[]{:S(2)}, u32[]{:S(2)}) %collective-permute-start.12) | collective-permute-done | bytes 524320 | tf_op jit(solution)/shard_map/ppermute | solution.py:37
  460.3 22.0 %collective-permute-done.13 = bf16[2,256,1024]{2,1,0:T(8,128)(2,1)} collective-permute-done((bf16[2,256,1024]{2,1,0:T(8,128)(2,1)}, bf16[2,256,1024]{2,1,0:T(8,128)(2,1)}, u32[]{:S(2)}, u32[]{:S(2)}) %collective-permute-start.13) | collective-permute-done | bytes 1048608 | tf_op jit(solution)/shard_map/ppermute | solution.py:37
  491.8 9.7 broadcast_add_fusion.1
  501.5 8.3 broadcast_add_fusion
  509.7 30.1 %all-gather.17.cloned.1.call-done = bf16[32,16,8,512]{3,2,1,0:T(8,128)(2,1)} async-done(((bf16[8,16,8,512]{3,2,1,0:T(8,128)(2,1)}), bf16[32,16,8,512]{3,2,1,0:T(8,128)(2,1)}) %all-gather.17.cloned.1.call-update) | async-done | bytes 4194320 | tf_op jit(solution)/shard_map/all_gather | solution.py:396
  545.2 9.7 fusion.17
  555.0 7.0 fusion.11
  562.9 7.0 fusion.18
  569.8 7.3 add_convert_fusion.4
  579.5 8.3 convolution_convert_fusion.3
  587.9 7.4 collective-permute-done.15
  595.3 8.6 add_convert_fusion.3
  607.1 6.9 fusion.138
  614.0 7.3 add_convert_fusion.2
  625.9 4.7 collective-permute-done.16
  637.3 11.2 %collective-permute-done.19 = bf16[256,1024]{1,0:T(8,128)(2,1)S(1)} collective-permute-done((bf16[256,1024]{1,0:T(8,128)(2,1)S(1)}, bf16[256,1024]{1,0:T(8,128)(2,1)S(1)}, u32[]{:S(2)}, u32[]{:S(2)}) %collective-permute-start.19) | collective-permute-done | bytes 524320 | tf_op jit(solution)/shard_map/ppermute | solution.py:37
  652.9 10.5 reduce-scatter.4.cloned.1.call-done
  665.7 12.8 %collective-permute-done.22 = bf16[256,1024]{1,0:T(8,128)(2,1)} collective-permute-done((bf16[256,1024]{1,0:T(8,128)(2,1)}, bf16[256,1024]{1,0:T(8,128)(2,1)}, u32[]{:S(2)}, u32[]{:S(2)}) %collective-permute-start.22) | collective-permute-done | bytes 524320 | tf_op jit(solution)/shard_map/ppermute | solution.py:37
  682.1 4.5 fusion.139
  687.9 16.0 %collective-permute-done.23 = bf16[2,256,1024]{2,1,0:T(8,128)(2,1)S(1)} collective-permute-done((bf16[2,256,1024]{2,1,0:T(8,128)(2,1)S(1)}, bf16[2,256,1024]{2,1,0:T(8,128)(2,1)S(1)}, u32[]{:S(2)}, u32[]{:S(2)}) %collective-permute-start.23) | collective-permute-done | bytes 1048608 | tf_op jit(solution)/shard_map/ppermute | solution.py:37
  709.0 4.8 collective-permute-done.24
  718.5 12.7 %attend_back.1 = (bf16[2048,256]{1,0:T(8,128)(2,1)S(1)}, bf16[2048,256]{1,0:T(8,128)(2,1)S(1)}, bf16[2048,256]{1,0:T(8,128)(2,1)S(1)}) custom-call(s32[2,1024,1]{2,1,0:T(8,128)S(1)} %copy.139.seg_col, s32[2,1,1024]{2,1,0:T(1,128)S(1)} %pad_add_fusion.1.seg_row, bf16[2048,768]{1,0:T(8,128)(2,1)S(1)} %copy-done.1, bf16[2048,768]{1,0:T(8,128)(2,1)S(1)} %copy-done.1, ...), custom_call_target="tpu_custom_call" | custom-call | flops 5368709120 | bytes 8388608 | tf_op jit(solution)/shard_map/attend_back/pallas_call | solution.py:226
  731.5 12.2 %reduce-scatter.6.cloned.1.call-done = bf16[1,8,16,8,512]{4,3,2,1,0:T(8,128)(2,1)} async-done(((bf16[4,8,16,8,512]{4,3,2,1,0:T(8,128)(2,1)}), bf16[1,8,16,8,512]{4,3,2,1,0:T(8,128)(2,1)}) %reduce-scatter.6.cloned.1.call-update) | async-done | bytes 1048592 | tf_op jit(solution)/shard_map/reduce_scatter | solution.py:399
  743.7 9.5 convolution_convert_fusion.4
  760.6 5.0 convolution_convert_fusion.1
  767.9 5.1 collective-permute-done.25
  773.0 5.8 add_convert_fusion.1
  783.6 6.3 all-to-all-start.2
  789.9 16.9 %collective-permute-done.28 = bf16[2,256,1024]{2,1,0:T(8,128)(2,1)} collective-permute-done((bf16[2,256,1024]{2,1,0:T(8,128)(2,1)}, bf16[2,256,1024]{2,1,0:T(8,128)(2,1)}, u32[]{:S(2)}, u32[]{:S(2)}) %collective-permute-start.28) | collective-permute-done | bytes 1048608 | tf_op jit(solution)/shard_map/ppermute | solution.py:37
  809.1 3.9 collective-permute-done.26
  815.0 6.0 convolution_convert_fusion.2
  821.1 18.7 %collective-permute-done.29 = bf16[256,1024]{1,0:T(8,128)(2,1)S(1)} collective-permute-done((bf16[256,1024]{1,0:T(8,128)(2,1)S(1)}, bf16[256,1024]{1,0:T(8,128)(2,1)S(1)}, u32[]{:S(2)}, u32[]{:S(2)}) %collective-permute-start.29) | collective-permute-done | bytes 524320 | tf_op jit(solution)/shard_map/ppermute | solution.py:37
  850.6 11.7 %all_to_all.41 = f32[32,1,768]{2,1,0:T(1,128)S(1)} all-to-all(f32[32,1,768]{2,1,0:T(1,128)S(1)} %bitcast.485), channel_id=1, replica_groups=mesh['p'=1,'q'=2,'i'=2,'c'=2,'h'=2,'l'=2] {'p','q','i','c','h','l'}, dimensions={0} | all-to-all | bytes 196608 | tf_op jit(solution)/shard_map/all_to_all | solution.py:355
  862.4 19.1 %all_to_all.40 = bf16[256,8,256]{2,1,0:T(8,128)(2,1)S(1)} all-to-all(bf16[256,8,256]{2,1,0:T(8,128)(2,1)} %bitcast.479), channel_id=1, replica_groups=mesh['p'=1,'q'=2,'i'=2,'c'=2,'h'=2,'l'=2] {'q','i','c'}, dimensions={0} | all-to-all | bytes 2097152 | tf_op jit(solution)/shard_map/all_to_all | solution.py:358
  892.8 4.9 all-to-all-start.5
  898.0 6.1 add_convert_fusion
  910.3 38.9 %collective-permute-done.31 = bf16[2,256,1024]{2,1,0:T(8,128)(2,1)} collective-permute-done((bf16[2,256,1024]{2,1,0:T(8,128)(2,1)}, bf16[2,256,1024]{2,1,0:T(8,128)(2,1)}, u32[]{:S(2)}, u32[]{:S(2)}) %collective-permute-start.31) | collective-permute-done | bytes 1048608 | tf_op jit(solution)/shard_map/ppermute | solution.py:37
  958.9 11.6 %collective-permute-done.34 = bf16[256,1024]{1,0:T(8,128)(2,1)S(1)} collective-permute-done((bf16[256,1024]{1,0:T(8,128)(2,1)S(1)}, bf16[256,1024]{1,0:T(8,128)(2,1)S(1)}, u32[]{:S(2)}, u32[]{:S(2)}) %collective-permute-start.34) | collective-permute-done | bytes 524320 | tf_op jit(solution)/shard_map/ppermute | solution.py:37
  978.2 6.8 all-to-all-start.6
  985.0 4.4 fusion.49
  990.4 3.4 copy.149
  1006.8 32.3 %update_blocks.1 = (f32[12,256,512]{2,1,0:T(8,128)}, f32[12,256,512]{2,1,0:T(8,128)}, f32[12,256,512]{2,1,0:T(8,128)}, bf16[12,256,512]{2,1,0:T(8,128)(2,1)}) custom-call(f32[1]{0:T(128)} %bitcast.185.clip_ref, f32[12,1,512]{2,1,0:T(1,128)S(1)} %and_select_fusion.scale_ref, f32[12,256,512]{2,1,0:T(8,128)S(1)} %bitcast.391, f32[12,256,512]{2,1,0:T(8,128)} %first_ref.1, ...), custom_call_target="tpu_custom_call" | custom-call | flops 14495514624 | bytes 72351744 | tf_op jit(solution)/shard_map/update_blocks/pallas_call | solution.py:326
  1039.9 17.2 %collective-permute-done.35 = bf16[256,2048]{1,0:T(8,128)(2,1)} collective-permute-done((bf16[256,2048]{1,0:T(8,128)(2,1)}, bf16[256,2048]{1,0:T(8,128)(2,1)}, u32[]{:S(2)}, u32[]{:S(2)}) %collective-permute-start.35) | collective-permute-done | bytes 1048608 | tf_op jit(solution)/shard_map/ppermute | solution.py:55
  1059.4 8.9 collective-permute-done.36
  (455 shorter events, 213.5 us)
Async XLA Ops:
  7.2 65.2 %copy-start.50 = (bf16[1,256,2048]{2,1,0:T(8,128)(2,1)S(1)}, bf16[1,256,2048]{2,1,0:T(8,128)(2,1)}, u32[]{:S(2)}) copy-start(bf16[1,256,2048]{2,1,0:T(8,128)(2,1)} %param.14) | copy-start | bytes 3145732
  7.2 241.5 %all-gather.9.cloned.1.call-start = ((), (), s32[]{:S(2)}) async-start(), calls=%async_computation.10 | async-start | bytes 9437184 | tf_op jit(solution)/shard_map/all_gather | solution.py:67
  7.2 62.5 %collective-permute-start.3 = (bf16[256,2048]{1,0:T(8,128)(2,1)}, bf16[256,2048]{1,0:T(8,128)(2,1)S(1)}, u32[]{:S(2)}, u32[]{:S(2)}) collective-permute-start(bf16[256,2048]{1,0:T(8,128)(2,1)} %bitcast.477), channel_id=1, source_target_pairs={{1,8},{2,4},{3,12},{4,2},{5,10},{7,14},{8,1},{10,5},{11,13},{12,3}... | collective-permute-start | bytes 3145736 | tf_op jit(solution)/shard_map/ppermute | solution.py:55
  10.8 81.2 %copy-start.60 = (f32[768]{0:T(1024)S(1)}, f32[768]{0:T(1024)}, u32[]{:S(2)}) copy-start(f32[768]{0:T(1024)} %param.21) | copy-start | bytes 9220
  72.3 201.7 %all-gather.11.cloned.1.call-start = ((), (), s32[]{:S(2)}) async-start(), calls=%async_computation.11 | async-start | bytes 9437184 | tf_op jit(solution)/shard_map/all_gather | solution.py:67
  72.3 17.7 %collective-permute-start.4 = (bf16[256,2048]{1,0:T(8,128)(2,1)S(1)}, bf16[256,2048]{1,0:T(8,128)(2,1)S(1)}, u32[]{:S(2)}, u32[]{:S(2)}) collective-permute-start(bf16[256,2048]{1,0:T(8,128)(2,1)S(1)} %bitcast.478), channel_id=1, source_target_pairs={{1,8},{2,4},{3,12},{4,2},{5,10},{7,14},{8,1},{10,5},{11,13},{12,3}... | collective-permute-start | bytes 3145736 | tf_op jit(solution)/shard_map/ppermute | solution.py:55
  97.7 77.7 %all-to-all-start = ((bf16[416,8,512]{2,1,0:T(8,128)(2,1)}), bf16[416,8,512]{2,1,0:T(8,128)(2,1)S(1)}, u32[]{:S(2)}, u32[]{:S(2)}) async-start(bf16[416,8,512]{2,1,0:T(8,128)(2,1)} %bitcast.435), calls=%async_computation | async-start | bytes 6815744 | tf_op jit(solution)/shard_map/all_to_all | solution.py:355
  100.8 233.2 %all-gather.13.cloned.1.call-start = ((), (), s32[]{:S(2)}) async-start(), calls=%async_computation.15 | async-start | bytes 5242880 | tf_op jit(solution)/shard_map/all_gather | solution.py:396
  100.8 1.2 collective-permute-start
  101.3 76.8 %copy-start.66 = (s32[384]{0:T(512)}, s32[384]{0:T(512)S(1)}, u32[]{:S(2)}) copy-start(s32[384]{0:T(512)S(1)} %multiply_add_fusion.1) | copy-start | bytes 4612
  102.1 30.0 %collective-permute-start.1 = (s32[2,1,1024]{2,1,0:T(1,128)S(1)}, s32[2,1,1024]{2,1,0:T(1,128)S(1)}, u32[]{:S(2)}, u32[]{:S(2)}) collective-permute-start(s32[2,1,1024]{2,1,0:T(1,128)S(1)} %pad_add_fusion), channel_id=1, source_target_pairs={{0,8},{8,0},{1,9},{9,1},{2,10},{10,2},{3,11},{11,3},{4,12},{12,4},... | collective-permute-start | bytes 24584 | tf_op jit(solution)/shard_map/ppermute | solution.py:37
  132.1 3.7 collective-permute-start.2
  249.9 193.1 %all-gather.15.cloned.1.call-start = ((), (), s32[]{:S(2)}) async-start(), calls=%async_computation.16 | async-start | bytes 5242880 | tf_op jit(solution)/shard_map/all_gather | solution.py:396
  341.0 27.8 %copy-start.2 = (bf16[256,2048]{1,0:T(8,128)(2,1)}, bf16[256,2048]{1,0:T(8,128)(2,1)S(1)}, u32[]{:S(2)}) copy-start(bf16[256,2048]{1,0:T(8,128)(2,1)S(1)} %lay_out.5) | copy-start | bytes 3145732
  361.3 7.5 collective-permute-start.5
  363.5 176.4 %all-gather.17.cloned.1.call-start = ((), (), s32[]{:S(2)}) async-start(), calls=%async_computation.17 | async-start | bytes 5242880 | tf_op jit(solution)/shard_map/all_gather | solution.py:396
  375.5 25.5 %collective-permute-start.8 = (bf16[2,256,1024]{2,1,0:T(8,128)(2,1)}, bf16[2,256,1024]{2,1,0:T(8,128)(2,1)}, u32[]{:S(2)}, u32[]{:S(2)}) collective-permute-start(bf16[2,256,1024]{2,1,0:T(8,128)(2,1)} %dynamic-slice_bitcast_fusion.2), channel_id=1, source_target_pairs={{0,8},{8,0},{1,9},{9,1},{2,10},{10,2},{3,11},{11,3},{4,12},{12,4},... | collective-permute-start | bytes 3145736 | tf_op jit(solution)/shard_map/ppermute | solution.py:37
  376.1 27.3 %copy-start.35 = (bf16[2,2,256,1024]{3,2,1,0:T(8,128)(2,1)S(1)}, bf16[2,2,256,1024]{3,2,1,0:T(8,128)(2,1)}, u32[]{:S(2)}) copy-start(bf16[2,2,256,1024]{3,2,1,0:T(8,128)(2,1)} %get-tuple-element.154) | copy-start | bytes 6291460
  377.5 25.8 %collective-permute-start.6 = (bf16[2,256,1024]{2,1,0:T(8,128)(2,1)S(1)}, bf16[2,256,1024]{2,1,0:T(8,128)(2,1)S(1)}, u32[]{:S(2)}, u32[]{:S(2)}) collective-permute-start(bf16[2,256,1024]{2,1,0:T(8,128)(2,1)S(1)} %dynamic-slice_bitcast_fusion.3), channel_id=1, source_target_pairs={{0,16},{16,0},{1,17},{17,1},{2,18},{18,2},{3,19},{19,3},{4,20},{20... | collective-permute-start | bytes 3145736 | tf_op jit(solution)/shard_map/ppermute | solution.py:37
  402.7 13.2 %collective-permute-start.9 = (bf16[256,1024]{1,0:T(8,128)(2,1)S(1)}, bf16[256,1024]{1,0:T(8,128)(2,1)S(1)}, u32[]{:S(2)}, u32[]{:S(2)}) collective-permute-start(bf16[256,1024]{1,0:T(8,128)(2,1)S(1)} %dynamic-slice_bitcast_fusion.6), channel_id=1, source_target_pairs={{0,16},{16,0},{1,17},{17,1},{2,18},{18,2},{3,19},{19,3},{4,20},{20... | collective-permute-start | bytes 1572872 | tf_op jit(solution)/shard_map/ppermute | solution.py:37
  403.8 12.9 %collective-permute-start.7 = (bf16[256,1024]{1,0:T(8,128)(2,1)S(1)}, bf16[256,1024]{1,0:T(8,128)(2,1)S(1)}, u32[]{:S(2)}, u32[]{:S(2)}) collective-permute-start(bf16[256,1024]{1,0:T(8,128)(2,1)S(1)} %dynamic-slice_bitcast_fusion.7), channel_id=1, source_target_pairs={{0,8},{8,0},{1,9},{9,1},{2,10},{10,2},{3,11},{11,3},{4,12},{12,4},... | collective-permute-start | bytes 1572872 | tf_op jit(solution)/shard_map/ppermute | solution.py:37
  443.2 13.7 %collective-permute-start.12 = (bf16[256,1024]{1,0:T(8,128)(2,1)S(1)}, bf16[256,1024]{1,0:T(8,128)(2,1)S(1)}, u32[]{:S(2)}, u32[]{:S(2)}) collective-permute-start(bf16[256,1024]{1,0:T(8,128)(2,1)S(1)} %get-tuple-element.175), channel_id=1, source_target_pairs={{0,16},{16,0},{1,17},{17,1},{2,18},{18,2},{3,19},{19,3},{4,20},{20... | collective-permute-start | bytes 1572872 | tf_op jit(solution)/shard_map/ppermute | solution.py:37
  443.8 14.8 %collective-permute-start.10 = (bf16[256,1024]{1,0:T(8,128)(2,1)S(1)}, bf16[256,1024]{1,0:T(8,128)(2,1)S(1)}, u32[]{:S(2)}, u32[]{:S(2)}) collective-permute-start(bf16[256,1024]{1,0:T(8,128)(2,1)S(1)} %get-tuple-element.176), channel_id=1, source_target_pairs={{0,8},{8,0},{1,9},{9,1},{2,10},{10,2},{3,11},{11,3},{4,12},{12,4},... | collective-permute-start | bytes 1572872 | tf_op jit(solution)/shard_map/ppermute | solution.py:37
  458.0 24.3 %collective-permute-start.13 = (bf16[2,256,1024]{2,1,0:T(8,128)(2,1)}, bf16[2,256,1024]{2,1,0:T(8,128)(2,1)}, u32[]{:S(2)}, u32[]{:S(2)}) collective-permute-start(bf16[2,256,1024]{2,1,0:T(8,128)(2,1)} %get-tuple-element.178), channel_id=1, source_target_pairs={{0,8},{8,0},{1,9},{9,1},{2,10},{10,2},{3,11},{11,3},{4,12},{12,4},... | collective-permute-start | bytes 3145736 | tf_op jit(solution)/shard_map/ppermute | solution.py:37
  459.7 24.1 %collective-permute-start.11 = (bf16[2,256,1024]{2,1,0:T(8,128)(2,1)}, bf16[2,256,1024]{2,1,0:T(8,128)(2,1)}, u32[]{:S(2)}, u32[]{:S(2)}) collective-permute-start(bf16[2,256,1024]{2,1,0:T(8,128)(2,1)} %get-tuple-element.172), channel_id=1, source_target_pairs={{0,16},{16,0},{1,17},{17,1},{2,18},{18,2},{3,19},{19,3},{4,20},{20... | collective-permute-start | bytes 3145736 | tf_op jit(solution)/shard_map/ppermute | solution.py:37
  460.3 203.1 %reduce-scatter.4.cloned.1.call-start = ((), (), s32[]{:S(2)}) async-start(), calls=%async_computation.12 | async-start | bytes 5242880 | tf_op jit(solution)/shard_map/reduce_scatter | solution.py:399
  487.7 13.8 %collective-permute-start.14 = (bf16[1024,2048]{1,0:T(8,128)(2,1)}, bf16[1024,2048]{1,0:T(8,128)(2,1)}, u32[]{:S(2)}, u32[]{:S(2)}) collective-permute-start(bf16[1024,2048]{1,0:T(8,128)(2,1)} %bitcast.65), channel_id=1, source_target_pairs={{0,4},{4,0},{1,5},{5,1},{2,6},{6,2},{3,7},{7,3},{8,12},{12,8},{9,1... | collective-permute-start | bytes 12582920 | tf_op jit(solution)/shard_map/ppermute | solution.py:37
  554.9 52.2 %copy-start.48 = (bf16[1024,1024]{1,0:T(8,128)(2,1)}, bf16[1024,1024]{1,0:T(8,128)(2,1)S(1)}, u32[]{:S(2)}) copy-start(bf16[1024,1024]{1,0:T(8,128)(2,1)S(1)} %fusion.17) | copy-start | bytes 6291460
  587.8 7.5 collective-permute-start.15
  587.8 155.8 %reduce-scatter.6.cloned.1.call-start = ((), (), s32[]{:S(2)}) async-start(), calls=%async_computation.13 | async-start | bytes 5242880 | tf_op jit(solution)/shard_map/reduce_scatter | solution.py:399
  605.0 25.5 %collective-permute-start.16 = (bf16[2,256,1024]{2,1,0:T(8,128)(2,1)}, bf16[2,256,1024]{2,1,0:T(8,128)(2,1)}, u32[]{:S(2)}, u32[]{:S(2)}) collective-permute-start(bf16[2,256,1024]{2,1,0:T(8,128)(2,1)} %slice_bitcast_fusion.6), channel_id=1, source_target_pairs={{0,16},{16,0},{1,17},{17,1},{2,18},{18,2},{3,19},{19,3},{4,20},{20... | collective-permute-start | bytes 3145736 | tf_op jit(solution)/shard_map/ppermute | solution.py:37
  606.6 25.5 %collective-permute-start.18 = (bf16[2,256,1024]{2,1,0:T(8,128)(2,1)}, bf16[2,256,1024]{2,1,0:T(8,128)(2,1)}, u32[]{:S(2)}, u32[]{:S(2)}) collective-permute-start(bf16[2,256,1024]{2,1,0:T(8,128)(2,1)} %slice_bitcast_fusion.4), channel_id=1, source_target_pairs={{0,8},{8,0},{1,9},{9,1},{2,10},{10,2},{3,11},{11,3},{4,12},{12,4},... | collective-permute-start | bytes 3145736 | tf_op jit(solution)/shard_map/ppermute | solution.py:37
  635.4 13.1 %collective-permute-start.19 = (bf16[256,1024]{1,0:T(8,128)(2,1)S(1)}, bf16[256,1024]{1,0:T(8,128)(2,1)S(1)}, u32[]{:S(2)}, u32[]{:S(2)}) collective-permute-start(bf16[256,1024]{1,0:T(8,128)(2,1)S(1)} %slice_bitcast_fusion.12), channel_id=1, source_target_pairs={{0,16},{16,0},{1,17},{17,1},{2,18},{18,2},{3,19},{19,3},{4,20},{20... | collective-permute-start | bytes 1572872 | tf_op jit(solution)/shard_map/ppermute | solution.py:37
  636.7 12.6 %collective-permute-start.17 = (bf16[256,1024]{1,0:T(8,128)(2,1)S(1)}, bf16[256,1024]{1,0:T(8,128)(2,1)S(1)}, u32[]{:S(2)}, u32[]{:S(2)}) collective-permute-start(bf16[256,1024]{1,0:T(8,128)(2,1)S(1)} %slice_bitcast_fusion.14), channel_id=1, source_target_pairs={{0,8},{8,0},{1,9},{9,1},{2,10},{10,2},{3,11},{11,3},{4,12},{12,4},... | collective-permute-start | bytes 1572872 | tf_op jit(solution)/shard_map/ppermute | solution.py:37
  652.9 26.8 %copy-start.29 = (bf16[256,2048]{1,0:T(8,128)(2,1)}, bf16[256,2048]{1,0:T(8,128)(2,1)S(1)}, u32[]{:S(2)}) copy-start(bf16[256,2048]{1,0:T(8,128)(2,1)S(1)} %get-tuple-element.84) | copy-start | bytes 3145732
  664.5 14.0 %collective-permute-start.22 = (bf16[256,1024]{1,0:T(8,128)(2,1)}, bf16[256,1024]{1,0:T(8,128)(2,1)}, u32[]{:S(2)}, u32[]{:S(2)}) collective-permute-start(bf16[256,1024]{1,0:T(8,128)(2,1)} %get-tuple-element.167), channel_id=1, source_target_pairs={{0,16},{16,0},{1,17},{17,1},{2,18},{18,2},{3,19},{19,3},{4,20},{20... | collective-permute-start | bytes 1572872 | tf_op jit(solution)/shard_map/ppermute | solution.py:37
  665.0 15.3 %collective-permute-start.20 = (bf16[256,1024]{1,0:T(8,128)(2,1)}, bf16[256,1024]{1,0:T(8,128)(2,1)}, u32[]{:S(2)}, u32[]{:S(2)}) collective-permute-start(bf16[256,1024]{1,0:T(8,128)(2,1)} %get-tuple-element.168), channel_id=1, source_target_pairs={{0,8},{8,0},{1,9},{9,1},{2,10},{10,2},{3,11},{11,3},{4,12},{12,4},... | collective-permute-start | bytes 1572872 | tf_op jit(solution)/shard_map/ppermute | solution.py:37
  665.6 196.7 %reduce-scatter.8.cloned.1.call-start = ((), (), s32[]{:S(2)}) async-start(), calls=%async_computation.14 | async-start | bytes 5242880 | tf_op jit(solution)/shard_map/reduce_scatter | solution.py:399
  679.7 24.2 %collective-permute-start.23 = (bf16[2,256,1024]{2,1,0:T(8,128)(2,1)S(1)}, bf16[2,256,1024]{2,1,0:T(8,128)(2,1)S(1)}, u32[]{:S(2)}, u32[]{:S(2)}) collective-permute-start(bf16[2,256,1024]{2,1,0:T(8,128)(2,1)S(1)} %get-tuple-element.170), channel_id=1, source_target_pairs={{0,8},{8,0},{1,9},{9,1},{2,10},{10,2},{3,11},{11,3},{4,12},{12,4},... | collective-permute-start | bytes 3145736 | tf_op jit(solution)/shard_map/ppermute | solution.py:37
  681.5 23.8 %collective-permute-start.21 = (bf16[2,256,1024]{2,1,0:T(8,128)(2,1)S(1)}, bf16[2,256,1024]{2,1,0:T(8,128)(2,1)S(1)}, u32[]{:S(2)}, u32[]{:S(2)}) collective-permute-start(bf16[2,256,1024]{2,1,0:T(8,128)(2,1)S(1)} %get-tuple-element.164), channel_id=1, source_target_pairs={{0,16},{16,0},{1,17},{17,1},{2,18},{18,2},{3,19},{19,3},{4,20},{20... | collective-permute-start | bytes 3145736 | tf_op jit(solution)/shard_map/ppermute | solution.py:37
  706.7 7.2 collective-permute-start.24
  765.5 7.5 collective-permute-start.25
  780.5 26.3 %collective-permute-start.28 = (bf16[2,256,1024]{2,1,0:T(8,128)(2,1)}, bf16[2,256,1024]{2,1,0:T(8,128)(2,1)}, u32[]{:S(2)}, u32[]{:S(2)}) collective-permute-start(bf16[2,256,1024]{2,1,0:T(8,128)(2,1)} %dynamic-slice_bitcast_fusion), channel_id=1, source_target_pairs={{0,8},{8,0},{1,9},{9,1},{2,10},{10,2},{3,11},{11,3},{4,12},{12,4},... | collective-permute-start | bytes 3145736 | tf_op jit(solution)/shard_map/ppermute | solution.py:37
  781.1 31.8 %collective-permute-start.26 = (bf16[2,256,1024]{2,1,0:T(8,128)(2,1)S(1)}, bf16[2,256,1024]{2,1,0:T(8,128)(2,1)}, u32[]{:S(2)}, u32[]{:S(2)}) collective-permute-start(bf16[2,256,1024]{2,1,0:T(8,128)(2,1)S(1)} %dynamic-slice_bitcast_fusion.1), channel_id=1, source_target_pairs={{0,16},{16,0},{1,17},{17,1},{2,18},{18,2},{3,19},{19,3},{4,20},{20... | collective-permute-start | bytes 3145736 | tf_op jit(solution)/shard_map/ppermute | solution.py:37
  783.6 58.0 %all-to-all-start.2 = ((bf16[256,8,512]{2,1,0:T(8,128)(2,1)}), bf16[256,8,512]{2,1,0:T(8,128)(2,1)}, u32[]{:S(2)}, u32[]{:S(2)}) async-start(bf16[256,8,512]{2,1,0:T(8,128)(2,1)} %bitcast.147), calls=%async_computation.5 | async-start | bytes 4194304 | tf_op jit(solution)/shard_map/all_to_all | solution.py:358
  789.9 25.1 %copy-start.9 = (bf16[1024,2048]{1,0:T(8,128)(2,1)S(1)}, bf16[1024,2048]{1,0:T(8,128)(2,1)}, u32[]{:S(2)}) copy-start(bf16[1024,2048]{1,0:T(8,128)(2,1)} %copy-done.7) | copy-start | bytes 12582916
  789.9 25.1 %copy-start.45 = (bf16[1024,1024]{1,0:T(8,128)(2,1)S(1)}, bf16[1024,1024]{1,0:T(8,128)(2,1)}, u32[]{:S(2)}) copy-start(bf16[1024,1024]{1,0:T(8,128)(2,1)} %copy-done.44) | copy-start | bytes 6291460
  808.5 31.3 %collective-permute-start.29 = (bf16[256,1024]{1,0:T(8,128)(2,1)S(1)}, bf16[256,1024]{1,0:T(8,128)(2,1)S(1)}, u32[]{:S(2)}, u32[]{:S(2)}) collective-permute-start(bf16[256,1024]{1,0:T(8,128)(2,1)S(1)} %dynamic-slice_bitcast_fusion.4), channel_id=1, source_target_pairs={{0,16},{16,0},{1,17},{17,1},{2,18},{18,2},{3,19},{19,3},{4,20},{20... | collective-permute-start | bytes 1572872 | tf_op jit(solution)/shard_map/ppermute | solution.py:37
  814.9 25.0 %collective-permute-start.27 = (bf16[256,1024]{1,0:T(8,128)(2,1)S(1)}, bf16[256,1024]{1,0:T(8,128)(2,1)S(1)}, u32[]{:S(2)}, u32[]{:S(2)}) collective-permute-start(bf16[256,1024]{1,0:T(8,128)(2,1)S(1)} %dynamic-slice_bitcast_fusion.5), channel_id=1, source_target_pairs={{0,8},{8,0},{1,9},{9,1},{2,10},{10,2},{3,11},{11,3},{4,12},{12,4},... | collective-permute-start | bytes 1572872 | tf_op jit(solution)/shard_map/ppermute | solution.py:37
  844.7 17.7 %collective-permute-start.30 = (bf16[1024,2048]{1,0:T(8,128)(2,1)}, bf16[1024,2048]{1,0:T(8,128)(2,1)}, u32[]{:S(2)}, u32[]{:S(2)}) collective-permute-start(bf16[1024,2048]{1,0:T(8,128)(2,1)} %convolution_convert_fusion.2), channel_id=1, source_target_pairs={{0,4},{4,0},{1,5},{5,1},{2,6},{6,2},{3,7},{7,3},{8,12},{12,8},{9,1... | collective-permute-start | bytes 12582920 | tf_op jit(solution)/shard_map/ppermute | solution.py:37
  862.3 176.9 %copy-start.56 = (f32[768]{0:T(1024)}, f32[768]{0:T(1024)S(1)}, u32[]{:S(2)}) copy-start(f32[768]{0:T(1024)S(1)} %reduce_sum.272) | copy-start | bytes 9220
  892.8 81.2 %all-to-all-start.5 = ((bf16[384,8,512]{2,1,0:T(8,128)(2,1)}), bf16[384,8,512]{2,1,0:T(8,128)(2,1)S(1)}, u32[]{:S(2)}, u32[]{:S(2)}) async-start(bf16[384,8,512]{2,1,0:T(8,128)(2,1)} %copy.146), calls=%async_computation.8 | async-start | bytes 6291456 | tf_op jit(solution)/shard_map/all_to_all | solution.py:355
  905.3 43.9 %collective-permute-start.31 = (bf16[2,256,1024]{2,1,0:T(8,128)(2,1)}, bf16[2,256,1024]{2,1,0:T(8,128)(2,1)}, u32[]{:S(2)}, u32[]{:S(2)}) collective-permute-start(bf16[2,256,1024]{2,1,0:T(8,128)(2,1)} %slice_bitcast_fusion.2), channel_id=1, source_target_pairs={{0,16},{16,0},{1,17},{17,1},{2,18},{18,2},{3,19},{19,3},{4,20},{20... | collective-permute-start | bytes 3145736 | tf_op jit(solution)/shard_map/ppermute | solution.py:37
  907.5 44.3 %collective-permute-start.33 = (bf16[2,256,1024]{2,1,0:T(8,128)(2,1)}, bf16[2,256,1024]{2,1,0:T(8,128)(2,1)}, u32[]{:S(2)}, u32[]{:S(2)}) collective-permute-start(bf16[2,256,1024]{2,1,0:T(8,128)(2,1)} %slice_bitcast_fusion), channel_id=1, source_target_pairs={{0,8},{8,0},{1,9},{9,1},{2,10},{10,2},{3,11},{11,3},{4,12},{12,4},... | collective-permute-start | bytes 3145736 | tf_op jit(solution)/shard_map/ppermute | solution.py:37
  955.0 15.5 %collective-permute-start.34 = (bf16[256,1024]{1,0:T(8,128)(2,1)S(1)}, bf16[256,1024]{1,0:T(8,128)(2,1)S(1)}, u32[]{:S(2)}, u32[]{:S(2)}) collective-permute-start(bf16[256,1024]{1,0:T(8,128)(2,1)S(1)} %slice_bitcast_fusion.8), channel_id=1, source_target_pairs={{0,16},{16,0},{1,17},{17,1},{2,18},{18,2},{3,19},{19,3},{4,20},{20... | collective-permute-start | bytes 1572872 | tf_op jit(solution)/shard_map/ppermute | solution.py:37
  955.6 16.8 %collective-permute-start.32 = (bf16[256,1024]{1,0:T(8,128)(2,1)S(1)}, bf16[256,1024]{1,0:T(8,128)(2,1)S(1)}, u32[]{:S(2)}, u32[]{:S(2)}) collective-permute-start(bf16[256,1024]{1,0:T(8,128)(2,1)S(1)} %slice_bitcast_fusion.10), channel_id=1, source_target_pairs={{0,8},{8,0},{1,9},{9,1},{2,10},{10,2},{3,11},{11,3},{4,12},{12,4},... | collective-permute-start | bytes 1572872 | tf_op jit(solution)/shard_map/ppermute | solution.py:37
  978.2 15.6 %all-to-all-start.6 = ((f32[32,1,128]{2,1,0:T(1,128)}), f32[32,1,128]{2,1,0:T(1,128)S(1)}, u32[]{:S(2)}, u32[]{:S(2)}) async-start(f32[32,1,128]{2,1,0:T(1,128)} %broadcast_in_dim.123), calls=%async_computation.9 | async-start | bytes 32768 | tf_op jit(solution)/shard_map/all_to_all | solution.py:355
  994.5 62.6 %collective-permute-start.35 = (bf16[256,2048]{1,0:T(8,128)(2,1)}, bf16[256,2048]{1,0:T(8,128)(2,1)}, u32[]{:S(2)}, u32[]{:S(2)}) collective-permute-start(bf16[256,2048]{1,0:T(8,128)(2,1)} %fusion.53), channel_id=1, source_target_pairs={{1,8},{2,4},{3,12},{4,2},{5,10},{7,14},{8,1},{10,5},{11,13},{12,3}... | collective-permute-start | bytes 3145736 | tf_op jit(solution)/shard_map/ppermute | solution.py:55
  997.9 70.5 %collective-permute-start.36 = (bf16[256,2048]{1,0:T(8,128)(2,1)}, bf16[256,2048]{1,0:T(8,128)(2,1)}, u32[]{:S(2)}, u32[]{:S(2)}) collective-permute-start(bf16[256,2048]{1,0:T(8,128)(2,1)} %fusion.49), channel_id=1, source_target_pairs={{1,8},{2,4},{3,12},{4,2},{5,10},{7,14},{8,1},{10,5},{11,13},{12,3}... | collective-permute-start | bytes 3145736 | tf_op jit(solution)/shard_map/ppermute | solution.py:55
  1006.8 32.4 %copy-start.61 = (f32[768]{0:T(1024)S(1)}, f32[768]{0:T(1024)}, u32[]{:S(2)}) copy-start(f32[768]{0:T(1024)} %param.21) | copy-start | bytes 9220
  1006.8 32.4 %copy-start.68 = (f32[768]{0:T(1024)S(1)}, f32[768]{0:T(1024)}, u32[]{:S(2)}) copy-start(f32[768]{0:T(1024)} %param.22) | copy-start | bytes 9220
  1006.8 32.4 %copy-start.69 = (f32[768]{0:T(1024)S(1)}, f32[768]{0:T(1024)}, u32[]{:S(2)}) copy-start(f32[768]{0:T(1024)} %param.23) | copy-start | bytes 9220
  1006.8 50.3 %copy-start.37 = (bf16[256,2048]{1,0:T(8,128)(2,1)S(1)}, bf16[256,2048]{1,0:T(8,128)(2,1)}, u32[]{:S(2)}) copy-start(bf16[256,2048]{1,0:T(8,128)(2,1)} %fusion.53) | copy-start | bytes 3145732
  1006.8 61.5 %copy-start.42 = (bf16[256,2048]{1,0:T(8,128)(2,1)S(1)}, bf16[256,2048]{1,0:T(8,128)(2,1)}, u32[]{:S(2)}) copy-start(bf16[256,2048]{1,0:T(8,128)(2,1)} %fusion.49) | copy-start | bytes 3145732
  (67 other events, 478.2 us)
Sparse Core Ops, SparseCore 0:
  72.4 83.9 all-gather.8
  158.3 92.3 all-gather.10
  252.8 81.0 all-gather.12
  363.6 79.2 all-gather.14
  460.4 79.4 all-gather.16
  588.0 75.3 reduce-scatter.3
  666.4 77.2 reduce-scatter.5
  768.1 77.4 reduce-scatter.7

commit v3 on v2

--- a/solution.py
+++ b/solution.py
@@ -408,7 +408,6 @@
         x_low = swap_tokens(tokens.reshape(CH, D))
         dy = swap_tokens(out_grad.reshape(CH, D))
         x_all = group_gather(x_low).reshape(2, 2, 2, CH, D)
-        dy_all = group_gather(dy).reshape(2, 2, 2, CH, D)
         slots, own_ids = block_tables(owners, per_owner, rank)
         rest_order = jnp.concatenate(
             [
@@ -446,45 +445,46 @@
             [part.reshape(TP, 12, rows, BC), pieces[qkv_end:].reshape(TP, 36, rows, BC)], axis=1
         )
         part = grouped(part.reshape(-1, rows, BC)).reshape(TP, 48, rows, BC)
-        part, x_all = together(part, x_all)
-        w_first, part = together(data_gather(part[:, :16]), part)
-        w_qkv, w_out = w_first[:, :, :12], w_first[:, :, 12:]
-        w_up = data_gather(part[:, 16:32])
-        w_down = data_gather(part[:, 32:])
+        part, x_all, dy = together(part, x_all, dy)
+        w_qkv, part = together(data_gather(part[:, :12]), part)
+        w_out = data_gather(part[:, 12:16])
+        w_rest = data_gather(part[:, 16:])
         w_qkv = assemble_qkv(w_qkv)
         w_out = assemble(w_out, 1, 4, BC)
         x = x_low.astype(F32)
         unit_all, _ = norm_parts(x_all.reshape(2 * LEN, D).astype(F32))
         a_all = (unit_all * ln1_gain + ln1_shift).astype(BF16)
         a_all = a_all.reshape(2, 2, 2, CH, D).transpose(0, 2, 1, 3, 4).reshape(2 * LEN, D)
-        dy_all = to_relative(dy_all.transpose(0, 2, 1, 3, 4)).reshape(2, 4 * CH, D)
+        dy_all = gather_relative(dy)
         unit1, inverse1 = norm_parts(x)
 
-        a_all, dy_all = together(a_all, dy_all)
         qkv = (jnp.dot(a_all, w_qkv, preferred_element_type=F32) + qkv_bias).astype(BF16)
         mixed, lse, tops = attend(seg_col, seg_row, qkv)
+        mixed, *dy_all = together(mixed, *dy_all)
         h1 = x + scatter_chips(scatter_core(mixed, w_out, 0)) + out_bias
         unit2, inverse2 = norm_parts(h1)
-        c_own, w_up = together((unit2 * ln2_gain + ln2_shift).astype(BF16), w_up)
+        c_own = (unit2 * ln2_gain + ln2_shift).astype(BF16)
+        w_up, w_down = w_rest[:, :, :16], w_rest[:, :, 16:]
         w_up = assemble(w_up, 8, 2, BC)
         c_two = gather_relative(c_own)
 
         u_two = [jnp.dot(tokens_of, w_up, preferred_element_type=F32) + up_bias for tokens_of in c_two]
-        u_two[0], u_two[1], w_down = together(u_two[0], u_two[1], w_down)
-        w_down = assemble(w_down, 4, 4, BC)
-
-        def half(u, grads):
-            dg = contract(grads, w_down, 1, 1)
-            cdf = 0.5 * (1.0 + lax.erf(u * math.sqrt(0.5)))
-            slope = cdf + u * jnp.exp(-0.5 * u * u) * (1.0 / math.sqrt(2.0 * math.pi))
-            return (u * cdf).astype(BF16), (dg * slope).astype(BF16)
-
-        g_mine, du_mine = half(u_two[0], dy_all[0])
-        g_other, du_other = half(u_two[1], dy_all[1])
+        def activate(u):
+            return (u * (0.5 * (1.0 + lax.erf(u * math.sqrt(0.5))))).astype(BF16)
+
+        g_mine, g_other = activate(u_two[0]), activate(u_two[1])
         grad_down = contract(g_mine, dy_all[0], 0, 0) + contract(g_other, dy_all[1], 0, 0)
         grad_down = take_apart(grad_down, 4, 4, BC)
-        du_mine, du_other, grad_down = together(du_mine, du_other, grad_down)
+        u_two[0], u_two[1], w_down, grad_down = together(u_two[0], u_two[1], w_down, grad_down)
         got_down = data_scatter(grad_down)
+        w_down = assemble(w_down, 4, 4, BC)
+
+        def back(u, grads):
+            slope = 0.5 * (1.0 + lax.erf(u * math.sqrt(0.5)))
+            slope = slope + u * jnp.exp(-0.5 * u * u) * (1.0 / math.sqrt(2.0 * math.pi))
+            return (contract(grads, w_down, 1, 1) * slope).astype(BF16)
+
+        du_mine, du_other = back(u_two[0], dy_all[0]), back(u_two[1], dy_all[1])
         send = contract(du_other, w_up, 1, 1).astype(BF16)
         keep = contract(after(du_mine, send), w_up, 1, 1)
         dc_core = keep, trade(send, "c")
@@ -534,7 +534,7 @@
         terms = jnp.concatenate([terms, spread(du_sum, FF)])
         vector_grads = jnp.sum(everyone(terms.reshape(devices, vector_part)), axis=0)
 
-        got_first, branch, vector_grads, got_rest = together(got_first, branch, vector_grads, got_rest)
+        got_first, branch, got_rest = together(got_first, branch, got_rest)
         got_first = grouped(got_first.reshape(-1, rows, CH))
         got_first = got_first.reshape(TP, 32, rows, CH)
         got_qkv = got_first[:, :24].reshape(4, 2, 24, rows, CH).transpose(0, 2, 3, 1, 4).reshape(-1, rows, BC)

time: 1090 us -> 1040 us (0.954)
  blocking collectives: 91.9 us -> 0 us
  starting transfers between devices: 51.7 us -> 97.8 us
  waiting for transfers between devices: 521 us -> 502 us
    all_to_all x3 -> x0, blocking collectives: 91.9 us -> none  [the longest x2 80.2 us: grouped(): return lax.all_to_all(array, GROUP, 0, 0, tiled=True)]
    all_to_all x1 -> x3, waiting for transfers between devices: 0.01 us -> 47 us  [grouped(): return lax.all_to_all(array, GROUP, 0, 0, tiled=True)]
    all_gather x3, waiting for transfers between devices: 96.7 us -> 57.9 us  [data_gather(): return lax.all_gather(piece, DATA, axis=0)]
    all_to_all x3 -> x4, waiting for transfers between devices: 34 us -> 1.55 us  [everyone(): return lax.all_to_all(array, EVERY, 0, 0, tiled=True)]
    all_to_all x1 -> x3, starting transfers between devices: 6.31 us -> 35.2 us  [grouped(): return lax.all_to_all(array, GROUP, 0, 0, tiled=True)]
    ppermute x33 -> x38, waiting for transfers between devices: 267 us -> 278 us  [trade(): return lax.ppermute(array, axis, [(0, 1), (1, 0)])]
    all_to_all x3 -> x4, starting transfers between devices: 14.8 us -> 22.9 us  [everyone(): return lax.all_to_all(array, EVERY, 0, 0, tiled=True)]
    ppermute x33 -> x38, starting transfers between devices: 17.8 us -> 25.2 us  [trade(): return lax.ppermute(array, axis, [(0, 1), (1, 0)])]
  transfers between devices with their start and end apart: 49 -> 56, of which waited for: 36 -> 41; matrix products, arithmetic and copies ran while one was open for 19% -> 23% of each run, Pallas kernels for 4% -> 5%
where the time goes in v3:
time: 1040 us; the launch traced here: 1030 us
  waiting for transfers between devices  502 us (48%)
  matrix products  146 us (14%)
  local copies, waits for them, and re-layouts  107 us (10%)
  starting transfers between devices  97.8 us (9%)
  other arithmetic  97.8 us (9%)
  Pallas kernels  56.4 us (5%)
  between operations  23.4 us (2%)
    ppermute x38, waiting for transfers between devices, trade(): return lax.ppermute(array, axis, [(0, 1), (1, 0)])  278 us
    dot_general x19, matrix products, contract(): lax.dot_general(left, right, (((left_dim,), (right_dim,)), ((), ())), pre...  111 us
    ppermute x4, waiting for transfers between devices, swap_tokens(): lax.ppermute(array, ('i', 'c', 'h', 'l'), [pair for pair in pairs if pair...  101 us
    all_gather x3, waiting for transfers between devices, data_gather(): return lax.all_gather(piece, DATA, axis=0)  57.9 us
    all_to_all x3, waiting for transfers between devices, grouped(): return lax.all_to_all(array, GROUP, 0, 0, tiled=True)  47 us
    all_to_all x3, starting transfers between devices, grouped(): return lax.all_to_all(array, GROUP, 0, 0, tiled=True)  35.2 us
    pallas_call x1, Pallas kernels, update_blocks(): pl.pallas_call(update_kernel, name='update_blocks', grid=(count,), in_spe...  32.3 us
    unnamed x175, local copies, waits for them, and re-layouts  30 us
  transfers between devices with their start and end apart: 56, of which 41 were waited for; matrix products, arithmetic and copies ran while one was open for 23% of the time, Pallas kernels for 5%

profile of v3, /device:TPU:6, one launch (start us, length us, event | category | flops | bytes accessed | tf_op | source)
XLA Modules:
  0.0 1030.7 jit_solution(12536978999247337098)
XLA Ops:
  10.7 36.4 %collective-permute-done.3 = bf16[256,2048]{1,0:T(8,128)(2,1)S(1)} collective-permute-done((bf16[256,2048]{1,0:T(8,128)(2,1)}, bf16[256,2048]{1,0:T(8,128)(2,1)S(1)}, u32[]{:S(2)}, u32[]{:S(2)}) %collective-permute-start.3) | collective-permute-done | bytes 1048608 | tf_op jit(solution)/shard_map/ppermute | solution.py:55
  55.4 3.8 all-to-all-start
  63.7 30.0 %collective-permute-done.1 = s32[2,1,1024]{2,1,0:T(1,128)S(1)} collective-permute-done((s32[2,1,1024]{2,1,0:T(1,128)S(1)}, s32[2,1,1024]{2,1,0:T(1,128)S(1)}, u32[]{:S(2)}, u32[]{:S(2)}) %collective-permute-start.1) | collective-permute-done | bytes 8224 | tf_op jit(solution)/shard_map/ppermute | solution.py:37
  99.8 38.3 %collective-permute-done.4 = bf16[256,2048]{1,0:T(8,128)(2,1)} collective-permute-done((bf16[256,2048]{1,0:T(8,128)(2,1)}, bf16[256,2048]{1,0:T(8,128)(2,1)}, u32[]{:S(2)}, u32[]{:S(2)}) %collective-permute-start.4) | collective-permute-done | bytes 1048608 | tf_op jit(solution)/shard_map/ppermute | solution.py:55
  158.5 22.9 %all-to-all-start.1 = ((bf16[384,8,512]{2,1,0:T(8,128)(2,1)}), bf16[384,8,512]{2,1,0:T(8,128)(2,1)S(1)}, u32[]{:S(2)}, u32[]{:S(2)}) async-start(bf16[384,8,512]{2,1,0:T(8,128)(2,1)} %bitcast.424), calls=%async_computation.1 | async-start | bytes 6291456 | tf_op jit(solution)/shard_map/all_to_all | solution.py:358
  181.4 36.1 %all-to-all-done.1 = bf16[384,8,512]{2,1,0:T(8,128)(2,1)S(1)} async-done(((bf16[384,8,512]{2,1,0:T(8,128)(2,1)}), bf16[384,8,512]{2,1,0:T(8,128)(2,1)S(1)}, u32[]{:S(2)}, u32[]{:S(2)}) %all-to-all-start.1) | async-done | bytes 3145760 | tf_op jit(solution)/shard_map/all_to_all | solution.py:358
  223.6 7.0 reshape.711
  234.2 3.6 slice_reduce_fusion
  239.8 5.9 collective-permute-done.5
  248.1 4.6 convert_reduce_fusion
  252.7 13.7 %collective-permute-done.8 = bf16[2,256,1024]{2,1,0:T(8,128)(2,1)S(1)} collective-permute-done((bf16[2,256,1024]{2,1,0:T(8,128)(2,1)S(1)}, bf16[2,256,1024]{2,1,0:T(8,128)(2,1)S(1)}, u32[]{:S(2)}, u32[]{:S(2)}) %collective-permute-start.8) | collective-permute-done | bytes 1048608 | tf_op jit(solution)/shard_map/ppermute | solution.py:37
  276.7 5.3 fusion.5
  288.2 10.0 add_convert_fusion.6.q_ref.k_ref.v_ref
  298.3 9.4 attend.1
  310.1 5.9 all-gather.12.cloned.1.call-done
  322.1 6.0 collective-permute-done.10
  328.0 4.0 add_convert_fusion.5
  337.4 21.8 %collective-permute-done.13 = bf16[2,256,1024]{2,1,0:T(8,128)(2,1)} collective-permute-done((bf16[2,256,1024]{2,1,0:T(8,128)(2,1)S(1)}, bf16[2,256,1024]{2,1,0:T(8,128)(2,1)}, u32[]{:S(2)}, u32[]{:S(2)}) %collective-permute-start.13) | collective-permute-done | bytes 1048608 | tf_op jit(solution)/shard_map/ppermute | solution.py:37
  365.3 8.8 collective-permute-done.14
  381.3 10.0 collective-permute-done.17
  393.8 20.7 %collective-permute-done.18 = bf16[2,256,1024]{2,1,0:T(8,128)(2,1)S(1)} collective-permute-done((bf16[2,256,1024]{2,1,0:T(8,128)(2,1)S(1)}, bf16[2,256,1024]{2,1,0:T(8,128)(2,1)S(1)}, u32[]{:S(2)}, u32[]{:S(2)}) %collective-permute-start.18) | collective-permute-done | bytes 1048608 | tf_op jit(solution)/shard_map/ppermute | solution.py:37
  419.4 52.0 %all-gather.14.cloned.1.call-done = bf16[32,32,8,512]{3,2,1,0:T(8,128)(2,1)} async-done(((bf16[8,32,8,512]{3,2,1,0:T(8,128)(2,1)}), bf16[32,32,8,512]{3,2,1,0:T(8,128)(2,1)}) %all-gather.14.cloned.1.call-update) | async-done | bytes 8388624 | tf_op jit(solution)/shard_map/all_gather | solution.py:396
  471.5 5.1 fusion.116
  477.3 10.1 multiply_convert_fusion.1
  487.4 9.3 multiply_convert_fusion
  496.8 7.1 fusion.122
  503.9 7.0 add_convert_fusion.4
  519.3 7.9 fusion.17
  527.2 6.1 convolution_convert_fusion.3
  533.5 9.4 fusion.11
  542.9 7.1 add_convert_fusion.3
  553.3 6.5 fusion.123
  559.8 7.4 add_convert_fusion.2
  571.6 5.3 collective-permute-done.21
  583.4 11.1 %collective-permute-done.24 = bf16[256,1024]{1,0:T(8,128)(2,1)S(1)} collective-permute-done((bf16[256,1024]{1,0:T(8,128)(2,1)S(1)}, bf16[256,1024]{1,0:T(8,128)(2,1)S(1)}, u32[]{:S(2)}, u32[]{:S(2)}) %collective-permute-start.24) | collective-permute-done | bytes 524320 | tf_op jit(solution)/shard_map/ppermute | solution.py:37
  599.4 9.2 reduce-scatter.4.cloned.1.call-done
  610.9 12.5 %collective-permute-done.27 = bf16[256,1024]{1,0:T(8,128)(2,1)S(1)} collective-permute-done((bf16[256,1024]{1,0:T(8,128)(2,1)S(1)}, bf16[256,1024]{1,0:T(8,128)(2,1)S(1)}, u32[]{:S(2)}, u32[]{:S(2)}) %collective-permute-start.27) | collective-permute-done | bytes 524320 | tf_op jit(solution)/shard_map/ppermute | solution.py:37
  627.8 4.5 fusion.124
  633.6 16.0 %collective-permute-done.28 = bf16[2,256,1024]{2,1,0:T(8,128)(2,1)S(1)} collective-permute-done((bf16[2,256,1024]{2,1,0:T(8,128)(2,1)S(1)}, bf16[2,256,1024]{2,1,0:T(8,128)(2,1)S(1)}, u32[]{:S(2)}, u32[]{:S(2)}) %collective-permute-start.28) | collective-permute-done | bytes 1048608 | tf_op jit(solution)/shard_map/ppermute | solution.py:37
  654.4 3.9 convolution_convert_fusion.6
  668.1 12.7 %attend_back.1 = (bf16[2048,256]{1,0:T(8,128)(2,1)S(1)}, bf16[2048,256]{1,0:T(8,128)(2,1)S(1)}, bf16[2048,256]{1,0:T(8,128)(2,1)S(1)}) custom-call(s32[2,1024,1]{2,1,0:T(8,128)S(1)} %copy-done.7, s32[2,1,1024]{2,1,0:T(1,128)S(1)} %copy-done.21, bf16[2048,768]{1,0:T(8,128)(2,1)S(1)} %copy-done.1, bf16[2048,768]{1,0:T(8,128)(2,1)S(1)} %copy-done.1, ...), custom_call_target="tpu_custom_call" | custom-call | flops 5368709120 | bytes 8388608 | tf_op jit(solution)/shard_map/attend_back/pallas_call | solution.py:226
  681.0 7.8 reduce-scatter.6.cloned.1.call-done
  688.8 9.5 convolution_convert_fusion.4
  703.0 3.6 fusion.24
  709.1 5.0 convolution_convert_fusion.1
  716.5 5.1 collective-permute-done.30
  721.6 5.8 add_convert_fusion.1
  732.0 6.3 all-to-all-start.2
  738.3 16.9 %collective-permute-done.33 = bf16[2,256,1024]{2,1,0:T(8,128)(2,1)} collective-permute-done((bf16[2,256,1024]{2,1,0:T(8,128)(2,1)}, bf16[2,256,1024]{2,1,0:T(8,128)(2,1)}, u32[]{:S(2)}, u32[]{:S(2)}) %collective-permute-start.33) | collective-permute-done | bytes 1048608 | tf_op jit(solution)/shard_map/ppermute | solution.py:37
  757.5 3.8 collective-permute-done.31
  763.4 6.0 convolution_convert_fusion.2
  769.5 18.7 %collective-permute-done.34 = bf16[256,1024]{1,0:T(8,128)(2,1)S(1)} collective-permute-done((bf16[256,1024]{1,0:T(8,128)(2,1)S(1)}, bf16[256,1024]{1,0:T(8,128)(2,1)S(1)}, u32[]{:S(2)}, u32[]{:S(2)}) %collective-permute-start.34) | collective-permute-done | bytes 524320 | tf_op jit(solution)/shard_map/ppermute | solution.py:37
  798.6 6.1 all-to-all-start.3
  806.9 10.9 %all-to-all-done.3 = bf16[256,8,256]{2,1,0:T(8,128)(2,1)} async-done(((bf16[256,8,256]{2,1,0:T(8,128)(2,1)}), bf16[256,8,256]{2,1,0:T(8,128)(2,1)}, u32[]{:S(2)}, u32[]{:S(2)}) %all-to-all-start.3) | async-done | bytes 1048608 | tf_op jit(solution)/shard_map/all_to_all | solution.py:358
  817.8 5.9 all-to-all-start.5
  837.1 6.2 all-to-all-start.4
  843.6 6.1 add_convert_fusion
  854.6 39.8 %collective-permute-done.36 = bf16[2,256,1024]{2,1,0:T(8,128)(2,1)S(1)} collective-permute-done((bf16[2,256,1024]{2,1,0:T(8,128)(2,1)S(1)}, bf16[2,256,1024]{2,1,0:T(8,128)(2,1)S(1)}, u32[]{:S(2)}, u32[]{:S(2)}) %collective-permute-start.36) | collective-permute-done | bytes 1048608 | tf_op jit(solution)/shard_map/ppermute | solution.py:37
  907.0 11.1 %collective-permute-done.39 = bf16[256,1024]{1,0:T(8,128)(2,1)} collective-permute-done((bf16[256,1024]{1,0:T(8,128)(2,1)}, bf16[256,1024]{1,0:T(8,128)(2,1)}, u32[]{:S(2)}, u32[]{:S(2)}) %collective-permute-start.39) | collective-permute-done | bytes 524320 | tf_op jit(solution)/shard_map/ppermute | solution.py:37
  922.4 4.3 multiply_reduce_fusion
  928.6 7.0 all-to-all-start.6
  958.4 32.3 %update_blocks.1 = (f32[12,256,512]{2,1,0:T(8,128)}, f32[12,256,512]{2,1,0:T(8,128)}, f32[12,256,512]{2,1,0:T(8,128)}, bf16[12,256,512]{2,1,0:T(8,128)(2,1)}) custom-call(f32[1]{0:T(128)} %bitcast.184.clip_ref, f32[12,1,512]{2,1,0:T(1,128)S(1)} %and_select_fusion.scale_ref, f32[12,256,512]{2,1,0:T(8,128)S(1)} %bitcast.377, f32[12,256,512]{2,1,0:T(8,128)} %first_ref.1, ...), custom_call_target="tpu_custom_call" | custom-call | flops 14495514624 | bytes 72351744 | tf_op jit(solution)/shard_map/update_blocks/pallas_call | solution.py:326
  991.4 17.2 %collective-permute-done.40 = bf16[256,2048]{1,0:T(8,128)(2,1)} collective-permute-done((bf16[256,2048]{1,0:T(8,128)(2,1)}, bf16[256,2048]{1,0:T(8,128)(2,1)}, u32[]{:S(2)}, u32[]{:S(2)}) %collective-permute-start.40) | collective-permute-done | bytes 1048608 | tf_op jit(solution)/shard_map/ppermute | solution.py:55
  1011.0 8.9 collective-permute-done.41
  (465 shorter events, 248.6 us)
Async XLA Ops:
  7.2 42.5 %copy-start.64 = (f32[768]{0:T(1024)S(1)}, f32[768]{0:T(1024)}, u32[]{:S(2)}) copy-start(f32[768]{0:T(1024)} %param.21) | copy-start | bytes 9220
  7.2 210.3 %all-gather.8.cloned.1.call-start = ((), (), s32[]{:S(2)}) async-start(), calls=%async_computation.10 | async-start | bytes 9437184 | tf_op jit(solution)/shard_map/all_gather | solution.py:67
  7.2 39.9 %collective-permute-start.3 = (bf16[256,2048]{1,0:T(8,128)(2,1)}, bf16[256,2048]{1,0:T(8,128)(2,1)S(1)}, u32[]{:S(2)}, u32[]{:S(2)}) collective-permute-start(bf16[256,2048]{1,0:T(8,128)(2,1)} %bitcast.447), channel_id=1, source_target_pairs={{1,8},{2,4},{3,12},{4,2},{5,10},{7,14},{8,1},{10,5},{11,13},{12,3}... | collective-permute-start | bytes 3145736 | tf_op jit(solution)/shard_map/ppermute | solution.py:55
  55.4 89.3 %all-to-all-start = ((bf16[416,8,512]{2,1,0:T(8,128)(2,1)}), bf16[416,8,512]{2,1,0:T(8,128)(2,1)S(1)}, u32[]{:S(2)}, u32[]{:S(2)}) async-start(bf16[416,8,512]{2,1,0:T(8,128)(2,1)} %bitcast.420), calls=%async_computation | async-start | bytes 6815744 | tf_op jit(solution)/shard_map/all_to_all | solution.py:355
  59.2 3.9 collective-permute-start
  59.4 78.7 %collective-permute-start.4 = (bf16[256,2048]{1,0:T(8,128)(2,1)}, bf16[256,2048]{1,0:T(8,128)(2,1)}, u32[]{:S(2)}, u32[]{:S(2)}) collective-permute-start(bf16[256,2048]{1,0:T(8,128)(2,1)} %bitcast.448), channel_id=1, source_target_pairs={{1,8},{2,4},{3,12},{4,2},{5,10},{7,14},{8,1},{10,5},{11,13},{12,3}... | collective-permute-start | bytes 3145736 | tf_op jit(solution)/shard_map/ppermute | solution.py:55
  63.0 84.3 %copy-start.70 = (s32[384]{0:T(512)}, s32[384]{0:T(512)S(1)}, u32[]{:S(2)}) copy-start(s32[384]{0:T(512)S(1)} %multiply_add_fusion.1) | copy-start | bytes 4612
  63.1 30.6 %collective-permute-start.1 = (s32[2,1,1024]{2,1,0:T(1,128)S(1)}, s32[2,1,1024]{2,1,0:T(1,128)S(1)}, u32[]{:S(2)}, u32[]{:S(2)}) collective-permute-start(s32[2,1,1024]{2,1,0:T(1,128)S(1)} %pad_add_fusion), channel_id=1, source_target_pairs={{0,8},{8,0},{1,9},{9,1},{2,10},{10,2},{3,11},{11,3},{4,12},{12,4},... | collective-permute-start | bytes 24584 | tf_op jit(solution)/shard_map/ppermute | solution.py:37
  93.8 3.7 collective-permute-start.2
  158.5 59.0 %all-to-all-start.1 = ((bf16[384,8,512]{2,1,0:T(8,128)(2,1)}), bf16[384,8,512]{2,1,0:T(8,128)(2,1)S(1)}, u32[]{:S(2)}, u32[]{:S(2)}) async-start(bf16[384,8,512]{2,1,0:T(8,128)(2,1)} %bitcast.424), calls=%async_computation.1 | async-start | bytes 6291456 | tf_op jit(solution)/shard_map/all_to_all | solution.py:358
  181.4 100.6 %all-gather.10.cloned.1.call-start = ((), (), s32[]{:S(2)}) async-start(), calls=%async_computation.14 | async-start | bytes 3932160 | tf_op jit(solution)/shard_map/all_gather | solution.py:396
  218.6 97.4 %all-gather.12.cloned.1.call-start = ((), (), s32[]{:S(2)}) async-start(), calls=%async_computation.15 | async-start | bytes 1310720 | tf_op jit(solution)/shard_map/all_gather | solution.py:396
  219.8 78.5 %copy-start.6 = (s32[2,1024,1]{2,1,0:T(8,128)}, s32[2,1024,1]{2,1,0:T(8,128)S(1)}, u32[]{:S(2)}) copy-start(s32[2,1024,1]{2,1,0:T(8,128)S(1)} %copy.148.seg_col) | copy-start | bytes 24580
  222.7 15.3 %collective-permute-start.7 = (bf16[256,1024]{1,0:T(8,128)(2,1)}, bf16[256,1024]{1,0:T(8,128)(2,1)}, u32[]{:S(2)}, u32[]{:S(2)}) collective-permute-start(bf16[256,1024]{1,0:T(8,128)(2,1)} %get-tuple-element.178), channel_id=1, source_target_pairs={{0,16},{16,0},{1,17},{17,1},{2,18},{18,2},{3,19},{19,3},{4,20},{20... | collective-permute-start | bytes 1572872 | tf_op jit(solution)/shard_map/ppermute | solution.py:37
  223.6 74.7 %copy-start.20 = (s32[2,1,1024]{2,1,0:T(1,128)}, s32[2,1,1024]{2,1,0:T(1,128)S(1)}, u32[]{:S(2)}) copy-start(s32[2,1,1024]{2,1,0:T(1,128)S(1)} %pad_add_fusion.1.seg_row) | copy-start | bytes 24580
  230.6 15.2 %collective-permute-start.5 = (bf16[256,1024]{1,0:T(8,128)(2,1)}, bf16[256,1024]{1,0:T(8,128)(2,1)}, u32[]{:S(2)}, u32[]{:S(2)}) collective-permute-start(bf16[256,1024]{1,0:T(8,128)(2,1)} %get-tuple-element.179), channel_id=1, source_target_pairs={{0,8},{8,0},{1,9},{9,1},{2,10},{10,2},{3,11},{11,3},{4,12},{12,4},... | collective-permute-start | bytes 1572872 | tf_op jit(solution)/shard_map/ppermute | solution.py:37
  239.2 27.2 %collective-permute-start.8 = (bf16[2,256,1024]{2,1,0:T(8,128)(2,1)S(1)}, bf16[2,256,1024]{2,1,0:T(8,128)(2,1)S(1)}, u32[]{:S(2)}, u32[]{:S(2)}) collective-permute-start(bf16[2,256,1024]{2,1,0:T(8,128)(2,1)S(1)} %get-tuple-element.181), channel_id=1, source_target_pairs={{0,8},{8,0},{1,9},{9,1},{2,10},{10,2},{3,11},{11,3},{4,12},{12,4},... | collective-permute-start | bytes 3145736 | tf_op jit(solution)/shard_map/ppermute | solution.py:37
  246.9 22.0 %collective-permute-start.6 = (bf16[2,256,1024]{2,1,0:T(8,128)(2,1)S(1)}, bf16[2,256,1024]{2,1,0:T(8,128)(2,1)S(1)}, u32[]{:S(2)}, u32[]{:S(2)}) collective-permute-start(bf16[2,256,1024]{2,1,0:T(8,128)(2,1)S(1)} %get-tuple-element.175), channel_id=1, source_target_pairs={{0,16},{16,0},{1,17},{17,1},{2,18},{18,2},{3,19},{19,3},{4,20},{20... | collective-permute-start | bytes 3145736 | tf_op jit(solution)/shard_map/ppermute | solution.py:37
  271.7 37.3 %collective-permute-start.9 = (bf16[1024,2048]{1,0:T(8,128)(2,1)}, bf16[1024,2048]{1,0:T(8,128)(2,1)}, u32[]{:S(2)}, u32[]{:S(2)}) collective-permute-start(bf16[1024,2048]{1,0:T(8,128)(2,1)} %bitcast.41), channel_id=1, source_target_pairs={{0,4},{4,0},{1,5},{5,1},{2,6},{6,2},{3,7},{7,3},{8,12},{12,8},{9,1... | collective-permute-start | bytes 12582920 | tf_op jit(solution)/shard_map/ppermute | solution.py:37
  287.8 183.7 %all-gather.14.cloned.1.call-start = ((), (), s32[]{:S(2)}) async-start(), calls=%async_computation.16 | async-start | bytes 10485760 | tf_op jit(solution)/shard_map/all_gather | solution.py:396
  320.5 7.5 collective-permute-start.10
  322.0 286.6 %reduce-scatter.4.cloned.1.call-start = ((), (), s32[]{:S(2)}) async-start(), calls=%async_computation.11 | async-start | bytes 5242880 | tf_op jit(solution)/shard_map/reduce_scatter | solution.py:399
  333.9 25.4 %collective-permute-start.13 = (bf16[2,256,1024]{2,1,0:T(8,128)(2,1)S(1)}, bf16[2,256,1024]{2,1,0:T(8,128)(2,1)}, u32[]{:S(2)}, u32[]{:S(2)}) collective-permute-start(bf16[2,256,1024]{2,1,0:T(8,128)(2,1)S(1)} %dynamic-slice_bitcast_fusion.2), channel_id=1, source_target_pairs={{0,8},{8,0},{1,9},{9,1},{2,10},{10,2},{3,11},{11,3},{4,12},{12,4},... | collective-permute-start | bytes 3145736 | tf_op jit(solution)/shard_map/ppermute | solution.py:37
  336.8 25.2 %collective-permute-start.11 = (bf16[2,256,1024]{2,1,0:T(8,128)(2,1)}, bf16[2,256,1024]{2,1,0:T(8,128)(2,1)}, u32[]{:S(2)}, u32[]{:S(2)}) collective-permute-start(bf16[2,256,1024]{2,1,0:T(8,128)(2,1)} %dynamic-slice_bitcast_fusion.3), channel_id=1, source_target_pairs={{0,16},{16,0},{1,17},{17,1},{2,18},{18,2},{3,19},{19,3},{4,20},{20... | collective-permute-start | bytes 3145736 | tf_op jit(solution)/shard_map/ppermute | solution.py:37
  360.9 13.2 %collective-permute-start.14 = (bf16[256,1024]{1,0:T(8,128)(2,1)S(1)}, bf16[256,1024]{1,0:T(8,128)(2,1)S(1)}, u32[]{:S(2)}, u32[]{:S(2)}) collective-permute-start(bf16[256,1024]{1,0:T(8,128)(2,1)S(1)} %dynamic-slice_bitcast_fusion.6), channel_id=1, source_target_pairs={{0,16},{16,0},{1,17},{17,1},{2,18},{18,2},{3,19},{19,3},{4,20},{20... | collective-permute-start | bytes 1572872 | tf_op jit(solution)/shard_map/ppermute | solution.py:37
  363.8 12.9 %collective-permute-start.12 = (bf16[256,1024]{1,0:T(8,128)(2,1)S(1)}, bf16[256,1024]{1,0:T(8,128)(2,1)S(1)}, u32[]{:S(2)}, u32[]{:S(2)}) collective-permute-start(bf16[256,1024]{1,0:T(8,128)(2,1)S(1)} %dynamic-slice_bitcast_fusion.7), channel_id=1, source_target_pairs={{0,8},{8,0},{1,9},{9,1},{2,10},{10,2},{3,11},{11,3},{4,12},{12,4},... | collective-permute-start | bytes 1572872 | tf_op jit(solution)/shard_map/ppermute | solution.py:37
  378.1 218.8 %copy-start.25 = (f32[256,2048]{1,0:T(8,128)}, f32[256,2048]{1,0:T(8,128)S(1)}, u32[]{:S(2)}) copy-start(f32[256,2048]{1,0:T(8,128)S(1)} %get-tuple-element.139) | copy-start | bytes 6291460
  379.2 12.1 %collective-permute-start.17 = (bf16[256,1024]{1,0:T(8,128)(2,1)S(1)}, bf16[256,1024]{1,0:T(8,128)(2,1)S(1)}, u32[]{:S(2)}, u32[]{:S(2)}) collective-permute-start(bf16[256,1024]{1,0:T(8,128)(2,1)S(1)} %get-tuple-element.168), channel_id=1, source_target_pairs={{0,16},{16,0},{1,17},{17,1},{2,18},{18,2},{3,19},{19,3},{4,20},{20... | collective-permute-start | bytes 1572872 | tf_op jit(solution)/shard_map/ppermute | solution.py:37
  380.3 12.8 %collective-permute-start.15 = (bf16[256,1024]{1,0:T(8,128)(2,1)S(1)}, bf16[256,1024]{1,0:T(8,128)(2,1)S(1)}, u32[]{:S(2)}, u32[]{:S(2)}) collective-permute-start(bf16[256,1024]{1,0:T(8,128)(2,1)S(1)} %get-tuple-element.169), channel_id=1, source_target_pairs={{0,8},{8,0},{1,9},{9,1},{2,10},{10,2},{3,11},{11,3},{4,12},{12,4},... | collective-permute-start | bytes 1572872 | tf_op jit(solution)/shard_map/ppermute | solution.py:37
  391.4 23.1 %collective-permute-start.18 = (bf16[2,256,1024]{2,1,0:T(8,128)(2,1)S(1)}, bf16[2,256,1024]{2,1,0:T(8,128)(2,1)S(1)}, u32[]{:S(2)}, u32[]{:S(2)}) collective-permute-start(bf16[2,256,1024]{2,1,0:T(8,128)(2,1)S(1)} %get-tuple-element.171), channel_id=1, source_target_pairs={{0,8},{8,0},{1,9},{9,1},{2,10},{10,2},{3,11},{11,3},{4,12},{12,4},... | collective-permute-start | bytes 3145736 | tf_op jit(solution)/shard_map/ppermute | solution.py:37
  393.2 22.3 %collective-permute-start.16 = (bf16[2,256,1024]{2,1,0:T(8,128)(2,1)S(1)}, bf16[2,256,1024]{2,1,0:T(8,128)(2,1)S(1)}, u32[]{:S(2)}, u32[]{:S(2)}) collective-permute-start(bf16[2,256,1024]{2,1,0:T(8,128)(2,1)S(1)} %get-tuple-element.165), channel_id=1, source_target_pairs={{0,16},{16,0},{1,17},{17,1},{2,18},{18,2},{3,19},{19,3},{4,20},{20... | collective-permute-start | bytes 3145736 | tf_op jit(solution)/shard_map/ppermute | solution.py:37
  418.3 69.1 %collective-permute-start.19 = (bf16[1024,2048]{1,0:T(8,128)(2,1)}, bf16[1024,2048]{1,0:T(8,128)(2,1)}, u32[]{:S(2)}, u32[]{:S(2)}) collective-permute-start(bf16[1024,2048]{1,0:T(8,128)(2,1)} %bitcast.65), channel_id=1, source_target_pairs={{0,4},{4,0},{1,5},{5,1},{2,6},{6,2},{3,7},{7,3},{8,12},{12,8},{9,1... | collective-permute-start | bytes 12582920 | tf_op jit(solution)/shard_map/ppermute | solution.py:37
  533.3 9.6 collective-permute-start.20
  533.4 155.4 %reduce-scatter.6.cloned.1.call-start = ((), (), s32[]{:S(2)}) async-start(), calls=%async_computation.12 | async-start | bytes 5242880 | tf_op jit(solution)/shard_map/reduce_scatter | solution.py:399
  551.1 25.7 %collective-permute-start.21 = (bf16[2,256,1024]{2,1,0:T(8,128)(2,1)}, bf16[2,256,1024]{2,1,0:T(8,128)(2,1)S(1)}, u32[]{:S(2)}, u32[]{:S(2)}) collective-permute-start(bf16[2,256,1024]{2,1,0:T(8,128)(2,1)} %slice_bitcast_fusion.6), channel_id=1, source_target_pairs={{0,16},{16,0},{1,17},{17,1},{2,18},{18,2},{3,19},{19,3},{4,20},{20... | collective-permute-start | bytes 3145736 | tf_op jit(solution)/shard_map/ppermute | solution.py:37
  552.7 25.6 %collective-permute-start.23 = (bf16[2,256,1024]{2,1,0:T(8,128)(2,1)}, bf16[2,256,1024]{2,1,0:T(8,128)(2,1)}, u32[]{:S(2)}, u32[]{:S(2)}) collective-permute-start(bf16[2,256,1024]{2,1,0:T(8,128)(2,1)} %slice_bitcast_fusion.4), channel_id=1, source_target_pairs={{0,8},{8,0},{1,9},{9,1},{2,10},{10,2},{3,11},{11,3},{4,12},{12,4},... | collective-permute-start | bytes 3145736 | tf_op jit(solution)/shard_map/ppermute | solution.py:37
  581.2 13.3 %collective-permute-start.24 = (bf16[256,1024]{1,0:T(8,128)(2,1)S(1)}, bf16[256,1024]{1,0:T(8,128)(2,1)S(1)}, u32[]{:S(2)}, u32[]{:S(2)}) collective-permute-start(bf16[256,1024]{1,0:T(8,128)(2,1)S(1)} %slice_bitcast_fusion.12), channel_id=1, source_target_pairs={{0,16},{16,0},{1,17},{17,1},{2,18},{18,2},{3,19},{19,3},{4,20},{20... | collective-permute-start | bytes 1572872 | tf_op jit(solution)/shard_map/ppermute | solution.py:37
  582.8 13.0 %collective-permute-start.22 = (bf16[256,1024]{1,0:T(8,128)(2,1)S(1)}, bf16[256,1024]{1,0:T(8,128)(2,1)S(1)}, u32[]{:S(2)}, u32[]{:S(2)}) collective-permute-start(bf16[256,1024]{1,0:T(8,128)(2,1)S(1)} %slice_bitcast_fusion.14), channel_id=1, source_target_pairs={{0,8},{8,0},{1,9},{9,1},{2,10},{10,2},{3,11},{11,3},{4,12},{12,4},... | collective-permute-start | bytes 1572872 | tf_op jit(solution)/shard_map/ppermute | solution.py:37
  609.7 13.7 %collective-permute-start.27 = (bf16[256,1024]{1,0:T(8,128)(2,1)S(1)}, bf16[256,1024]{1,0:T(8,128)(2,1)S(1)}, u32[]{:S(2)}, u32[]{:S(2)}) collective-permute-start(bf16[256,1024]{1,0:T(8,128)(2,1)S(1)} %get-tuple-element.160), channel_id=1, source_target_pairs={{0,16},{16,0},{1,17},{17,1},{2,18},{18,2},{3,19},{19,3},{4,20},{20... | collective-permute-start | bytes 1572872 | tf_op jit(solution)/shard_map/ppermute | solution.py:37
  610.3 15.8 %collective-permute-start.25 = (bf16[256,1024]{1,0:T(8,128)(2,1)}, bf16[256,1024]{1,0:T(8,128)(2,1)}, u32[]{:S(2)}, u32[]{:S(2)}) collective-permute-start(bf16[256,1024]{1,0:T(8,128)(2,1)} %get-tuple-element.161), channel_id=1, source_target_pairs={{0,8},{8,0},{1,9},{9,1},{2,10},{10,2},{3,11},{11,3},{4,12},{12,4},... | collective-permute-start | bytes 1572872 | tf_op jit(solution)/shard_map/ppermute | solution.py:37
  610.9 184.6 %reduce-scatter.8.cloned.1.call-start = ((), (), s32[]{:S(2)}) async-start(), calls=%async_computation.13 | async-start | bytes 5242880 | tf_op jit(solution)/shard_map/reduce_scatter | solution.py:399
  625.4 24.2 %collective-permute-start.28 = (bf16[2,256,1024]{2,1,0:T(8,128)(2,1)S(1)}, bf16[2,256,1024]{2,1,0:T(8,128)(2,1)S(1)}, u32[]{:S(2)}, u32[]{:S(2)}) collective-permute-start(bf16[2,256,1024]{2,1,0:T(8,128)(2,1)S(1)} %get-tuple-element.163), channel_id=1, source_target_pairs={{0,8},{8,0},{1,9},{9,1},{2,10},{10,2},{3,11},{11,3},{4,12},{12,4},... | collective-permute-start | bytes 3145736 | tf_op jit(solution)/shard_map/ppermute | solution.py:37
  627.2 24.0 %collective-permute-start.26 = (bf16[2,256,1024]{2,1,0:T(8,128)(2,1)S(1)}, bf16[2,256,1024]{2,1,0:T(8,128)(2,1)S(1)}, u32[]{:S(2)}, u32[]{:S(2)}) collective-permute-start(bf16[2,256,1024]{2,1,0:T(8,128)(2,1)S(1)} %get-tuple-element.157), channel_id=1, source_target_pairs={{0,16},{16,0},{1,17},{17,1},{2,18},{18,2},{3,19},{19,3},{4,20},{20... | collective-permute-start | bytes 3145736 | tf_op jit(solution)/shard_map/ppermute | solution.py:37
  654.1 7.5 collective-permute-start.29
  714.1 7.5 collective-permute-start.30
  728.9 26.3 %collective-permute-start.33 = (bf16[2,256,1024]{2,1,0:T(8,128)(2,1)}, bf16[2,256,1024]{2,1,0:T(8,128)(2,1)}, u32[]{:S(2)}, u32[]{:S(2)}) collective-permute-start(bf16[2,256,1024]{2,1,0:T(8,128)(2,1)} %dynamic-slice_bitcast_fusion), channel_id=1, source_target_pairs={{0,8},{8,0},{1,9},{9,1},{2,10},{10,2},{3,11},{11,3},{4,12},{12,4},... | collective-permute-start | bytes 3145736 | tf_op jit(solution)/shard_map/ppermute | solution.py:37
  729.5 31.8 %collective-permute-start.31 = (bf16[2,256,1024]{2,1,0:T(8,128)(2,1)S(1)}, bf16[2,256,1024]{2,1,0:T(8,128)(2,1)}, u32[]{:S(2)}, u32[]{:S(2)}) collective-permute-start(bf16[2,256,1024]{2,1,0:T(8,128)(2,1)S(1)} %dynamic-slice_bitcast_fusion.1), channel_id=1, source_target_pairs={{0,16},{16,0},{1,17},{17,1},{2,18},{18,2},{3,19},{19,3},{4,20},{20... | collective-permute-start | bytes 3145736 | tf_op jit(solution)/shard_map/ppermute | solution.py:37
  732.0 56.7 %all-to-all-start.2 = ((bf16[256,8,512]{2,1,0:T(8,128)(2,1)}), bf16[256,8,512]{2,1,0:T(8,128)(2,1)}, u32[]{:S(2)}, u32[]{:S(2)}) async-start(bf16[256,8,512]{2,1,0:T(8,128)(2,1)} %bitcast.146), calls=%async_computation.5 | async-start | bytes 4194304 | tf_op jit(solution)/shard_map/all_to_all | solution.py:358
  756.9 31.3 %collective-permute-start.34 = (bf16[256,1024]{1,0:T(8,128)(2,1)S(1)}, bf16[256,1024]{1,0:T(8,128)(2,1)S(1)}, u32[]{:S(2)}, u32[]{:S(2)}) collective-permute-start(bf16[256,1024]{1,0:T(8,128)(2,1)S(1)} %dynamic-slice_bitcast_fusion.4), channel_id=1, source_target_pairs={{0,16},{16,0},{1,17},{17,1},{2,18},{18,2},{3,19},{19,3},{4,20},{20... | collective-permute-start | bytes 1572872 | tf_op jit(solution)/shard_map/ppermute | solution.py:37
  763.3 25.0 %collective-permute-start.32 = (bf16[256,1024]{1,0:T(8,128)(2,1)S(1)}, bf16[256,1024]{1,0:T(8,128)(2,1)S(1)}, u32[]{:S(2)}, u32[]{:S(2)}) collective-permute-start(bf16[256,1024]{1,0:T(8,128)(2,1)S(1)} %dynamic-slice_bitcast_fusion.5), channel_id=1, source_target_pairs={{0,8},{8,0},{1,9},{9,1},{2,10},{10,2},{3,11},{11,3},{4,12},{12,4},... | collective-permute-start | bytes 1572872 | tf_op jit(solution)/shard_map/ppermute | solution.py:37
  791.0 7.6 collective-permute-start.35
  798.6 19.2 %all-to-all-start.3 = ((bf16[256,8,256]{2,1,0:T(8,128)(2,1)}), bf16[256,8,256]{2,1,0:T(8,128)(2,1)}, u32[]{:S(2)}, u32[]{:S(2)}) async-start(bf16[256,8,256]{2,1,0:T(8,128)(2,1)} %bitcast.449), calls=%async_computation.6 | async-start | bytes 2097152 | tf_op jit(solution)/shard_map/all_to_all | solution.py:358
  817.8 19.3 %all-to-all-start.5 = ((f32[32,1,768]{2,1,0:T(1,128)}), f32[32,1,768]{2,1,0:T(1,128)S(1)}, u32[]{:S(2)}, u32[]{:S(2)}) async-start(f32[32,1,768]{2,1,0:T(1,128)} %bitcast.165), calls=%async_computation.8 | async-start | bytes 196608 | tf_op jit(solution)/shard_map/all_to_all | solution.py:355
  837.1 85.3 %all-to-all-start.4 = ((bf16[384,8,512]{2,1,0:T(8,128)(2,1)}), bf16[384,8,512]{2,1,0:T(8,128)(2,1)}, u32[]{:S(2)}, u32[]{:S(2)}) async-start(bf16[384,8,512]{2,1,0:T(8,128)(2,1)} %copy.153), calls=%async_computation.7 | async-start | bytes 6291456 | tf_op jit(solution)/shard_map/all_to_all | solution.py:355
  849.7 44.7 %collective-permute-start.36 = (bf16[2,256,1024]{2,1,0:T(8,128)(2,1)S(1)}, bf16[2,256,1024]{2,1,0:T(8,128)(2,1)S(1)}, u32[]{:S(2)}, u32[]{:S(2)}) collective-permute-start(bf16[2,256,1024]{2,1,0:T(8,128)(2,1)S(1)} %slice_bitcast_fusion.2), channel_id=1, source_target_pairs={{0,16},{16,0},{1,17},{17,1},{2,18},{18,2},{3,19},{19,3},{4,20},{20... | collective-permute-start | bytes 3145736 | tf_op jit(solution)/shard_map/ppermute | solution.py:37
  851.7 45.5 %collective-permute-start.38 = (bf16[2,256,1024]{2,1,0:T(8,128)(2,1)S(1)}, bf16[2,256,1024]{2,1,0:T(8,128)(2,1)}, u32[]{:S(2)}, u32[]{:S(2)}) collective-permute-start(bf16[2,256,1024]{2,1,0:T(8,128)(2,1)S(1)} %slice_bitcast_fusion), channel_id=1, source_target_pairs={{0,8},{8,0},{1,9},{9,1},{2,10},{10,2},{3,11},{11,3},{4,12},{12,4},... | collective-permute-start | bytes 3145736 | tf_op jit(solution)/shard_map/ppermute | solution.py:37
  902.2 16.0 %collective-permute-start.39 = (bf16[256,1024]{1,0:T(8,128)(2,1)}, bf16[256,1024]{1,0:T(8,128)(2,1)}, u32[]{:S(2)}, u32[]{:S(2)}) collective-permute-start(bf16[256,1024]{1,0:T(8,128)(2,1)} %slice_bitcast_fusion.8), channel_id=1, source_target_pairs={{0,16},{16,0},{1,17},{17,1},{2,18},{18,2},{3,19},{19,3},{4,20},{20... | collective-permute-start | bytes 1572872 | tf_op jit(solution)/shard_map/ppermute | solution.py:37
  903.6 16.1 %collective-permute-start.37 = (bf16[256,1024]{1,0:T(8,128)(2,1)}, bf16[256,1024]{1,0:T(8,128)(2,1)}, u32[]{:S(2)}, u32[]{:S(2)}) collective-permute-start(bf16[256,1024]{1,0:T(8,128)(2,1)} %slice_bitcast_fusion.10), channel_id=1, source_target_pairs={{0,8},{8,0},{1,9},{9,1},{2,10},{10,2},{3,11},{11,3},{4,12},{12,4},... | collective-permute-start | bytes 1572872 | tf_op jit(solution)/shard_map/ppermute | solution.py:37
  906.4 84.4 %copy-start.61 = (f32[768]{0:T(1024)}, f32[768]{0:T(1024)S(1)}, u32[]{:S(2)}) copy-start(f32[768]{0:T(1024)S(1)} %reduce_sum.273) | copy-start | bytes 9220
  928.6 16.7 %all-to-all-start.6 = ((f32[32,1,128]{2,1,0:T(1,128)}), f32[32,1,128]{2,1,0:T(1,128)S(1)}, u32[]{:S(2)}, u32[]{:S(2)}) async-start(f32[32,1,128]{2,1,0:T(1,128)} %broadcast_in_dim.123), calls=%async_computation.9 | async-start | bytes 32768 | tf_op jit(solution)/shard_map/all_to_all | solution.py:355
  946.0 62.6 %collective-permute-start.40 = (bf16[256,2048]{1,0:T(8,128)(2,1)}, bf16[256,2048]{1,0:T(8,128)(2,1)}, u32[]{:S(2)}, u32[]{:S(2)}) collective-permute-start(bf16[256,2048]{1,0:T(8,128)(2,1)} %fusion.39), channel_id=1, source_target_pairs={{1,8},{2,4},{3,12},{4,2},{5,10},{7,14},{8,1},{10,5},{11,13},{12,3}... | collective-permute-start | bytes 3145736 | tf_op jit(solution)/shard_map/ppermute | solution.py:55
  949.4 70.5 %collective-permute-start.41 = (bf16[256,2048]{1,0:T(8,128)(2,1)}, bf16[256,2048]{1,0:T(8,128)(2,1)}, u32[]{:S(2)}, u32[]{:S(2)}) collective-permute-start(bf16[256,2048]{1,0:T(8,128)(2,1)} %fusion.35), channel_id=1, source_target_pairs={{1,8},{2,4},{3,12},{4,2},{5,10},{7,14},{8,1},{10,5},{11,13},{12,3}... | collective-permute-start | bytes 3145736 | tf_op jit(solution)/shard_map/ppermute | solution.py:55
  958.4 50.3 %copy-start.47 = (bf16[256,2048]{1,0:T(8,128)(2,1)S(1)}, bf16[256,2048]{1,0:T(8,128)(2,1)}, u32[]{:S(2)}) copy-start(bf16[256,2048]{1,0:T(8,128)(2,1)} %fusion.39) | copy-start | bytes 3145732
  958.4 61.5 %copy-start.48 = (bf16[256,2048]{1,0:T(8,128)(2,1)S(1)}, bf16[256,2048]{1,0:T(8,128)(2,1)}, u32[]{:S(2)}) copy-start(bf16[256,2048]{1,0:T(8,128)(2,1)} %fusion.35) | copy-start | bytes 3145732
  (77 other events, 725.0 us)
Sparse Core Ops, SparseCore 0:
  49.8 106.6 all-gather.7
  218.7 62.1 all-gather.9
  287.9 28.0 all-gather.11
  322.1 149.2 all-gather.13
  533.5 75.0 reduce-scatter.3
  611.5 77.2 reduce-scatter.5
  716.6 77.3 reduce-scatter.7

commit v4 on v3

--- a/solution.py
+++ b/solution.py
@@ -446,8 +446,8 @@
         )
         part = grouped(part.reshape(-1, rows, BC)).reshape(TP, 48, rows, BC)
         part, x_all, dy = together(part, x_all, dy)
-        w_qkv, part = together(data_gather(part[:, :12]), part)
-        w_out = data_gather(part[:, 12:16])
+        w_first, part = together(data_gather(part[:, :16]), part)
+        w_qkv, w_out = w_first[:, :, :12], w_first[:, :, 12:]
         w_rest = data_gather(part[:, 16:])
         w_qkv = assemble_qkv(w_qkv)
         w_out = assemble(w_out, 1, 4, BC)
@@ -466,7 +466,7 @@
         c_own = (unit2 * ln2_gain + ln2_shift).astype(BF16)
         w_up, w_down = w_rest[:, :, :16], w_rest[:, :, 16:]
         w_up = assemble(w_up, 8, 2, BC)
-        c_two = gather_relative(c_own)
+        c_two = gather_relative(c_own, w_rest)
 
         u_two = [jnp.dot(tokens_of, w_up, preferred_element_type=F32) + up_bias for tokens_of in c_two]
         def activate(u):

time: 1040 us -> 1030 us (level)
  blocking collectives: 0 us -> 58.2 us
  waiting for transfers between devices: 502 us -> 453 us
  starting transfers between devices: 97.8 us -> 74.5 us
    all_to_all x0 -> x1, blocking collectives: none -> 58.2 us  [grouped(): return lax.all_to_all(array, GROUP, 0, 0, tiled=True)]
    all_to_all x3 -> x2, waiting for transfers between devices: 47 us -> 10.9 us  [grouped(): return lax.all_to_all(array, GROUP, 0, 0, tiled=True)]
    all_to_all x3 -> x2, starting transfers between devices: 35.2 us -> 12.3 us  [grouped(): return lax.all_to_all(array, GROUP, 0, 0, tiled=True)]
    ppermute x38, waiting for transfers between devices: 278 us -> 258 us  [trade(): return lax.ppermute(array, axis, [(0, 1), (1, 0)])]
    all_gather x3 -> x2, waiting for transfers between devices: 57.9 us -> 63.5 us  [data_gather(): return lax.all_gather(piece, DATA, axis=0)]
    unnamed x175 -> x173, local copies, waits for them, and re-layouts: 30 us -> 25.3 us
  transfers between devices with their start and end apart: 56 -> 54, of which waited for: 41 -> 38; matrix products, arithmetic and copies ran while one was open for 23% -> 24% of each run, Pallas kernels for 5% -> 6%
where the time goes in v4:
time: 1030 us; the launch traced here: 1020 us
  waiting for transfers between devices  453 us (44%)
  matrix products  146 us (14%)
  local copies, waits for them, and re-layouts  106 us (10%)
  other arithmetic  101 us (10%)
  starting transfers between devices  74.5 us (7%)
  blocking collectives  58.2 us (6%)
  Pallas kernels  56.8 us (6%)
  between operations  24.2 us (2%)
    ppermute x38, waiting for transfers between devices, trade(): return lax.ppermute(array, axis, [(0, 1), (1, 0)])  258 us
    dot_general x19, matrix products, contract(): lax.dot_general(left, right, (((left_dim,), (right_dim,)), ((), ())), pre...  111 us
    ppermute x4, waiting for transfers between devices, swap_tokens(): lax.ppermute(array, ('i', 'c', 'h', 'l'), [pair for pair in pairs if pair...  101 us
    all_gather x2, waiting for transfers between devices, data_gather(): return lax.all_gather(piece, DATA, axis=0)  63.5 us
    all_to_all x1, blocking collectives, grouped(): return lax.all_to_all(array, GROUP, 0, 0, tiled=True)  58.2 us
    pallas_call x1, Pallas kernels, update_blocks(): pl.pallas_call(update_kernel, name='update_blocks', grid=(count,), in_spe...  32.3 us
    unnamed x173, local copies, waits for them, and re-layouts  25.3 us
    ppermute x38, starting transfers between devices, trade(): return lax.ppermute(array, axis, [(0, 1), (1, 0)])  25.3 us
  transfers between devices with their start and end apart: 54, of which 38 were waited for; matrix products, arithmetic and copies ran while one was open for 24% of the time, Pallas kernels for 6%

profile of v4, /device:TPU:6, one launch (start us, length us, event | category | flops | bytes accessed | tf_op | source)
XLA Modules:
  0.0 1019.3 jit_solution(17523243261122793257)
XLA Ops:
  7.2 3.5 collective-permute-start.3
  10.7 36.4 %collective-permute-done.3 = bf16[256,2048]{1,0:T(8,128)(2,1)S(1)} collective-permute-done((bf16[256,2048]{1,0:T(8,128)(2,1)}, bf16[256,2048]{1,0:T(8,128)(2,1)S(1)}, u32[]{:S(2)}, u32[]{:S(2)}) %collective-permute-start.3) | collective-permute-done | bytes 1048608 | tf_op jit(solution)/shard_map/ppermute | solution.py:55
  55.4 3.8 all-to-all-start
  63.8 29.9 %collective-permute-done.1 = s32[2,1,1024]{2,1,0:T(1,128)S(1)} collective-permute-done((s32[2,1,1024]{2,1,0:T(1,128)S(1)}, s32[2,1,1024]{2,1,0:T(1,128)S(1)}, u32[]{:S(2)}, u32[]{:S(2)}) %collective-permute-start.1) | collective-permute-done | bytes 8224 | tf_op jit(solution)/shard_map/ppermute | solution.py:37
  99.8 38.3 %collective-permute-done.4 = bf16[256,2048]{1,0:T(8,128)(2,1)} collective-permute-done((bf16[256,2048]{1,0:T(8,128)(2,1)}, bf16[256,2048]{1,0:T(8,128)(2,1)}, u32[]{:S(2)}, u32[]{:S(2)}) %collective-permute-start.4) | collective-permute-done | bytes 1048608 | tf_op jit(solution)/shard_map/ppermute | solution.py:55
  156.9 58.2 %all_to_all.39 = bf16[384,8,512]{2,1,0:T(8,128)(2,1)S(1)} all-to-all(bf16[384,8,512]{2,1,0:T(8,128)(2,1)S(1)} %bitcast.426), channel_id=1, replica_groups=mesh['p'=1,'q'=2,'i'=2,'c'=2,'h'=2,'l'=2] {'q','i','c'}, dimensions={0} | all-to-all | bytes 6291456 | tf_op jit(solution)/shard_map/all_to_all | solution.py:358
  221.7 7.1 reshape.715
  232.4 3.6 slice_reduce_fusion
  238.1 5.9 collective-permute-done.5
  245.8 4.6 convert_reduce_fusion
  250.5 14.5 %collective-permute-done.8 = bf16[2,256,1024]{2,1,0:T(8,128)(2,1)S(1)} collective-permute-done((bf16[2,256,1024]{2,1,0:T(8,128)(2,1)S(1)}, bf16[2,256,1024]{2,1,0:T(8,128)(2,1)S(1)}, u32[]{:S(2)}, u32[]{:S(2)}) %collective-permute-start.8) | collective-permute-done | bytes 1048608 | tf_op jit(solution)/shard_map/ppermute | solution.py:37
  275.5 5.3 fusion.5
  280.8 15.6 %all-gather.8.cloned.1.call-done = bf16[32,16,8,512]{3,2,1,0:T(8,128)(2,1)} async-done(((bf16[8,16,8,512]{3,2,1,0:T(8,128)(2,1)}), bf16[32,16,8,512]{3,2,1,0:T(8,128)(2,1)}) %all-gather.8.cloned.1.call-update) | async-done | bytes 4194320 | tf_op jit(solution)/shard_map/all_gather | solution.py:396
  303.0 10.0 add_convert_fusion.6.q_ref.k_ref.v_ref
  315.3 9.8 attend.1
  328.6 7.5 collective-permute-done.10
  344.8 21.9 %collective-permute-done.13 = bf16[2,256,1024]{2,1,0:T(8,128)(2,1)} collective-permute-done((bf16[2,256,1024]{2,1,0:T(8,128)(2,1)S(1)}, bf16[2,256,1024]{2,1,0:T(8,128)(2,1)}, u32[]{:S(2)}, u32[]{:S(2)}) %collective-permute-start.13) | collective-permute-done | bytes 1048608 | tf_op jit(solution)/shard_map/ppermute | solution.py:37
  372.8 8.9 collective-permute-done.14
  388.8 10.0 collective-permute-done.17
  403.4 47.9 %all-gather.10.cloned.1.call-done = bf16[32,32,8,512]{3,2,1,0:T(8,128)(2,1)} async-done(((bf16[8,32,8,512]{3,2,1,0:T(8,128)(2,1)}), bf16[32,32,8,512]{3,2,1,0:T(8,128)(2,1)}) %all-gather.10.cloned.1.call-update) | async-done | bytes 8388624 | tf_op jit(solution)/shard_map/all_gather | solution.py:396
  459.9 5.1 fusion.116
  465.8 10.1 multiply_convert_fusion.1
  475.9 9.3 multiply_convert_fusion
  485.2 7.1 fusion.122
  492.4 7.0 add_convert_fusion.4
  507.8 7.7 fusion.17
  515.5 6.1 convolution_convert_fusion.3
  522.2 9.6 fusion.11
  531.8 7.1 add_convert_fusion.3
  542.2 6.5 fusion.123
  548.8 7.4 add_convert_fusion.2
  560.5 4.9 collective-permute-done.21
  571.9 11.2 %collective-permute-done.24 = bf16[256,1024]{1,0:T(8,128)(2,1)S(1)} collective-permute-done((bf16[256,1024]{1,0:T(8,128)(2,1)S(1)}, bf16[256,1024]{1,0:T(8,128)(2,1)S(1)}, u32[]{:S(2)}, u32[]{:S(2)}) %collective-permute-start.24) | collective-permute-done | bytes 524320 | tf_op jit(solution)/shard_map/ppermute | solution.py:37
  587.6 9.7 reduce-scatter.4.cloned.1.call-done
  599.5 12.5 %collective-permute-done.27 = bf16[256,1024]{1,0:T(8,128)(2,1)S(1)} collective-permute-done((bf16[256,1024]{1,0:T(8,128)(2,1)S(1)}, bf16[256,1024]{1,0:T(8,128)(2,1)S(1)}, u32[]{:S(2)}, u32[]{:S(2)}) %collective-permute-start.27) | collective-permute-done | bytes 524320 | tf_op jit(solution)/shard_map/ppermute | solution.py:37
  616.4 4.5 fusion.124
  622.2 16.0 %collective-permute-done.28 = bf16[2,256,1024]{2,1,0:T(8,128)(2,1)S(1)} collective-permute-done((bf16[2,256,1024]{2,1,0:T(8,128)(2,1)S(1)}, bf16[2,256,1024]{2,1,0:T(8,128)(2,1)S(1)}, u32[]{:S(2)}, u32[]{:S(2)}) %collective-permute-start.28) | collective-permute-done | bytes 1048608 | tf_op jit(solution)/shard_map/ppermute | solution.py:37
  643.0 3.9 convolution_convert_fusion.6
  650.2 3.5 convolution_convert_fusion.5
  656.6 12.7 %attend_back.1 = (bf16[2048,256]{1,0:T(8,128)(2,1)S(1)}, bf16[2048,256]{1,0:T(8,128)(2,1)S(1)}, bf16[2048,256]{1,0:T(8,128)(2,1)S(1)}) custom-call(s32[2,1024,1]{2,1,0:T(8,128)S(1)} %copy-done.7, s32[2,1,1024]{2,1,0:T(1,128)S(1)} %copy-done.19, bf16[2048,768]{1,0:T(8,128)(2,1)S(1)} %copy-done.1, bf16[2048,768]{1,0:T(8,128)(2,1)S(1)} %copy-done.1, ...), custom_call_target="tpu_custom_call" | custom-call | flops 5368709120 | bytes 8388608 | tf_op jit(solution)/shard_map/attend_back/pallas_call | solution.py:226
  669.6 7.8 reduce-scatter.6.cloned.1.call-done
  677.4 9.5 convolution_convert_fusion.4
  688.1 3.5 fusion.55
  691.5 3.6 fusion.24
  697.6 5.0 convolution_convert_fusion.1
  705.0 5.1 collective-permute-done.30
  710.1 5.8 add_convert_fusion.1
  720.6 6.3 all-to-all-start.2
  726.9 16.9 %collective-permute-done.33 = bf16[2,256,1024]{2,1,0:T(8,128)(2,1)} collective-permute-done((bf16[2,256,1024]{2,1,0:T(8,128)(2,1)}, bf16[2,256,1024]{2,1,0:T(8,128)(2,1)}, u32[]{:S(2)}, u32[]{:S(2)}) %collective-permute-start.33) | collective-permute-done | bytes 1048608 | tf_op jit(solution)/shard_map/ppermute | solution.py:37
  746.1 3.8 collective-permute-done.31
  752.0 6.0 convolution_convert_fusion.2
  758.0 18.7 %collective-permute-done.34 = bf16[256,1024]{1,0:T(8,128)(2,1)S(1)} collective-permute-done((bf16[256,1024]{1,0:T(8,128)(2,1)S(1)}, bf16[256,1024]{1,0:T(8,128)(2,1)S(1)}, u32[]{:S(2)}, u32[]{:S(2)}) %collective-permute-start.34) | collective-permute-done | bytes 524320 | tf_op jit(solution)/shard_map/ppermute | solution.py:37
  787.1 6.1 all-to-all-start.3
  795.4 10.9 %all-to-all-done.3 = bf16[256,8,256]{2,1,0:T(8,128)(2,1)} async-done(((bf16[256,8,256]{2,1,0:T(8,128)(2,1)}), bf16[256,8,256]{2,1,0:T(8,128)(2,1)}, u32[]{:S(2)}, u32[]{:S(2)}) %all-to-all-start.3) | async-done | bytes 1048608 | tf_op jit(solution)/shard_map/all_to_all | solution.py:358
  806.3 5.9 all-to-all-start.5
  825.6 6.2 all-to-all-start.4
  832.1 6.1 add_convert_fusion
  843.2 39.8 %collective-permute-done.36 = bf16[2,256,1024]{2,1,0:T(8,128)(2,1)S(1)} collective-permute-done((bf16[2,256,1024]{2,1,0:T(8,128)(2,1)S(1)}, bf16[2,256,1024]{2,1,0:T(8,128)(2,1)S(1)}, u32[]{:S(2)}, u32[]{:S(2)}) %collective-permute-start.36) | collective-permute-done | bytes 1048608 | tf_op jit(solution)/shard_map/ppermute | solution.py:37
  895.6 11.1 %collective-permute-done.39 = bf16[256,1024]{1,0:T(8,128)(2,1)} collective-permute-done((bf16[256,1024]{1,0:T(8,128)(2,1)}, bf16[256,1024]{1,0:T(8,128)(2,1)}, u32[]{:S(2)}, u32[]{:S(2)}) %collective-permute-start.39) | collective-permute-done | bytes 524320 | tf_op jit(solution)/shard_map/ppermute | solution.py:37
  910.9 4.3 multiply_reduce_fusion
  917.2 7.0 all-to-all-start.6
  946.9 32.3 %update_blocks.1 = (f32[12,256,512]{2,1,0:T(8,128)}, f32[12,256,512]{2,1,0:T(8,128)}, f32[12,256,512]{2,1,0:T(8,128)}, bf16[12,256,512]{2,1,0:T(8,128)(2,1)}) custom-call(f32[1]{0:T(128)} %bitcast.184.clip_ref, f32[12,1,512]{2,1,0:T(1,128)S(1)} %and_select_fusion.scale_ref, f32[12,256,512]{2,1,0:T(8,128)S(1)} %bitcast.381, f32[12,256,512]{2,1,0:T(8,128)} %first_ref.1, ...), custom_call_target="tpu_custom_call" | custom-call | flops 14495514624 | bytes 72351744 | tf_op jit(solution)/shard_map/update_blocks/pallas_call | solution.py:326
  980.0 17.2 %collective-permute-done.40 = bf16[256,2048]{1,0:T(8,128)(2,1)} collective-permute-done((bf16[256,2048]{1,0:T(8,128)(2,1)}, bf16[256,2048]{1,0:T(8,128)(2,1)}, u32[]{:S(2)}, u32[]{:S(2)}) %collective-permute-start.40) | collective-permute-done | bytes 1048608 | tf_op jit(solution)/shard_map/ppermute | solution.py:55
  999.5 8.9 collective-permute-done.41
  (463 shorter events, 242.8 us)
Async XLA Ops:
  7.2 42.5 %copy-start.63 = (f32[768]{0:T(1024)S(1)}, f32[768]{0:T(1024)}, u32[]{:S(2)}) copy-start(f32[768]{0:T(1024)} %param.21) | copy-start | bytes 9220
  7.2 207.8 %all-gather.6.cloned.1.call-start = ((), (), s32[]{:S(2)}) async-start(), calls=%async_computation.10 | async-start | bytes 9437184 | tf_op jit(solution)/shard_map/all_gather | solution.py:67
  7.2 39.9 %collective-permute-start.3 = (bf16[256,2048]{1,0:T(8,128)(2,1)}, bf16[256,2048]{1,0:T(8,128)(2,1)S(1)}, u32[]{:S(2)}, u32[]{:S(2)}) collective-permute-start(bf16[256,2048]{1,0:T(8,128)(2,1)} %bitcast.452), channel_id=1, source_target_pairs={{1,8},{2,4},{3,12},{4,2},{5,10},{7,14},{8,1},{10,5},{11,13},{12,3}... | collective-permute-start | bytes 3145736 | tf_op jit(solution)/shard_map/ppermute | solution.py:55
  55.4 89.3 %all-to-all-start = ((bf16[416,8,512]{2,1,0:T(8,128)(2,1)}), bf16[416,8,512]{2,1,0:T(8,128)(2,1)S(1)}, u32[]{:S(2)}, u32[]{:S(2)}) async-start(bf16[416,8,512]{2,1,0:T(8,128)(2,1)} %bitcast.423), calls=%async_computation | async-start | bytes 6815744 | tf_op jit(solution)/shard_map/all_to_all | solution.py:355
  59.2 237.2 %all-gather.8.cloned.1.call-start = ((), (), s32[]{:S(2)}) async-start(), calls=%async_computation.14 | async-start | bytes 5242880 | tf_op jit(solution)/shard_map/all_gather | solution.py:396
  59.2 3.9 collective-permute-start
  59.5 78.6 %collective-permute-start.4 = (bf16[256,2048]{1,0:T(8,128)(2,1)}, bf16[256,2048]{1,0:T(8,128)(2,1)}, u32[]{:S(2)}, u32[]{:S(2)}) collective-permute-start(bf16[256,2048]{1,0:T(8,128)(2,1)} %bitcast.453), channel_id=1, source_target_pairs={{1,8},{2,4},{3,12},{4,2},{5,10},{7,14},{8,1},{10,5},{11,13},{12,3}... | collective-permute-start | bytes 3145736 | tf_op jit(solution)/shard_map/ppermute | solution.py:55
  63.1 84.3 %copy-start.69 = (s32[384]{0:T(512)}, s32[384]{0:T(512)S(1)}, u32[]{:S(2)}) copy-start(s32[384]{0:T(512)S(1)} %multiply_add_fusion.1) | copy-start | bytes 4612
  63.1 30.6 %collective-permute-start.1 = (s32[2,1,1024]{2,1,0:T(1,128)S(1)}, s32[2,1,1024]{2,1,0:T(1,128)S(1)}, u32[]{:S(2)}, u32[]{:S(2)}) collective-permute-start(s32[2,1,1024]{2,1,0:T(1,128)S(1)} %pad_add_fusion), channel_id=1, source_target_pairs={{0,8},{8,0},{1,9},{9,1},{2,10},{10,2},{3,11},{11,3},{4,12},{12,4},... | collective-permute-start | bytes 24584 | tf_op jit(solution)/shard_map/ppermute | solution.py:37
  93.8 3.7 collective-permute-start.2
  216.2 235.0 %all-gather.10.cloned.1.call-start = ((), (), s32[]{:S(2)}) async-start(), calls=%async_computation.15 | async-start | bytes 10485760 | tf_op jit(solution)/shard_map/all_gather | solution.py:396
  217.4 97.8 %copy-start.6 = (s32[2,1024,1]{2,1,0:T(8,128)}, s32[2,1024,1]{2,1,0:T(8,128)S(1)}, u32[]{:S(2)}) copy-start(s32[2,1024,1]{2,1,0:T(8,128)S(1)} %copy.151.seg_col) | copy-start | bytes 24580
  220.3 15.9 %collective-permute-start.7 = (bf16[256,1024]{1,0:T(8,128)(2,1)}, bf16[256,1024]{1,0:T(8,128)(2,1)}, u32[]{:S(2)}, u32[]{:S(2)}) collective-permute-start(bf16[256,1024]{1,0:T(8,128)(2,1)} %get-tuple-element.178), channel_id=1, source_target_pairs={{0,16},{16,0},{1,17},{17,1},{2,18},{18,2},{3,19},{19,3},{4,20},{20... | collective-permute-start | bytes 1572872 | tf_op jit(solution)/shard_map/ppermute | solution.py:37
  221.7 93.5 %copy-start.18 = (s32[2,1,1024]{2,1,0:T(1,128)}, s32[2,1,1024]{2,1,0:T(1,128)S(1)}, u32[]{:S(2)}) copy-start(s32[2,1,1024]{2,1,0:T(1,128)S(1)} %pad_add_fusion.1.seg_row) | copy-start | bytes 24580
  228.8 15.2 %collective-permute-start.5 = (bf16[256,1024]{1,0:T(8,128)(2,1)}, bf16[256,1024]{1,0:T(8,128)(2,1)}, u32[]{:S(2)}, u32[]{:S(2)}) collective-permute-start(bf16[256,1024]{1,0:T(8,128)(2,1)} %get-tuple-element.179), channel_id=1, source_target_pairs={{0,8},{8,0},{1,9},{9,1},{2,10},{10,2},{3,11},{11,3},{4,12},{12,4},... | collective-permute-start | bytes 1572872 | tf_op jit(solution)/shard_map/ppermute | solution.py:37
  236.0 39.5 %copy-start.58 = (f32[2048]{0:T(1024)}, f32[2048]{0:T(1024)S(1)}, u32[]{:S(2)}) copy-start(f32[2048]{0:T(1024)S(1)} %get-tuple-element.125) | copy-start | bytes 24580
  237.4 27.6 %collective-permute-start.8 = (bf16[2,256,1024]{2,1,0:T(8,128)(2,1)S(1)}, bf16[2,256,1024]{2,1,0:T(8,128)(2,1)S(1)}, u32[]{:S(2)}, u32[]{:S(2)}) collective-permute-start(bf16[2,256,1024]{2,1,0:T(8,128)(2,1)S(1)} %get-tuple-element.181), channel_id=1, source_target_pairs={{0,8},{8,0},{1,9},{9,1},{2,10},{10,2},{3,11},{11,3},{4,12},{12,4},... | collective-permute-start | bytes 3145736 | tf_op jit(solution)/shard_map/ppermute | solution.py:37
  245.1 22.5 %collective-permute-start.6 = (bf16[2,256,1024]{2,1,0:T(8,128)(2,1)S(1)}, bf16[2,256,1024]{2,1,0:T(8,128)(2,1)S(1)}, u32[]{:S(2)}, u32[]{:S(2)}) collective-permute-start(bf16[2,256,1024]{2,1,0:T(8,128)(2,1)S(1)} %get-tuple-element.175), channel_id=1, source_target_pairs={{0,16},{16,0},{1,17},{17,1},{2,18},{18,2},{3,19},{19,3},{4,20},{20... | collective-permute-start | bytes 3145736 | tf_op jit(solution)/shard_map/ppermute | solution.py:37
  270.5 54.6 %collective-permute-start.9 = (bf16[1024,2048]{1,0:T(8,128)(2,1)}, bf16[1024,2048]{1,0:T(8,128)(2,1)}, u32[]{:S(2)}, u32[]{:S(2)}) collective-permute-start(bf16[1024,2048]{1,0:T(8,128)(2,1)} %bitcast.41), channel_id=1, source_target_pairs={{0,4},{4,0},{1,5},{5,1},{2,6},{6,2},{3,7},{7,3},{8,12},{12,8},{9,1... | collective-permute-start | bytes 12582920 | tf_op jit(solution)/shard_map/ppermute | solution.py:37
  303.0 294.3 %reduce-scatter.4.cloned.1.call-start = ((), (), s32[]{:S(2)}) async-start(), calls=%async_computation.11 | async-start | bytes 5242880 | tf_op jit(solution)/shard_map/reduce_scatter | solution.py:399
  328.6 7.5 collective-permute-start.10
  341.4 25.4 %collective-permute-start.13 = (bf16[2,256,1024]{2,1,0:T(8,128)(2,1)S(1)}, bf16[2,256,1024]{2,1,0:T(8,128)(2,1)}, u32[]{:S(2)}, u32[]{:S(2)}) collective-permute-start(bf16[2,256,1024]{2,1,0:T(8,128)(2,1)S(1)} %dynamic-slice_bitcast_fusion.2), channel_id=1, source_target_pairs={{0,8},{8,0},{1,9},{9,1},{2,10},{10,2},{3,11},{11,3},{4,12},{12,4},... | collective-permute-start | bytes 3145736 | tf_op jit(solution)/shard_map/ppermute | solution.py:37
  344.3 25.2 %collective-permute-start.11 = (bf16[2,256,1024]{2,1,0:T(8,128)(2,1)}, bf16[2,256,1024]{2,1,0:T(8,128)(2,1)}, u32[]{:S(2)}, u32[]{:S(2)}) collective-permute-start(bf16[2,256,1024]{2,1,0:T(8,128)(2,1)} %dynamic-slice_bitcast_fusion.3), channel_id=1, source_target_pairs={{0,16},{16,0},{1,17},{17,1},{2,18},{18,2},{3,19},{19,3},{4,20},{20... | collective-permute-start | bytes 3145736 | tf_op jit(solution)/shard_map/ppermute | solution.py:37
  368.5 13.2 %collective-permute-start.14 = (bf16[256,1024]{1,0:T(8,128)(2,1)S(1)}, bf16[256,1024]{1,0:T(8,128)(2,1)S(1)}, u32[]{:S(2)}, u32[]{:S(2)}) collective-permute-start(bf16[256,1024]{1,0:T(8,128)(2,1)S(1)} %dynamic-slice_bitcast_fusion.6), channel_id=1, source_target_pairs={{0,16},{16,0},{1,17},{17,1},{2,18},{18,2},{3,19},{19,3},{4,20},{20... | collective-permute-start | bytes 1572872 | tf_op jit(solution)/shard_map/ppermute | solution.py:37
  371.2 12.9 %collective-permute-start.12 = (bf16[256,1024]{1,0:T(8,128)(2,1)S(1)}, bf16[256,1024]{1,0:T(8,128)(2,1)S(1)}, u32[]{:S(2)}, u32[]{:S(2)}) collective-permute-start(bf16[256,1024]{1,0:T(8,128)(2,1)S(1)} %dynamic-slice_bitcast_fusion.7), channel_id=1, source_target_pairs={{0,8},{8,0},{1,9},{9,1},{2,10},{10,2},{3,11},{11,3},{4,12},{12,4},... | collective-permute-start | bytes 1572872 | tf_op jit(solution)/shard_map/ppermute | solution.py:37
  385.6 199.5 %copy-start.23 = (f32[256,2048]{1,0:T(8,128)}, f32[256,2048]{1,0:T(8,128)S(1)}, u32[]{:S(2)}) copy-start(f32[256,2048]{1,0:T(8,128)S(1)} %get-tuple-element.139) | copy-start | bytes 6291460
  386.7 12.1 %collective-permute-start.17 = (bf16[256,1024]{1,0:T(8,128)(2,1)S(1)}, bf16[256,1024]{1,0:T(8,128)(2,1)S(1)}, u32[]{:S(2)}, u32[]{:S(2)}) collective-permute-start(bf16[256,1024]{1,0:T(8,128)(2,1)S(1)} %get-tuple-element.168), channel_id=1, source_target_pairs={{0,16},{16,0},{1,17},{17,1},{2,18},{18,2},{3,19},{19,3},{4,20},{20... | collective-permute-start | bytes 1572872 | tf_op jit(solution)/shard_map/ppermute | solution.py:37
  387.8 13.5 %collective-permute-start.15 = (bf16[256,1024]{1,0:T(8,128)(2,1)S(1)}, bf16[256,1024]{1,0:T(8,128)(2,1)S(1)}, u32[]{:S(2)}, u32[]{:S(2)}) collective-permute-start(bf16[256,1024]{1,0:T(8,128)(2,1)S(1)} %get-tuple-element.169), channel_id=1, source_target_pairs={{0,8},{8,0},{1,9},{9,1},{2,10},{10,2},{3,11},{11,3},{4,12},{12,4},... | collective-permute-start | bytes 1572872 | tf_op jit(solution)/shard_map/ppermute | solution.py:37
  399.9 53.3 %collective-permute-start.18 = (bf16[2,256,1024]{2,1,0:T(8,128)(2,1)}, bf16[2,256,1024]{2,1,0:T(8,128)(2,1)}, u32[]{:S(2)}, u32[]{:S(2)}) collective-permute-start(bf16[2,256,1024]{2,1,0:T(8,128)(2,1)} %get-tuple-element.171), channel_id=1, source_target_pairs={{0,8},{8,0},{1,9},{9,1},{2,10},{10,2},{3,11},{11,3},{4,12},{12,4},... | collective-permute-start | bytes 3145736 | tf_op jit(solution)/shard_map/ppermute | solution.py:37
  402.8 52.0 %collective-permute-start.16 = (bf16[2,256,1024]{2,1,0:T(8,128)(2,1)}, bf16[2,256,1024]{2,1,0:T(8,128)(2,1)}, u32[]{:S(2)}, u32[]{:S(2)}) collective-permute-start(bf16[2,256,1024]{2,1,0:T(8,128)(2,1)} %get-tuple-element.165), channel_id=1, source_target_pairs={{0,16},{16,0},{1,17},{17,1},{2,18},{18,2},{3,19},{19,3},{4,20},{20... | collective-permute-start | bytes 3145736 | tf_op jit(solution)/shard_map/ppermute | solution.py:37
  458.8 17.1 %collective-permute-start.19 = (bf16[1024,2048]{1,0:T(8,128)(2,1)}, bf16[1024,2048]{1,0:T(8,128)(2,1)}, u32[]{:S(2)}, u32[]{:S(2)}) collective-permute-start(bf16[1024,2048]{1,0:T(8,128)(2,1)} %bitcast.67), channel_id=1, source_target_pairs={{0,4},{4,0},{1,5},{5,1},{2,6},{6,2},{3,7},{7,3},{8,12},{12,8},{9,1... | collective-permute-start | bytes 12582920 | tf_op jit(solution)/shard_map/ppermute | solution.py:37
  521.6 10.2 collective-permute-start.20
  522.1 155.3 %reduce-scatter.6.cloned.1.call-start = ((), (), s32[]{:S(2)}) async-start(), calls=%async_computation.12 | async-start | bytes 5242880 | tf_op jit(solution)/shard_map/reduce_scatter | solution.py:399
  540.1 25.3 %collective-permute-start.21 = (bf16[2,256,1024]{2,1,0:T(8,128)(2,1)}, bf16[2,256,1024]{2,1,0:T(8,128)(2,1)S(1)}, u32[]{:S(2)}, u32[]{:S(2)}) collective-permute-start(bf16[2,256,1024]{2,1,0:T(8,128)(2,1)} %slice_bitcast_fusion.6), channel_id=1, source_target_pairs={{0,16},{16,0},{1,17},{17,1},{2,18},{18,2},{3,19},{19,3},{4,20},{20... | collective-permute-start | bytes 3145736 | tf_op jit(solution)/shard_map/ppermute | solution.py:37
  541.7 25.4 %collective-permute-start.23 = (bf16[2,256,1024]{2,1,0:T(8,128)(2,1)}, bf16[2,256,1024]{2,1,0:T(8,128)(2,1)}, u32[]{:S(2)}, u32[]{:S(2)}) collective-permute-start(bf16[2,256,1024]{2,1,0:T(8,128)(2,1)} %slice_bitcast_fusion.4), channel_id=1, source_target_pairs={{0,8},{8,0},{1,9},{9,1},{2,10},{10,2},{3,11},{11,3},{4,12},{12,4},... | collective-permute-start | bytes 3145736 | tf_op jit(solution)/shard_map/ppermute | solution.py:37
  570.0 13.1 %collective-permute-start.24 = (bf16[256,1024]{1,0:T(8,128)(2,1)S(1)}, bf16[256,1024]{1,0:T(8,128)(2,1)S(1)}, u32[]{:S(2)}, u32[]{:S(2)}) collective-permute-start(bf16[256,1024]{1,0:T(8,128)(2,1)S(1)} %slice_bitcast_fusion.12), channel_id=1, source_target_pairs={{0,16},{16,0},{1,17},{17,1},{2,18},{18,2},{3,19},{19,3},{4,20},{20... | collective-permute-start | bytes 1572872 | tf_op jit(solution)/shard_map/ppermute | solution.py:37
  571.3 12.5 %collective-permute-start.22 = (bf16[256,1024]{1,0:T(8,128)(2,1)S(1)}, bf16[256,1024]{1,0:T(8,128)(2,1)S(1)}, u32[]{:S(2)}, u32[]{:S(2)}) collective-permute-start(bf16[256,1024]{1,0:T(8,128)(2,1)S(1)} %slice_bitcast_fusion.14), channel_id=1, source_target_pairs={{0,8},{8,0},{1,9},{9,1},{2,10},{10,2},{3,11},{11,3},{4,12},{12,4},... | collective-permute-start | bytes 1572872 | tf_op jit(solution)/shard_map/ppermute | solution.py:37
  598.3 13.7 %collective-permute-start.27 = (bf16[256,1024]{1,0:T(8,128)(2,1)S(1)}, bf16[256,1024]{1,0:T(8,128)(2,1)S(1)}, u32[]{:S(2)}, u32[]{:S(2)}) collective-permute-start(bf16[256,1024]{1,0:T(8,128)(2,1)S(1)} %get-tuple-element.160), channel_id=1, source_target_pairs={{0,16},{16,0},{1,17},{17,1},{2,18},{18,2},{3,19},{19,3},{4,20},{20... | collective-permute-start | bytes 1572872 | tf_op jit(solution)/shard_map/ppermute | solution.py:37
  598.9 15.8 %collective-permute-start.25 = (bf16[256,1024]{1,0:T(8,128)(2,1)}, bf16[256,1024]{1,0:T(8,128)(2,1)}, u32[]{:S(2)}, u32[]{:S(2)}) collective-permute-start(bf16[256,1024]{1,0:T(8,128)(2,1)} %get-tuple-element.161), channel_id=1, source_target_pairs={{0,8},{8,0},{1,9},{9,1},{2,10},{10,2},{3,11},{11,3},{4,12},{12,4},... | collective-permute-start | bytes 1572872 | tf_op jit(solution)/shard_map/ppermute | solution.py:37
  599.5 184.6 %reduce-scatter.8.cloned.1.call-start = ((), (), s32[]{:S(2)}) async-start(), calls=%async_computation.13 | async-start | bytes 5242880 | tf_op jit(solution)/shard_map/reduce_scatter | solution.py:399
  614.0 24.2 %collective-permute-start.28 = (bf16[2,256,1024]{2,1,0:T(8,128)(2,1)S(1)}, bf16[2,256,1024]{2,1,0:T(8,128)(2,1)S(1)}, u32[]{:S(2)}, u32[]{:S(2)}) collective-permute-start(bf16[2,256,1024]{2,1,0:T(8,128)(2,1)S(1)} %get-tuple-element.163), channel_id=1, source_target_pairs={{0,8},{8,0},{1,9},{9,1},{2,10},{10,2},{3,11},{11,3},{4,12},{12,4},... | collective-permute-start | bytes 3145736 | tf_op jit(solution)/shard_map/ppermute | solution.py:37
  615.8 23.9 %collective-permute-start.26 = (bf16[2,256,1024]{2,1,0:T(8,128)(2,1)S(1)}, bf16[2,256,1024]{2,1,0:T(8,128)(2,1)S(1)}, u32[]{:S(2)}, u32[]{:S(2)}) collective-permute-start(bf16[2,256,1024]{2,1,0:T(8,128)(2,1)S(1)} %get-tuple-element.157), channel_id=1, source_target_pairs={{0,16},{16,0},{1,17},{17,1},{2,18},{18,2},{3,19},{19,3},{4,20},{20... | collective-permute-start | bytes 3145736 | tf_op jit(solution)/shard_map/ppermute | solution.py:37
  642.7 7.5 collective-permute-start.29
  702.6 7.5 collective-permute-start.30
  717.4 26.3 %collective-permute-start.33 = (bf16[2,256,1024]{2,1,0:T(8,128)(2,1)}, bf16[2,256,1024]{2,1,0:T(8,128)(2,1)}, u32[]{:S(2)}, u32[]{:S(2)}) collective-permute-start(bf16[2,256,1024]{2,1,0:T(8,128)(2,1)} %dynamic-slice_bitcast_fusion), channel_id=1, source_target_pairs={{0,8},{8,0},{1,9},{9,1},{2,10},{10,2},{3,11},{11,3},{4,12},{12,4},... | collective-permute-start | bytes 3145736 | tf_op jit(solution)/shard_map/ppermute | solution.py:37
  718.1 31.8 %collective-permute-start.31 = (bf16[2,256,1024]{2,1,0:T(8,128)(2,1)S(1)}, bf16[2,256,1024]{2,1,0:T(8,128)(2,1)}, u32[]{:S(2)}, u32[]{:S(2)}) collective-permute-start(bf16[2,256,1024]{2,1,0:T(8,128)(2,1)S(1)} %dynamic-slice_bitcast_fusion.1), channel_id=1, source_target_pairs={{0,16},{16,0},{1,17},{17,1},{2,18},{18,2},{3,19},{19,3},{4,20},{20... | collective-permute-start | bytes 3145736 | tf_op jit(solution)/shard_map/ppermute | solution.py:37
  720.6 56.7 %all-to-all-start.2 = ((bf16[256,8,512]{2,1,0:T(8,128)(2,1)}), bf16[256,8,512]{2,1,0:T(8,128)(2,1)}, u32[]{:S(2)}, u32[]{:S(2)}) async-start(bf16[256,8,512]{2,1,0:T(8,128)(2,1)} %bitcast.146), calls=%async_computation.5 | async-start | bytes 4194304 | tf_op jit(solution)/shard_map/all_to_all | solution.py:358
  745.4 31.3 %collective-permute-start.34 = (bf16[256,1024]{1,0:T(8,128)(2,1)S(1)}, bf16[256,1024]{1,0:T(8,128)(2,1)S(1)}, u32[]{:S(2)}, u32[]{:S(2)}) collective-permute-start(bf16[256,1024]{1,0:T(8,128)(2,1)S(1)} %dynamic-slice_bitcast_fusion.4), channel_id=1, source_target_pairs={{0,16},{16,0},{1,17},{17,1},{2,18},{18,2},{3,19},{19,3},{4,20},{20... | collective-permute-start | bytes 1572872 | tf_op jit(solution)/shard_map/ppermute | solution.py:37
  751.9 25.0 %collective-permute-start.32 = (bf16[256,1024]{1,0:T(8,128)(2,1)S(1)}, bf16[256,1024]{1,0:T(8,128)(2,1)S(1)}, u32[]{:S(2)}, u32[]{:S(2)}) collective-permute-start(bf16[256,1024]{1,0:T(8,128)(2,1)S(1)} %dynamic-slice_bitcast_fusion.5), channel_id=1, source_target_pairs={{0,8},{8,0},{1,9},{9,1},{2,10},{10,2},{3,11},{11,3},{4,12},{12,4},... | collective-permute-start | bytes 1572872 | tf_op jit(solution)/shard_map/ppermute | solution.py:37
  779.6 7.6 collective-permute-start.35
  787.1 19.2 %all-to-all-start.3 = ((bf16[256,8,256]{2,1,0:T(8,128)(2,1)}), bf16[256,8,256]{2,1,0:T(8,128)(2,1)}, u32[]{:S(2)}, u32[]{:S(2)}) async-start(bf16[256,8,256]{2,1,0:T(8,128)(2,1)} %bitcast.454), calls=%async_computation.6 | async-start | bytes 2097152 | tf_op jit(solution)/shard_map/all_to_all | solution.py:358
  806.3 19.3 %all-to-all-start.5 = ((f32[32,1,768]{2,1,0:T(1,128)}), f32[32,1,768]{2,1,0:T(1,128)S(1)}, u32[]{:S(2)}, u32[]{:S(2)}) async-start(f32[32,1,768]{2,1,0:T(1,128)} %bitcast.165), calls=%async_computation.8 | async-start | bytes 196608 | tf_op jit(solution)/shard_map/all_to_all | solution.py:355
  825.6 85.3 %all-to-all-start.4 = ((bf16[384,8,512]{2,1,0:T(8,128)(2,1)}), bf16[384,8,512]{2,1,0:T(8,128)(2,1)}, u32[]{:S(2)}, u32[]{:S(2)}) async-start(bf16[384,8,512]{2,1,0:T(8,128)(2,1)} %copy.156), calls=%async_computation.7 | async-start | bytes 6291456 | tf_op jit(solution)/shard_map/all_to_all | solution.py:355
  838.3 44.7 %collective-permute-start.36 = (bf16[2,256,1024]{2,1,0:T(8,128)(2,1)S(1)}, bf16[2,256,1024]{2,1,0:T(8,128)(2,1)S(1)}, u32[]{:S(2)}, u32[]{:S(2)}) collective-permute-start(bf16[2,256,1024]{2,1,0:T(8,128)(2,1)S(1)} %slice_bitcast_fusion.2), channel_id=1, source_target_pairs={{0,16},{16,0},{1,17},{17,1},{2,18},{18,2},{3,19},{19,3},{4,20},{20... | collective-permute-start | bytes 3145736 | tf_op jit(solution)/shard_map/ppermute | solution.py:37
  840.3 45.5 %collective-permute-start.38 = (bf16[2,256,1024]{2,1,0:T(8,128)(2,1)S(1)}, bf16[2,256,1024]{2,1,0:T(8,128)(2,1)}, u32[]{:S(2)}, u32[]{:S(2)}) collective-permute-start(bf16[2,256,1024]{2,1,0:T(8,128)(2,1)S(1)} %slice_bitcast_fusion), channel_id=1, source_target_pairs={{0,8},{8,0},{1,9},{9,1},{2,10},{10,2},{3,11},{11,3},{4,12},{12,4},... | collective-permute-start | bytes 3145736 | tf_op jit(solution)/shard_map/ppermute | solution.py:37
  890.7 16.0 %collective-permute-start.39 = (bf16[256,1024]{1,0:T(8,128)(2,1)}, bf16[256,1024]{1,0:T(8,128)(2,1)}, u32[]{:S(2)}, u32[]{:S(2)}) collective-permute-start(bf16[256,1024]{1,0:T(8,128)(2,1)} %slice_bitcast_fusion.8), channel_id=1, source_target_pairs={{0,16},{16,0},{1,17},{17,1},{2,18},{18,2},{3,19},{19,3},{4,20},{20... | collective-permute-start | bytes 1572872 | tf_op jit(solution)/shard_map/ppermute | solution.py:37
  892.1 16.1 %collective-permute-start.37 = (bf16[256,1024]{1,0:T(8,128)(2,1)}, bf16[256,1024]{1,0:T(8,128)(2,1)}, u32[]{:S(2)}, u32[]{:S(2)}) collective-permute-start(bf16[256,1024]{1,0:T(8,128)(2,1)} %slice_bitcast_fusion.10), channel_id=1, source_target_pairs={{0,8},{8,0},{1,9},{9,1},{2,10},{10,2},{3,11},{11,3},{4,12},{12,4},... | collective-permute-start | bytes 1572872 | tf_op jit(solution)/shard_map/ppermute | solution.py:37
  895.0 84.4 %copy-start.60 = (f32[768]{0:T(1024)}, f32[768]{0:T(1024)S(1)}, u32[]{:S(2)}) copy-start(f32[768]{0:T(1024)S(1)} %reduce_sum.273) | copy-start | bytes 9220
  917.2 16.7 %all-to-all-start.6 = ((f32[32,1,128]{2,1,0:T(1,128)}), f32[32,1,128]{2,1,0:T(1,128)S(1)}, u32[]{:S(2)}, u32[]{:S(2)}) async-start(f32[32,1,128]{2,1,0:T(1,128)} %broadcast_in_dim.123), calls=%async_computation.9 | async-start | bytes 32768 | tf_op jit(solution)/shard_map/all_to_all | solution.py:355
  934.6 62.6 %collective-permute-start.40 = (bf16[256,2048]{1,0:T(8,128)(2,1)}, bf16[256,2048]{1,0:T(8,128)(2,1)}, u32[]{:S(2)}, u32[]{:S(2)}) collective-permute-start(bf16[256,2048]{1,0:T(8,128)(2,1)} %fusion.39), channel_id=1, source_target_pairs={{1,8},{2,4},{3,12},{4,2},{5,10},{7,14},{8,1},{10,5},{11,13},{12,3}... | collective-permute-start | bytes 3145736 | tf_op jit(solution)/shard_map/ppermute | solution.py:55
  937.9 70.5 %collective-permute-start.41 = (bf16[256,2048]{1,0:T(8,128)(2,1)}, bf16[256,2048]{1,0:T(8,128)(2,1)}, u32[]{:S(2)}, u32[]{:S(2)}) collective-permute-start(bf16[256,2048]{1,0:T(8,128)(2,1)} %fusion.35), channel_id=1, source_target_pairs={{1,8},{2,4},{3,12},{4,2},{5,10},{7,14},{8,1},{10,5},{11,13},{12,3}... | collective-permute-start | bytes 3145736 | tf_op jit(solution)/shard_map/ppermute | solution.py:55
  946.9 32.4 %copy-start.72 = (f32[768]{0:T(1024)S(1)}, f32[768]{0:T(1024)}, u32[]{:S(2)}) copy-start(f32[768]{0:T(1024)} %param.23) | copy-start | bytes 9220
  946.9 50.3 %copy-start.45 = (bf16[256,2048]{1,0:T(8,128)(2,1)S(1)}, bf16[256,2048]{1,0:T(8,128)(2,1)}, u32[]{:S(2)}) copy-start(bf16[256,2048]{1,0:T(8,128)(2,1)} %fusion.39) | copy-start | bytes 3145732
  946.9 61.5 %copy-start.46 = (bf16[256,2048]{1,0:T(8,128)(2,1)S(1)}, bf16[256,2048]{1,0:T(8,128)(2,1)}, u32[]{:S(2)}) copy-start(bf16[256,2048]{1,0:T(8,128)(2,1)} %fusion.35) | copy-start | bytes 3145732
  (74 other events, 658.2 us)
Sparse Core Ops, SparseCore 0:
  49.8 106.6 all-gather.5
  216.3 80.0 all-gather.7
  303.1 148.1 all-gather.9
  522.2 74.9 reduce-scatter.3
  600.1 77.2 reduce-scatter.5
  705.1 77.4 reduce-scatter.7
